TPU v7x, 128 devices: a whole 4x4x4 slice. The times are simulated.
128 devices in a mesh: ta: 4 (over y), ha: 8 (over z_lo, x), wa: 4 (over z_hi, core).
Axes of the slice: x: 4, y: 4, z: 4 (z_hi: 2, z_lo: 2; z = z_hi * 2 + z_lo), core: 2. Of those that a mesh axis runs over, the one named last changes fastest.
Arguments:
- latent: bfloat16 [16, 128, 128, 256], P('ta', 'ha', 'wa'), may hold values from -6 to 6
- kernel: bfloat16 [27, 256, 256], replicated, may hold values from -0.078125 to 0.078125
- bias: float32 [256], replicated, may hold values from -3 to 3
- cotangent: bfloat16 [16, 128, 128, 256], P('ta', 'ha', 'wa'), may hold values from -6 to 6
Outputs:
- activation: bfloat16 [16, 128, 128, 256], P('ta', 'ha', 'wa')
- latent_grad: bfloat16 [16, 128, 128, 256], P('ta', 'ha', 'wa')
- kernel_grad: float32 [27, 256, 256], replicated
- bias_grad: float32 [256], replicated
All inputs are finite; a program needn't handle non-finite values.
Results may differ from a plain program's by a relative error of at most 0.0055.
Values may be sent and summed in bfloat16 or wider, within the bound.
No kernel may reach another device: no remote copies, remote signals or barrier semaphores. Data moves between devices by JAX's collectives and lax.ppermute only.
A program may use at most 128 MiB of HBM per device.

v0:
```python
import functools
import itertools

import jax
import jax.numpy as jnp
import numpy as np
from jax import lax
from jax.experimental import pallas as pl
from jax.experimental.pallas import tpu as pltpu
from jax.sharding import Mesh
from jax.sharding import PartitionSpec as P

AXES = ("ta", "hz", "hx", "wz", "wc")
HA = ("hz", "hx")
WA = ("wz", "wc")
BF = jnp.bfloat16
F32 = jnp.float32
HALF = 14
VMEM = pl.BlockSpec(memory_space=pltpu.VMEM)
MIB = 1 << 20


def number(x, y, z, core):
    return (((y * 2 + z % 2) * 4 + x) * 2 + z // 2) * 2 + core


def cubes(pairs):
    out = []
    for core in (0, 1):
        for px, py, pz in itertools.product(pairs, repeat=3):
            cube = []
            for a, b, c in itertools.product(range(2), repeat=3):
                place = [(p + core) % 4 for p in (px[a], py[b], pz[c])]
                cube.append(number(*place, core))
            out.append(cube)
    return out


NEAR = cubes(((0, 1), (3, 2)))
FAR = cubes(((0, 3), (1, 2)))


def exchange(pieces, groups):
    return lax.all_to_all(pieces, AXES, 0, 0, axis_index_groups=groups)


def shift(block, axis, distance):
    names = axis if isinstance(axis, tuple) else (axis,)
    count = 1
    for name in names:
        count *= lax.axis_size(name)
    route = [(i, i + distance) for i in range(count) if 0 <= i + distance < count]
    return lax.ppermute(block, axis, route)


def halo(field, near_frames, direction):
    frames = field.shape[0]
    remote = shift(near_frames(field), "ta", direction)
    low = shift(field[:, -1:], HA, 1)
    high = shift(field[:, :1], HA, -1)
    last = jnp.concatenate([low[:, :, -1:], field[:, :, -1:], high[:, :, -1:]], axis=1)
    first = jnp.concatenate([low[:, :, :1], field[:, :, :1], high[:, :, :1]], axis=1)
    left = shift(last, WA, 1)
    right = shift(first, WA, -1)
    rows = jnp.stack([near_frames(low), near_frames(high)])
    columns = jnp.stack([near_frames(left), near_frames(right)])
    count = rows.size // rows.shape[-1]
    flat = jnp.concatenate([rows.reshape(count, -1), columns.reshape(-1, rows.shape[-1])])
    flat = shift(flat, "ta", direction)
    rows = flat[:count].reshape(rows.shape)
    columns = flat[count:].reshape(columns.shape)
    return (field, low, high, left, right, remote, rows, columns)


def place(parts, own, far, taps):
    field, low, high, left, right, remote, rows, columns = parts
    _, height, width, depth = field.shape

    def put(at, middle, top, bottom, west, east):
        block = jnp.concatenate([top, middle, bottom], axis=0).astype(F32)
        column = lax.broadcasted_iota(jnp.int32, block.shape, 1)
        taps[1, at] = block.astype(BF)
        moved = pltpu.roll(block, 1, 1)
        taps[0, at] = jnp.where(column == 0, west.astype(F32), moved).astype(BF)
        moved = pltpu.roll(block, width - 1, 1)
        taps[2, at] = jnp.where(column == width - 1, east.astype(F32), moved).astype(BF)

    @pl.loop(0, 4)
    def _(t):
        put(own + t, field[t], low[t], high[t], left[t], right[t])

    @pl.loop(0, 2)
    def _(t):
        put(far + t, remote[t], rows[0, t], rows[1, t], columns[0, t], columns[1, t])


def window(taps, c, frame, b):
    piece = taps[c, frame, pl.ds(b, 16)]
    return piece.reshape(-1, piece.shape[-1])


def forward_kernel(*refs):
    parts, (kernel, bias, cotangent), rest = refs[:8], refs[8:11], refs[11:]
    activation, dpre, dpre_t, taps, send = rest
    place(parts, 2, 0, taps)

    @pl.loop(0, 4)
    def _(t):
        total = jnp.broadcast_to(bias[...], (512, 256))
        for a in range(3):
            pieces = [window(taps, c, t + a, b) for b in range(3) for c in range(3)]
            total = total + jnp.dot(
                jnp.concatenate(pieces, axis=1), kernel[a], preferred_element_type=F32
            )
        sig = jax.nn.sigmoid(total)
        activation[t] = (total * sig).astype(BF).reshape(16, 32, 256)
        cot = cotangent[t].reshape(512, 256).astype(F32)
        slope = cot * sig * (1.0 + total * (1.0 - sig))
        dpre[t] = slope.astype(BF).reshape(16, 32, 256)
        dpre_t[:, pl.ds(pl.multiple_of(t * 512, 512), 512)] = slope.T.astype(BF)

    first = HALF * (1 - lax.axis_index("wc"))

    def emit(j, value):
        send[j] = value.astype(BF)

    weight_terms(taps, dpre_t, first, emit)


def weight_terms(taps, dpre_t, first, emit):
    @pl.loop(0, HALF)
    def _(j):
        k = first + j

        @pl.when(k < 27)
        def _():
            a, b, c = k // 9, (k // 3) % 3, k % 3
            block = taps[c, pl.ds(a, 4), pl.ds(b, 16)].reshape(2048, 256)
            emit(j, jnp.dot(dpre_t[...], block, preferred_element_type=F32))

        @pl.when(k == 27)
        def _():
            total = jnp.sum(dpre_t[...].astype(F32), axis=1, keepdims=True)
            high = total.astype(BF).astype(F32)
            lane = lax.broadcasted_iota(jnp.int32, (256, 256), 1)
            emit(j, jnp.where(lane < 128, high, total - high))


def weight_kernel(taps, dpre_t, received, out):
    def emit(j, value):
        out[j] = (value + received[j].astype(F32)).astype(BF)

    weight_terms(taps, dpre_t, HALF * lax.axis_index("wc"), emit)


def backward_kernel(*refs):
    parts, (turned, latent_grad, taps) = refs[:8], refs[8:]
    place(parts, 0, 4, taps)

    @pl.loop(0, 4)
    def _(t):
        total = jnp.zeros((512, 256), F32)
        for a in range(3):
            pieces = [window(taps, 2 - c, t + 2 - a, 2 - b) for b in range(3) for c in range(3)]
            total = total + jnp.dot(
                jnp.concatenate(pieces, axis=1), turned[a], preferred_element_type=F32
            )
        latent_grad[t] = total.astype(BF).reshape(16, 32, 256)


def turn_kernel(kernel, out):
    @pl.loop(0, 27)
    def _(k):
        out[k] = kernel[k].astype(F32).T.astype(BF)


def finish_kernel(scale, mine, other, kernel_grad, bias_grad):
    step = pl.program_id(0)
    k = jnp.where(step == 0, 27, step - 1)
    core = lax.axis_index("wc")
    row = lax.broadcasted_iota(jnp.int32, (256, 256), 0)
    lane = lax.broadcasted_iota(jnp.int32, (256, 256), 1)
    unit = jnp.where(row == lane, 1.0, 0.0).astype(BF)

    def flip(block):
        turned = lax.dot_general(unit, block, (((1,), (1,)), ((), ())), preferred_element_type=F32)

        @pl.when(step == 0)
        def _():
            bias_grad[...] = (turned[0:1] + turned[128:129]) * scale

        @pl.when(step > 0)
        def _():
            kernel_grad[0] = turned * scale

    owner = k // HALF
    j = k - HALF * owner

    @pl.when(owner == core)
    def _():
        flip(mine[j])

    @pl.when(owner != core)
    def _():
        flip(other[j])


def call(body, outs, scratch=(), vmem=48, flops=0, n_in=0):
    return pl.pallas_call(
        body,
        out_shape=outs,
        in_specs=[VMEM] * n_in,
        out_specs=jax.tree.map(lambda _: VMEM, outs),
        scratch_shapes=list(scratch),
        compiler_params=pltpu.CompilerParams(vmem_limit_bytes=vmem * MIB),
        cost_estimate=pl.CostEstimate(flops=flops, bytes_accessed=8 * MIB, transcendentals=0),
    )


def sum_pieces(pieces, special):
    total = jnp.sum(pieces.astype(F32), axis=0)
    value = total[:, :128] + total[:, 128:]
    high = lax.reduce_precision(value, 8, 7)
    split = jnp.concatenate([high, value - high], axis=1)
    return jnp.where(special, split, total).astype(BF)


def shards(latent, kernel, bias, cotangent):
    frames, rows, columns, width = latent.shape
    cells = frames * rows * columns
    for name in AXES:
        cells *= lax.axis_size(name)
    scale = float(1.0 / np.sqrt(np.float32(cells)))
    conv_flops = 2 * 2048 * 27 * 256 * 256
    block = jax.ShapeDtypeStruct(latent.shape, BF)

    turned = call(
        turn_kernel, jax.ShapeDtypeStruct(kernel.shape, BF), vmem=16, flops=conv_flops // 4, n_in=1
    )(kernel)
    padded = halo(latent, lambda x: x[2:], 1)
    half = jax.ShapeDtypeStruct((HALF, 256, 256), BF)
    activation, dpre, dpre_t, taps, send = call(
        forward_kernel,
        (
            block,
            block,
            jax.ShapeDtypeStruct((256, 2048), BF),
            jax.ShapeDtypeStruct((3, 6, 18, 32, 256), BF),
            half,
        ),
        flops=conv_flops * 3 // 2,
        n_in=11,
    )(*padded, kernel.reshape(3, 2304, 256), bias.reshape(1, 256), cotangent)
    received = lax.ppermute(send, "wc", [(0, 1), (1, 0)])
    terms = call(weight_kernel, half, flops=conv_flops // 2, n_in=3)(taps, dpre_t, received)

    core = lax.axis_index("wc")
    z = 2 * lax.axis_index("wz") + lax.axis_index("hz")
    spot = [(p - core) % 4 for p in (lax.axis_index("hx"), lax.axis_index("ta"), z)]
    near = sum(w * ((p == 1) | (p == 2)) for w, p in zip((4, 2, 1), spot))
    far = sum(w * (p >= 2) for w, p in zip((4, 2, 1), spot))
    first_bias = (HALF - 1) * 256

    pieces = exchange(terms.reshape(8, 448, 256), NEAR)
    row = near * 448 + lax.broadcasted_iota(jnp.int32, (448, 1), 0)
    total = sum_pieces(pieces, (core == 1) & (row >= first_bias))
    pieces = exchange(total.reshape(8, 56, 256), FAR)
    row = near * 448 + far * 56 + lax.broadcasted_iota(jnp.int32, (56, 1), 0)
    total = sum_pieces(pieces, (core == 1) & (row >= first_bias))
    total = exchange(jnp.broadcast_to(total[None], (8, 56, 256)), FAR).reshape(448, 256)
    total = exchange(jnp.broadcast_to(total[None], (8, 448, 256)), NEAR)
    mine = total.reshape(HALF, 256, 256)
    other = lax.ppermute(mine, "wc", [(0, 1), (1, 0)])

    spread = halo(dpre, lambda x: x[:2], -1)
    latent_grad = call(
        backward_kernel,
        block,
        (pltpu.VMEM((3, 6, 18, 32, 256), BF),),
        flops=conv_flops,
        n_in=9,
    )(*spread, turned.reshape(3, 2304, 256))

    whole = pl.BlockSpec((HALF, 256, 256), lambda k: (0, 0, 0))
    kernel_grad, bias_grad = pl.pallas_call(
        functools.partial(finish_kernel, scale),
        grid=(28,),
        out_shape=(
            jax.ShapeDtypeStruct((27, 256, 256), F32),
            jax.ShapeDtypeStruct((1, 256), F32),
        ),
        in_specs=[whole, whole],
        out_specs=(
            pl.BlockSpec((1, 256, 256), lambda k: (jnp.maximum(k - 1, 0), 0, 0)),
            pl.BlockSpec((1, 256), lambda k: (0, 0)),
        ),
        compiler_params=pltpu.CompilerParams(vmem_limit_bytes=24 * MIB),
    )(mine, other)
    return (activation, latent_grad, kernel_grad, bias_grad.reshape(256))


def solution(mesh):
    split = Mesh(np.asarray(mesh.devices).reshape(4, 2, 4, 2, 2), AXES)
    placed = P("ta", HA, WA, None)
    return jax.shard_map(
        shards,
        mesh=split,
        in_specs=(placed, P(), P(), placed),
        out_specs=(placed, placed, P(), P()),
        check_vma=False,
    )
```

profile of v0, /device:TPU:1, one launch (start us, length us, event | category | flops | bytes accessed | tf_op | source)
XLA Modules:
  0.0 187.6 jit_solution(5659489598682029300)
XLA Ops:
  0.6 0.0 copy-start.3
  0.7 1.0 fusion.8
  1.6 3.9 %collective-permute-start = (bf16[4,1,32,256]{3,2,1,0:T(8,128)(2,1)S(1)}, bf16[4,1,32,256]{3,2,1,0:T(8,128)(2,1)S(1)}, u32[]{:S(2)}, u32[]{:S(2)}) collective-permute-start(bf16[4,1,32,256]{3,2,1,0:T(8,128)(2,1)S(1)} %get-tuple-element.25), channel_id=1, source_target_pairs={{0,4},{4,8},{8,12},{12,16},{16,20},{20,24},{24,28},{1,5},{5,9},{9,... | collective-permute-start | bytes 196616 | tf_op jit(solution)/shard_map/ppermute | solution.py:53
  5.6 1.3 collective-permute-start.1
  6.9 1.1 slice.110
  8.0 3.2 %collective-permute-start.4 = (bf16[2,16,32,256]{3,2,1,0:T(8,128)(2,1)S(1)}, bf16[2,16,32,256]{3,2,1,0:T(8,128)(2,1)S(1)}, u32[]{:S(2)}, u32[]{:S(2)}) collective-permute-start(bf16[2,16,32,256]{3,2,1,0:T(8,128)(2,1)S(1)} %slice.110), channel_id=1, source_target_pairs={{0,32},{32,64},{64,96},{1,33},{33,65},{65,97},{2,34},{34,66},{66,9... | collective-permute-start | bytes 1572872 | tf_op jit(solution)/shard_map/ppermute | solution.py:53
  11.2 1.1 fusion.7
  12.3 0.0 collective-permute-done.refs_1_
  12.4 0.0 collective-permute-done.1.refs_2_
  12.4 0.1 pad_maximum_fusion.3
  12.5 3.1 %collective-permute-start.3 = (bf16[4,18,1,256]{3,2,1,0:T(2,128)(2,1)S(1)}, bf16[4,18,1,256]{3,2,1,0:T(2,128)(2,1)S(1)}, u32[]{:S(2)}, u32[]{:S(2)}) collective-permute-start(bf16[4,18,1,256]{3,2,1,0:T(2,128)(2,1)S(1)} %pad_maximum_fusion.3), channel_id=1, source_target_pairs={{1,0},{2,1},{3,2},{5,4},{6,5},{7,6},{9,8},{10,9},{11,10},{13,12},{... | collective-permute-start | bytes 110600 | tf_op jit(solution)/shard_map/ppermute | solution.py:53
  15.7 0.1 pad_maximum_fusion.2
  15.8 5.4 %collective-permute-start.2 = (bf16[4,18,1,256]{3,2,1,0:T(2,128)(2,1)S(1)}, bf16[4,18,1,256]{3,2,1,0:T(2,128)(2,1)S(1)}, u32[]{:S(2)}, u32[]{:S(2)}) collective-permute-start(bf16[4,18,1,256]{3,2,1,0:T(2,128)(2,1)S(1)} %pad_maximum_fusion.2), channel_id=1, source_target_pairs={{0,1},{1,2},{2,3},{4,5},{5,6},{6,7},{8,9},{9,10},{10,11},{12,13},{... | collective-permute-start | bytes 110600 | tf_op jit(solution)/shard_map/ppermute | solution.py:53
  21.3 0.0 collective-permute-done.3.refs_4_
  21.3 1.3 collective-permute-done.2.refs_3_
  22.7 0.1 pad_maximum_fusion.8
  22.8 3.2 %collective-permute-start.5 = (bf16[200,256]{1,0:T(8,128)(2,1)S(1)}, bf16[200,256]{1,0:T(8,128)(2,1)S(1)}, u32[]{:S(2)}, u32[]{:S(2)}) collective-permute-start(bf16[200,256]{1,0:T(8,128)(2,1)S(1)} %pad_maximum_fusion), channel_id=1, source_target_pairs={{0,32},{32,64},{64,96},{1,33},{33,65},{65,97},{2,34},{34,66},{66,9... | collective-permute-start | bytes 307208 | tf_op jit(solution)/shard_map/ppermute | solution.py:53
  26.0 1.7 collective-permute-done.5
  27.7 0.0 collective-permute-done.4.refs_5_
  27.7 0.0 copy-start.4
  27.7 1.2 copy-done.4
  28.9 21.6 %shard_map.75 = (bf16[4,16,32,256]{3,2,1,0:T(8,128)(2,1)}, bf16[4,16,32,256]{3,2,1,0:T(8,128)(2,1)S(1)}, bf16[256,2048]{1,0:T(8,128)(2,1)S(1)}, bf16[3,6,18,32,2...) custom-call(bf16[4,16,32,256]{3,2,1,0:T(8,128)(2,1)S(1)} %copy-done.3, ...), custom_call_target="tpu_custom_call" | custom-call | flops 10871635968 | bytes 8388608 | tf_op jit(solution)/shard_map/pallas_call | solution.py:242
  50.6 0.0 collective-permute-start.12
  50.6 4.0 %collective-permute-done.12.received = bf16[14,256,256]{2,1,0:T(8,128)(2,1)S(1)} collective-permute-done((bf16[14,256,256]{2,1,0:T(8,128)(2,1)}, bf16[14,256,256]{2,1,0:T(8,128)(2,1)S(1)}, u32[]{:S(2)}, u32[]{:S(2)}) %collective-permute-start.12) | collective-permute-done | bytes 1835040 | tf_op jit(solution)/shard_map/ppermute | solution.py:254
  54.6 10.1 %shard_map.78 = bf16[14,256,256]{2,1,0:T(8,128)(2,1)} custom-call(bf16[3,6,18,32,256]{4,3,2,1,0:T(8,128)(2,1)} %get-tuple-element.13.taps, bf16[256,2048]{1,0:T(8,128)(2,1)S(1)} %get-tuple-element.14.dpre_t, bf16[14,256,256]{2,1,0:T(8,128)(2,1)S(1)} %collective-permute-done.12.received), custom_call_target="tpu_custom_call" | custom-call | flops 3623878656 | bytes 8388608 | tf_op jit(solution)/shard_map/pallas_call | solution.py:255
  64.7 10.7 %all-to-all-start = ((bf16[8,448,256]{2,1,0:T(8,128)(2,1)}), bf16[8,448,256]{2,1,0:T(8,128)(2,1)S(1)}, u32[]{:S(2)}, u32[]{:S(2)}) async-start(bf16[8,448,256]{2,1,0:T(8,128)(2,1)} %bitcast.15), calls=%async_computation | async-start | bytes 3670016 | tf_op jit(solution)/shard_map/all_to_all | solution.py:44
  75.4 15.8 %all-to-all-done = bf16[8,448,256]{2,1,0:T(8,128)(2,1)S(1)} async-done(((bf16[8,448,256]{2,1,0:T(8,128)(2,1)}), bf16[8,448,256]{2,1,0:T(8,128)(2,1)S(1)}, u32[]{:S(2)}, u32[]{:S(2)}) %all-to-all-start) | async-done | bytes 1835040 | tf_op jit(solution)/shard_map/all_to_all | solution.py:44
  91.2 0.2 convert_reduce_fusion
  91.5 0.8 fusion
  92.3 4.5 %all-to-all-start.1 = ((bf16[8,56,256]{2,1,0:T(8,128)(2,1)}), bf16[8,56,256]{2,1,0:T(8,128)(2,1)S(1)}, u32[]{:S(2)}, u32[]{:S(2)}) async-start(bf16[8,56,256]{2,1,0:T(8,128)(2,1)} %fusion), calls=%async_computation.1 | async-start | bytes 458752 | tf_op jit(solution)/shard_map/all_to_all | solution.py:44
  96.8 3.0 %all-to-all-done.1 = bf16[8,56,256]{2,1,0:T(8,128)(2,1)S(1)} async-done(((bf16[8,56,256]{2,1,0:T(8,128)(2,1)}), bf16[8,56,256]{2,1,0:T(8,128)(2,1)S(1)}, u32[]{:S(2)}, u32[]{:S(2)}) %all-to-all-start.1) | async-done | bytes 229408 | tf_op jit(solution)/shard_map/all_to_all | solution.py:44
  99.9 0.1 fusion.2
  100.0 7.4 %all_to_all.20 = bf16[8,56,256]{2,1,0:T(8,128)(2,1)S(1)} all-to-all(bf16[8,56,256]{2,1,0:T(8,128)(2,1)S(1)} %broadcast_in_dim.31), channel_id=1, replica_groups={{0,18,96,114,12,30,108,126},{16,2,112,98,28,14,124,110},{32,50,64,82,44..., dimensions={0} | all-to-all | bytes 458752 | tf_op jit(solution)/shard_map/all_to_all | solution.py:44
  107.4 1.3 broadcast_in_dim.33
  108.8 3.8 %all-to-all-start.3 = ((bf16[8,448,256]{2,1,0:T(8,128)(2,1)}), bf16[8,448,256]{2,1,0:T(8,128)(2,1)S(1)}, u32[]{:S(2)}, u32[]{:S(2)}) async-start(bf16[8,448,256]{2,1,0:T(8,128)(2,1)} %broadcast_in_dim.33), calls=%async_computation.3 | async-start | bytes 3670016 | tf_op jit(solution)/shard_map/all_to_all | solution.py:44
  112.5 3.1 %collective-permute-start.6 = (bf16[4,1,32,256]{3,2,1,0:T(8,128)(2,1)S(1)}, bf16[4,1,32,256]{3,2,1,0:T(8,128)(2,1)S(1)}, u32[]{:S(2)}, u32[]{:S(2)}) collective-permute-start(bf16[4,1,32,256]{3,2,1,0:T(8,128)(2,1)S(1)} %get-tuple-element.21), channel_id=1, source_target_pairs={{0,4},{4,8},{8,12},{12,16},{16,20},{20,24},{24,28},{1,5},{5,9},{9,... | collective-permute-start | bytes 196616 | tf_op jit(solution)/shard_map/ppermute | solution.py:53
  115.6 0.1 fusion.5
  115.7 0.8 slice.125
  116.6 1.3 collective-permute-start.7
  117.9 1.3 collective-permute-start.10
  119.2 0.0 collective-permute-done.6.refs_1_
  119.2 2.5 %collective-permute-done.7.refs_2_ = bf16[4,1,32,256]{3,2,1,0:T(8,128)(2,1)S(1)} collective-permute-done((bf16[4,1,32,256]{3,2,1,0:T(8,128)(2,1)S(1)}, bf16[4,1,32,256]{3,2,1,0:T(8,128)(2,1)S(1)}, u32[]{:S(2)}, u32[]{:S(2)}) %collective-permute-start.7) | collective-permute-done | bytes 65568 | tf_op jit(solution)/shard_map/ppermute | solution.py:53
  121.7 6.6 %all-to-all-done.3 = bf16[8,448,256]{2,1,0:T(8,128)(2,1)S(1)} async-done(((bf16[8,448,256]{2,1,0:T(8,128)(2,1)}), bf16[8,448,256]{2,1,0:T(8,128)(2,1)S(1)}, u32[]{:S(2)}, u32[]{:S(2)}) %all-to-all-start.3) | async-done | bytes 1835040 | tf_op jit(solution)/shard_map/all_to_all | solution.py:44
  128.3 14.1 %collective-permute-start.13 = (bf16[14,256,256]{2,1,0:T(8,128)(2,1)S(1)}, bf16[14,256,256]{2,1,0:T(8,128)(2,1)}, u32[]{:S(2)}, u32[]{:S(2)}) collective-permute-start(bf16[14,256,256]{2,1,0:T(8,128)(2,1)S(1)} %bitcast.38), channel_id=1, source_target_pairs={{0,1},{1,0},{2,3},{3,2},{4,5},{5,4},{6,7},{7,6},{8,9},{9,8},{10,11... | collective-permute-start | bytes 5505032 | tf_op jit(solution)/shard_map/ppermute | solution.py:273
  142.4 0.1 pad_maximum_fusion.5
  142.5 1.9 %collective-permute-start.9 = (bf16[4,18,1,256]{3,2,1,0:T(2,128)(2,1)S(1)}, bf16[4,18,1,256]{3,2,1,0:T(2,128)(2,1)S(1)}, u32[]{:S(2)}, u32[]{:S(2)}) collective-permute-start(bf16[4,18,1,256]{3,2,1,0:T(2,128)(2,1)S(1)} %pad_maximum_fusion.5), channel_id=1, source_target_pairs={{1,0},{2,1},{3,2},{5,4},{6,5},{7,6},{9,8},{10,9},{11,10},{13,12},{... | collective-permute-start | bytes 110600 | tf_op jit(solution)/shard_map/ppermute | solution.py:53
  144.4 0.1 pad_maximum_fusion.4
  144.5 5.1 %collective-permute-start.8 = (bf16[4,18,1,256]{3,2,1,0:T(2,128)(2,1)S(1)}, bf16[4,18,1,256]{3,2,1,0:T(2,128)(2,1)S(1)}, u32[]{:S(2)}, u32[]{:S(2)}) collective-permute-start(bf16[4,18,1,256]{3,2,1,0:T(2,128)(2,1)S(1)} %pad_maximum_fusion.4), channel_id=1, source_target_pairs={{0,1},{1,2},{2,3},{4,5},{5,6},{6,7},{8,9},{9,10},{10,11},{12,13},{... | collective-permute-start | bytes 110600 | tf_op jit(solution)/shard_map/ppermute | solution.py:53
  149.7 0.0 collective-permute-done.9.refs_4_
  149.8 1.3 collective-permute-done.8.refs_3_
  151.1 0.1 pad_maximum_fusion.9
  151.3 1.3 collective-permute-start.11
  152.6 0.0 copy-start
  152.6 2.0 %copy-done = bf16[27,256,256]{2,1,0:T(8,128)(2,1)S(1)} copy-done((bf16[27,256,256]{2,1,0:T(8,128)(2,1)S(1)}, bf16[27,256,256]{2,1,0:T(8,128)(2,1)}, u32[]{:S(2)}) %copy-start) | copy-done | bytes 3538968
  154.6 2.8 %shard_map.76 = bf16[27,256,256]{2,1,0:T(8,128)(2,1)S(1)} custom-call(bf16[27,256,256]{2,1,0:T(8,128)(2,1)S(1)} %copy-done), custom_call_target="tpu_custom_call" | custom-call | flops 1811939328 | bytes 8388608 | tf_op jit(solution)/shard_map/pallas_call | solution.py:237
  157.4 0.0 copy-start.1
  157.4 1.8 copy-done.1
  159.2 0.0 collective-permute-done.11
  159.2 0.0 collective-permute-done.10.refs_5_
  159.3 0.0 copy-start.2
  159.3 2.0 %copy-done.2 = bf16[27,256,256]{2,1,0:T(8,128)(2,1)S(1)} copy-done((bf16[27,256,256]{2,1,0:T(8,128)(2,1)S(1)}, bf16[27,256,256]{2,1,0:T(8,128)(2,1)}, u32[]{:S(2)}) %copy-start.2) | copy-done | bytes 3538968
  161.3 11.1 %shard_map.77 = bf16[4,16,32,256]{3,2,1,0:T(8,128)(2,1)} custom-call(bf16[4,16,32,256]{3,2,1,0:T(8,128)(2,1)S(1)} %get-tuple-element.12.refs_0_, bf16[4,1,32,256]{3,2,1,0:T(8,128)(2,1)S(1)} %collective-permute-done.6.refs_1_, bf16[4,1,32,256]{3,2,1,0:T(8,128)(2,1)S(1)} %collective-permute-done.7.refs_2_, ...), custom_call_target="tpu_custom_call" | custom-call | flops 7247757312 | bytes 8388608 | tf_op jit(solution)/shard_map/pallas_call | solution.py:276
  172.4 0.0 collective-permute-done.13.other
  172.4 15.2 %shard_map.79 = (f32[27,256,256]{2,1,0:T(8,128)}, f32[1,256]{1,0:T(1,128)}) custom-call(bf16[14,256,256]{2,1,0:T(8,128)(2,1)S(1)} %bitcast.39, bf16[14,256,256]{2,1,0:T(8,128)(2,1)} %collective-permute-done.13.other), custom_call_target="tpu_custom_call" | custom-call | tf_op jit(solution)/shard_map/pallas_call | solution.py:285
  (40 shorter events, 0.6 us)
Async XLA Ops:
  0.6 27.1 %copy-start.3 = (bf16[4,16,32,256]{3,2,1,0:T(8,128)(2,1)S(1)}, bf16[4,16,32,256]{3,2,1,0:T(8,128)(2,1)}, u32[]{:S(2)}) copy-start(bf16[4,16,32,256]{3,2,1,0:T(8,128)(2,1)} %refs_0_.1) | copy-start | bytes 3145732
  0.6 27.1 %copy-start.5 = (f32[256]{0:T(256)S(1)}, f32[256]{0:T(256)}, u32[]{:S(2)}) copy-start(f32[256]{0:T(256)} %param.6) | copy-start | bytes 3076
  1.6 10.7 %collective-permute-start = (bf16[4,1,32,256]{3,2,1,0:T(8,128)(2,1)S(1)}, bf16[4,1,32,256]{3,2,1,0:T(8,128)(2,1)S(1)}, u32[]{:S(2)}, u32[]{:S(2)}) collective-permute-start(bf16[4,1,32,256]{3,2,1,0:T(8,128)(2,1)S(1)} %get-tuple-element.25), channel_id=1, source_target_pairs={{0,4},{4,8},{8,12},{12,16},{16,20},{20,24},{24,28},{1,5},{5,9},{9,... | collective-permute-start | bytes 196616 | tf_op jit(solution)/shard_map/ppermute | solution.py:53
  5.6 6.8 %collective-permute-start.1 = (bf16[4,1,32,256]{3,2,1,0:T(8,128)(2,1)S(1)}, bf16[4,1,32,256]{3,2,1,0:T(8,128)(2,1)S(1)}, u32[]{:S(2)}, u32[]{:S(2)}) collective-permute-start(bf16[4,1,32,256]{3,2,1,0:T(8,128)(2,1)S(1)} %get-tuple-element.24), channel_id=1, source_target_pairs={{4,0},{8,4},{12,8},{16,12},{20,16},{24,20},{28,24},{5,1},{9,5},{13... | collective-permute-start | bytes 196616 | tf_op jit(solution)/shard_map/ppermute | solution.py:53
  8.0 19.7 %collective-permute-start.4 = (bf16[2,16,32,256]{3,2,1,0:T(8,128)(2,1)S(1)}, bf16[2,16,32,256]{3,2,1,0:T(8,128)(2,1)S(1)}, u32[]{:S(2)}, u32[]{:S(2)}) collective-permute-start(bf16[2,16,32,256]{3,2,1,0:T(8,128)(2,1)S(1)} %slice.110), channel_id=1, source_target_pairs={{0,32},{32,64},{64,96},{1,33},{33,65},{65,97},{2,34},{34,66},{66,9... | collective-permute-start | bytes 1572872 | tf_op jit(solution)/shard_map/ppermute | solution.py:53
  12.5 8.7 %collective-permute-start.3 = (bf16[4,18,1,256]{3,2,1,0:T(2,128)(2,1)S(1)}, bf16[4,18,1,256]{3,2,1,0:T(2,128)(2,1)S(1)}, u32[]{:S(2)}, u32[]{:S(2)}) collective-permute-start(bf16[4,18,1,256]{3,2,1,0:T(2,128)(2,1)S(1)} %pad_maximum_fusion.3), channel_id=1, source_target_pairs={{1,0},{2,1},{3,2},{5,4},{6,5},{7,6},{9,8},{10,9},{11,10},{13,12},{... | collective-permute-start | bytes 110600 | tf_op jit(solution)/shard_map/ppermute | solution.py:53
  15.8 6.8 %collective-permute-start.2 = (bf16[4,18,1,256]{3,2,1,0:T(2,128)(2,1)S(1)}, bf16[4,18,1,256]{3,2,1,0:T(2,128)(2,1)S(1)}, u32[]{:S(2)}, u32[]{:S(2)}) collective-permute-start(bf16[4,18,1,256]{3,2,1,0:T(2,128)(2,1)S(1)} %pad_maximum_fusion.2), channel_id=1, source_target_pairs={{0,1},{1,2},{2,3},{4,5},{5,6},{6,7},{8,9},{9,10},{10,11},{12,13},{... | collective-permute-start | bytes 110600 | tf_op jit(solution)/shard_map/ppermute | solution.py:53
  22.8 4.8 %collective-permute-start.5 = (bf16[200,256]{1,0:T(8,128)(2,1)S(1)}, bf16[200,256]{1,0:T(8,128)(2,1)S(1)}, u32[]{:S(2)}, u32[]{:S(2)}) collective-permute-start(bf16[200,256]{1,0:T(8,128)(2,1)S(1)} %pad_maximum_fusion), channel_id=1, source_target_pairs={{0,32},{32,64},{64,96},{1,33},{33,65},{65,97},{2,34},{34,66},{66,9... | collective-permute-start | bytes 307208 | tf_op jit(solution)/shard_map/ppermute | solution.py:53
  27.7 1.2 copy-start.4
  50.6 4.0 %collective-permute-start.12 = (bf16[14,256,256]{2,1,0:T(8,128)(2,1)}, bf16[14,256,256]{2,1,0:T(8,128)(2,1)S(1)}, u32[]{:S(2)}, u32[]{:S(2)}) collective-permute-start(bf16[14,256,256]{2,1,0:T(8,128)(2,1)} %get-tuple-element.15), channel_id=1, source_target_pairs={{0,1},{1,0},{2,3},{3,2},{4,5},{5,4},{6,7},{7,6},{8,9},{9,8},{10,11... | collective-permute-start | bytes 5505032 | tf_op jit(solution)/shard_map/ppermute | solution.py:254
  64.7 26.5 %all-to-all-start = ((bf16[8,448,256]{2,1,0:T(8,128)(2,1)}), bf16[8,448,256]{2,1,0:T(8,128)(2,1)S(1)}, u32[]{:S(2)}, u32[]{:S(2)}) async-start(bf16[8,448,256]{2,1,0:T(8,128)(2,1)} %bitcast.15), calls=%async_computation | async-start | bytes 3670016 | tf_op jit(solution)/shard_map/all_to_all | solution.py:44
  92.3 7.5 %all-to-all-start.1 = ((bf16[8,56,256]{2,1,0:T(8,128)(2,1)}), bf16[8,56,256]{2,1,0:T(8,128)(2,1)S(1)}, u32[]{:S(2)}, u32[]{:S(2)}) async-start(bf16[8,56,256]{2,1,0:T(8,128)(2,1)} %fusion), calls=%async_computation.1 | async-start | bytes 458752 | tf_op jit(solution)/shard_map/all_to_all | solution.py:44
  108.8 19.5 %all-to-all-start.3 = ((bf16[8,448,256]{2,1,0:T(8,128)(2,1)}), bf16[8,448,256]{2,1,0:T(8,128)(2,1)S(1)}, u32[]{:S(2)}, u32[]{:S(2)}) async-start(bf16[8,448,256]{2,1,0:T(8,128)(2,1)} %broadcast_in_dim.33), calls=%async_computation.3 | async-start | bytes 3670016 | tf_op jit(solution)/shard_map/all_to_all | solution.py:44
  112.5 6.6 %collective-permute-start.6 = (bf16[4,1,32,256]{3,2,1,0:T(8,128)(2,1)S(1)}, bf16[4,1,32,256]{3,2,1,0:T(8,128)(2,1)S(1)}, u32[]{:S(2)}, u32[]{:S(2)}) collective-permute-start(bf16[4,1,32,256]{3,2,1,0:T(8,128)(2,1)S(1)} %get-tuple-element.21), channel_id=1, source_target_pairs={{0,4},{4,8},{8,12},{12,16},{16,20},{20,24},{24,28},{1,5},{5,9},{9,... | collective-permute-start | bytes 196616 | tf_op jit(solution)/shard_map/ppermute | solution.py:53
  116.6 5.1 %collective-permute-start.7 = (bf16[4,1,32,256]{3,2,1,0:T(8,128)(2,1)S(1)}, bf16[4,1,32,256]{3,2,1,0:T(8,128)(2,1)S(1)}, u32[]{:S(2)}, u32[]{:S(2)}) collective-permute-start(bf16[4,1,32,256]{3,2,1,0:T(8,128)(2,1)S(1)} %get-tuple-element.20), channel_id=1, source_target_pairs={{4,0},{8,4},{12,8},{16,12},{20,16},{24,20},{28,24},{5,1},{9,5},{13... | collective-permute-start | bytes 196616 | tf_op jit(solution)/shard_map/ppermute | solution.py:53
  117.9 41.4 %collective-permute-start.10 = (bf16[2,16,32,256]{3,2,1,0:T(8,128)(2,1)}, bf16[2,16,32,256]{3,2,1,0:T(8,128)(2,1)}, u32[]{:S(2)}, u32[]{:S(2)}) collective-permute-start(bf16[2,16,32,256]{3,2,1,0:T(8,128)(2,1)} %slice.125), channel_id=1, source_target_pairs={{32,0},{64,32},{96,64},{33,1},{65,33},{97,65},{34,2},{66,34},{98,6... | collective-permute-start | bytes 1572872 | tf_op jit(solution)/shard_map/ppermute | solution.py:53
  128.3 44.1 %collective-permute-start.13 = (bf16[14,256,256]{2,1,0:T(8,128)(2,1)S(1)}, bf16[14,256,256]{2,1,0:T(8,128)(2,1)}, u32[]{:S(2)}, u32[]{:S(2)}) collective-permute-start(bf16[14,256,256]{2,1,0:T(8,128)(2,1)S(1)} %bitcast.38), channel_id=1, source_target_pairs={{0,1},{1,0},{2,3},{3,2},{4,5},{5,4},{6,7},{7,6},{8,9},{9,8},{10,11... | collective-permute-start | bytes 5505032 | tf_op jit(solution)/shard_map/ppermute | solution.py:273
  142.5 7.3 %collective-permute-start.9 = (bf16[4,18,1,256]{3,2,1,0:T(2,128)(2,1)S(1)}, bf16[4,18,1,256]{3,2,1,0:T(2,128)(2,1)S(1)}, u32[]{:S(2)}, u32[]{:S(2)}) collective-permute-start(bf16[4,18,1,256]{3,2,1,0:T(2,128)(2,1)S(1)} %pad_maximum_fusion.5), channel_id=1, source_target_pairs={{1,0},{2,1},{3,2},{5,4},{6,5},{7,6},{9,8},{10,9},{11,10},{13,12},{... | collective-permute-start | bytes 110600 | tf_op jit(solution)/shard_map/ppermute | solution.py:53
  144.5 6.5 %collective-permute-start.8 = (bf16[4,18,1,256]{3,2,1,0:T(2,128)(2,1)S(1)}, bf16[4,18,1,256]{3,2,1,0:T(2,128)(2,1)S(1)}, u32[]{:S(2)}, u32[]{:S(2)}) collective-permute-start(bf16[4,18,1,256]{3,2,1,0:T(2,128)(2,1)S(1)} %pad_maximum_fusion.4), channel_id=1, source_target_pairs={{0,1},{1,2},{2,3},{4,5},{5,6},{6,7},{8,9},{9,10},{10,11},{12,13},{... | collective-permute-start | bytes 110600 | tf_op jit(solution)/shard_map/ppermute | solution.py:53
  151.3 7.9 %collective-permute-start.11 = (bf16[200,256]{1,0:T(8,128)(2,1)S(1)}, bf16[200,256]{1,0:T(8,128)(2,1)S(1)}, u32[]{:S(2)}, u32[]{:S(2)}) collective-permute-start(bf16[200,256]{1,0:T(8,128)(2,1)S(1)} %pad_maximum_fusion.1), channel_id=1, source_target_pairs={{32,0},{64,32},{96,64},{33,1},{65,33},{97,65},{34,2},{66,34},{98,6... | collective-permute-start | bytes 307208 | tf_op jit(solution)/shard_map/ppermute | solution.py:53
  152.6 2.0 %copy-start = (bf16[27,256,256]{2,1,0:T(8,128)(2,1)S(1)}, bf16[27,256,256]{2,1,0:T(8,128)(2,1)}, u32[]{:S(2)}) copy-start(bf16[27,256,256]{2,1,0:T(8,128)(2,1)} %kernel.1) | copy-start | bytes 10616836
  157.4 1.8 copy-start.1
  159.3 2.0 %copy-start.2 = (bf16[27,256,256]{2,1,0:T(8,128)(2,1)S(1)}, bf16[27,256,256]{2,1,0:T(8,128)(2,1)}, u32[]{:S(2)}) copy-start(bf16[27,256,256]{2,1,0:T(8,128)(2,1)} %copy-done.1) | copy-start | bytes 10616836
where the time goes:
time: 189 us; the launch traced here: 188 us
  starting transfers between devices  67.3 us (36%)
  Pallas kernels  60.9 us (32%)
  waiting for transfers between devices  36 us (19%)
  local copies, waits for them, and re-layouts  12.9 us (7%)
  blocking collectives  7.44 us (4%)
    ppermute x12, starting transfers between devices, shift(): return lax.ppermute(block, axis, route)  34.2 us
    all_to_all x3, waiting for transfers between devices, exchange(): return lax.all_to_all(pieces, AXES, 0, 0, axis_index_groups=groups)  25.3 us
    pallas_call x1, Pallas kernels, shards(): call(forward_kernel, (block, block, jax.ShapeDtypeStruct((256, 2048), BF)...  21.6 us
    all_to_all x3, starting transfers between devices, exchange(): return lax.all_to_all(pieces, AXES, 0, 0, axis_index_groups=groups)  19 us
    pallas_call x1, Pallas kernels, shards(): pl.pallas_call(functools.partial(finish_kernel, scale), grid=(28,), out_s...  15.2 us
    ppermute x1, starting transfers between devices, shards(): other = lax.ppermute(mine, 'wc', [(0, 1), (1, 0)])  14.1 us
    pallas_call x1, Pallas kernels, shards(): call(backward_kernel, block, (pltpu.VMEM((3, 6, 18, 32, 256), BF),), flop...  11.1 us
    pallas_call x1, Pallas kernels, shards(): call(weight_kernel, half, flops=conv_flops // 2, n_in=3)  10.1 us
  transfers between devices with their start and end apart: 17, of which 8 were waited for; matrix products, arithmetic and copies ran while one was open for 2% of the time, Pallas kernels for 7%

commit v1 on v0

--- a/solution.py
+++ b/solution.py
@@ -15,7 +15,6 @@
 WA = ("wz", "wc")
 BF = jnp.bfloat16
 F32 = jnp.float32
-HALF = 14
 VMEM = pl.BlockSpec(memory_space=pltpu.VMEM)
 MIB = 1 << 20
 
@@ -99,9 +98,38 @@
     return piece.reshape(-1, piece.shape[-1])
 
 
+def weight_terms(taps, slope, half, emit):
+    lanes = pl.ds(pl.multiple_of(half * 128, 128), 128)
+
+    @pl.loop(0, 3)
+    def _(a):
+        pieces = [
+            taps[c, pl.ds(a, 4), b : b + 16, :, lanes].reshape(2048, 128)
+            for b in range(3)
+            for c in range(3)
+        ]
+        value = lax.dot_general(
+            jnp.concatenate(pieces, axis=1),
+            slope[...].reshape(2048, 256),
+            (((0,), (0,)), ((), ())),
+            preferred_element_type=F32,
+        )
+        emit(pl.ds(9 * a, 9), value.reshape(9, 128, 256))
+
+
+def bias_rows(value):
+    high = value.astype(BF).astype(F32)
+    return jnp.concatenate([high, value - high, jnp.zeros((112, 256), F32)], axis=0)
+
+
+def bias_term(slope):
+    total = jnp.sum(slope[...].reshape(2048, 256).astype(F32), axis=0, keepdims=True)
+    return jnp.broadcast_to(total, (8, 256))
+
+
 def forward_kernel(*refs):
     parts, (kernel, bias, cotangent), rest = refs[:8], refs[8:11], refs[11:]
-    activation, dpre, dpre_t, taps, send = rest
+    activation, dpre, taps, send = rest
     place(parts, 2, 0, taps)
 
     @pl.loop(0, 4)
@@ -117,40 +145,44 @@
         cot = cotangent[t].reshape(512, 256).astype(F32)
         slope = cot * sig * (1.0 + total * (1.0 - sig))
         dpre[t] = slope.astype(BF).reshape(16, 32, 256)
-        dpre_t[:, pl.ds(pl.multiple_of(t * 512, 512), 512)] = slope.T.astype(BF)
-
-    first = HALF * (1 - lax.axis_index("wc"))
-
-    def emit(j, value):
-        send[j] = value.astype(BF)
-
-    weight_terms(taps, dpre_t, first, emit)
-
-
-def weight_terms(taps, dpre_t, first, emit):
-    @pl.loop(0, HALF)
-    def _(j):
-        k = first + j
-
-        @pl.when(k < 27)
-        def _():
-            a, b, c = k // 9, (k // 3) % 3, k % 3
-            block = taps[c, pl.ds(a, 4), pl.ds(b, 16)].reshape(2048, 256)
-            emit(j, jnp.dot(dpre_t[...], block, preferred_element_type=F32))
-
-        @pl.when(k == 27)
-        def _():
-            total = jnp.sum(dpre_t[...].astype(F32), axis=1, keepdims=True)
-            high = total.astype(BF).astype(F32)
-            lane = lax.broadcasted_iota(jnp.int32, (256, 256), 1)
-            emit(j, jnp.where(lane < 128, high, total - high))
-
-
-def weight_kernel(taps, dpre_t, received, out):
-    def emit(j, value):
-        out[j] = (value + received[j].astype(F32)).astype(BF)
-
-    weight_terms(taps, dpre_t, HALF * lax.axis_index("wc"), emit)
+
+    def emit(at, value):
+        send[at] = value.astype(BF)
+
+    weight_terms(taps, dpre, 1 - lax.axis_index("wc"), emit)
+    send[27] = bias_rows(bias_term(dpre)).astype(BF)
+
+
+def weight_kernel(taps, dpre, out):
+    def emit(at, value):
+        out[at] = value
+
+    weight_terms(taps, dpre, lax.axis_index("wc"), emit)
+    out[27, 0:8] = bias_term(dpre)
+
+
+def join_kernel(own, received, out):
+    out[0:27] = (own[0:27] + received[0:27].astype(F32)).astype(BF)
+    value = own[27, 0:8] + received[27, 0:8].astype(F32) + received[27, 8:16].astype(F32)
+    out[27] = bias_rows(value).astype(BF)
+
+
+def sum_kernel(local, pieces, flag, out):
+    total = pieces[0].astype(F32)
+    for i in range(1, 8):
+        total = total + pieces[i].astype(F32)
+    rows = total.shape[0]
+    total = total.astype(BF)
+    copies = out.shape[0] // rows
+    for i in range(copies):
+        out[i * rows : (i + 1) * rows] = total
+
+    @pl.when(flag[0] == 1)
+    def _():
+        value = sum(pieces[i, local : local + 16].astype(F32) for i in range(8))
+        value = bias_rows(value[0:8] + value[8:16])[0:16].astype(BF)
+        for i in range(copies):
+            out[i * rows + local : i * rows + local + 16] = value
 
 
 def backward_kernel(*refs):
@@ -174,42 +206,19 @@
         out[k] = kernel[k].astype(F32).T.astype(BF)
 
 
-def finish_kernel(scale, mine, other, kernel_grad, bias_grad):
-    step = pl.program_id(0)
-    k = jnp.where(step == 0, 27, step - 1)
+def finish_kernel(scale, mine, other, bias_mine, kernel_grad, bias_grad):
     core = lax.axis_index("wc")
-    row = lax.broadcasted_iota(jnp.int32, (256, 256), 0)
-    lane = lax.broadcasted_iota(jnp.int32, (256, 256), 1)
-    unit = jnp.where(row == lane, 1.0, 0.0).astype(BF)
-
-    def flip(block):
-        turned = lax.dot_general(unit, block, (((1,), (1,)), ((), ())), preferred_element_type=F32)
-
-        @pl.when(step == 0)
-        def _():
-            bias_grad[...] = (turned[0:1] + turned[128:129]) * scale
-
-        @pl.when(step > 0)
-        def _():
-            kernel_grad[0] = turned * scale
-
-    owner = k // HALF
-    j = k - HALF * owner
-
-    @pl.when(owner == core)
-    def _():
-        flip(mine[j])
-
-    @pl.when(owner != core)
-    def _():
-        flip(other[j])
-
-
-def call(body, outs, scratch=(), vmem=48, flops=0, n_in=0):
+    kernel_grad[:, pl.ds(pl.multiple_of(core * 128, 128), 128)] = mine[...].astype(F32) * scale
+    at = pl.ds(pl.multiple_of(128 - core * 128, 128), 128)
+    kernel_grad[:, at] = other[...].astype(F32) * scale
+    bias_grad[...] = (bias_mine[0, 0:1].astype(F32) + bias_mine[0, 8:9].astype(F32)) * scale
+
+
+def call(body, outs, scratch=(), vmem=24, flops=0, specs=(), n_in=0):
     return pl.pallas_call(
         body,
         out_shape=outs,
-        in_specs=[VMEM] * n_in,
+        in_specs=list(specs) or [VMEM] * n_in,
         out_specs=jax.tree.map(lambda _: VMEM, outs),
         scratch_shapes=list(scratch),
         compiler_params=pltpu.CompilerParams(vmem_limit_bytes=vmem * MIB),
@@ -217,12 +226,14 @@
     )
 
 
-def sum_pieces(pieces, special):
-    total = jnp.sum(pieces.astype(F32), axis=0)
-    value = total[:, :128] + total[:, 128:]
-    high = lax.reduce_precision(value, 8, 7)
-    split = jnp.concatenate([high, value - high], axis=1)
-    return jnp.where(special, split, total).astype(BF)
+def sum_pieces(pieces, local, special, copies):
+    rows = pieces.shape[1]
+    return call(
+        functools.partial(sum_kernel, local),
+        jax.ShapeDtypeStruct((copies * rows, 256), BF),
+        vmem=12,
+        specs=(VMEM, pl.BlockSpec(memory_space=pltpu.SMEM)),
+    )(pieces, special.astype(jnp.int32).reshape(1))
 
 
 def shards(latent, kernel, bias, cotangent):
@@ -233,46 +244,43 @@
     scale = float(1.0 / np.sqrt(np.float32(cells)))
     conv_flops = 2 * 2048 * 27 * 256 * 256
     block = jax.ShapeDtypeStruct(latent.shape, BF)
+    half = (28, 128, 256)
 
     turned = call(
         turn_kernel, jax.ShapeDtypeStruct(kernel.shape, BF), vmem=16, flops=conv_flops // 4, n_in=1
     )(kernel)
     padded = halo(latent, lambda x: x[2:], 1)
-    half = jax.ShapeDtypeStruct((HALF, 256, 256), BF)
-    activation, dpre, dpre_t, taps, send = call(
+    padded, turned = lax.optimization_barrier((padded, turned))
+    activation, dpre, taps, send = call(
         forward_kernel,
         (
             block,
             block,
-            jax.ShapeDtypeStruct((256, 2048), BF),
             jax.ShapeDtypeStruct((3, 6, 18, 32, 256), BF),
-            half,
+            jax.ShapeDtypeStruct(half, BF),
         ),
+        vmem=28,
         flops=conv_flops * 3 // 2,
         n_in=11,
     )(*padded, kernel.reshape(3, 2304, 256), bias.reshape(1, 256), cotangent)
     received = lax.ppermute(send, "wc", [(0, 1), (1, 0)])
-    terms = call(weight_kernel, half, flops=conv_flops // 2, n_in=3)(taps, dpre_t, received)
+    own = call(
+        weight_kernel, jax.ShapeDtypeStruct(half, F32), flops=conv_flops // 2, n_in=2
+    )(taps, dpre)
+    terms = call(join_kernel, jax.ShapeDtypeStruct(half, BF), vmem=16, n_in=2)(own, received)
 
     core = lax.axis_index("wc")
     z = 2 * lax.axis_index("wz") + lax.axis_index("hz")
     spot = [(p - core) % 4 for p in (lax.axis_index("hx"), lax.axis_index("ta"), z)]
     near = sum(w * ((p == 1) | (p == 2)) for w, p in zip((4, 2, 1), spot))
     far = sum(w * (p >= 2) for w, p in zip((4, 2, 1), spot))
-    first_bias = (HALF - 1) * 256
-
     pieces = exchange(terms.reshape(8, 448, 256), NEAR)
-    row = near * 448 + lax.broadcasted_iota(jnp.int32, (448, 1), 0)
-    total = sum_pieces(pieces, (core == 1) & (row >= first_bias))
+    spread = halo(dpre, lambda x: x[:2], -1)
+    total = sum_pieces(pieces, 320, near == 7, 1)
     pieces = exchange(total.reshape(8, 56, 256), FAR)
-    row = near * 448 + far * 56 + lax.broadcasted_iota(jnp.int32, (56, 1), 0)
-    total = sum_pieces(pieces, (core == 1) & (row >= first_bias))
-    total = exchange(jnp.broadcast_to(total[None], (8, 56, 256)), FAR).reshape(448, 256)
-    total = exchange(jnp.broadcast_to(total[None], (8, 448, 256)), NEAR)
-    mine = total.reshape(HALF, 256, 256)
-    other = lax.ppermute(mine, "wc", [(0, 1), (1, 0)])
-
-    spread = halo(dpre, lambda x: x[:2], -1)
+    total = sum_pieces(pieces, 40, (near == 7) & (far == 5), 8)
+    total, spread = lax.optimization_barrier((total, spread))
+    total = exchange(total.reshape(8, 56, 256), FAR).reshape(448, 256)
     latent_grad = call(
         backward_kernel,
         block,
@@ -280,22 +288,26 @@
         flops=conv_flops,
         n_in=9,
     )(*spread, turned.reshape(3, 2304, 256))
-
-    whole = pl.BlockSpec((HALF, 256, 256), lambda k: (0, 0, 0))
+    total = exchange(jnp.broadcast_to(total[None], (8, 448, 256)), NEAR)
+    total, latent_grad = lax.optimization_barrier((total, latent_grad))
+    mine = total.reshape(half)
+    other = lax.ppermute(mine, "wc", [(0, 1), (1, 0)])
+
+    part = pl.BlockSpec((3, 128, 256), lambda k: (k, 0, 0))
     kernel_grad, bias_grad = pl.pallas_call(
         functools.partial(finish_kernel, scale),
-        grid=(28,),
+        grid=(9,),
         out_shape=(
             jax.ShapeDtypeStruct((27, 256, 256), F32),
             jax.ShapeDtypeStruct((1, 256), F32),
         ),
-        in_specs=[whole, whole],
+        in_specs=[part, part, pl.BlockSpec((1, 128, 256), lambda k: (27, 0, 0))],
         out_specs=(
-            pl.BlockSpec((1, 256, 256), lambda k: (jnp.maximum(k - 1, 0), 0, 0)),
+            pl.BlockSpec((3, 256, 256), lambda k: (k, 0, 0)),
             pl.BlockSpec((1, 256), lambda k: (0, 0)),
         ),
-        compiler_params=pltpu.CompilerParams(vmem_limit_bytes=24 * MIB),
-    )(mine, other)
+        compiler_params=pltpu.CompilerParams(vmem_limit_bytes=12 * MIB),
+    )(mine, other, mine)
     return (activation, latent_grad, kernel_grad, bias_grad.reshape(256))
 
 

time: 189 us -> 168 us (0.89)
  Pallas kernels: 60.9 us -> 42.1 us
  local copies, waits for them, and re-layouts: 12.9 us -> 31 us
  waiting for transfers between devices: 36 us -> 21.3 us
  starting transfers between devices: 67.3 us -> 63.4 us
    all_to_all x3, waiting for transfers between devices: 25.3 us -> 2.49 us  [exchange(): return lax.all_to_all(pieces, AXES, 0, 0, axis_index_groups=groups)]
    pallas_call x3 -> x6, Pallas kernels: 46.9 us -> 28.2 us  [the longest x1 16.3 us: shards(): call(forward_kernel, (block, block, jax.ShapeDtypeStruct((3, 6, 18, 32, 2...]
    unnamed x12 -> x40, local copies, waits for them, and re-layouts: 7.01 us -> 19.9 us
    ppermute x12, waiting for transfers between devices: 6.71 us -> 15.4 us  [shift(): return lax.ppermute(block, axis, route)]
    ppermute x12, starting transfers between devices: 34.2 us -> 42.3 us  [shift(): return lax.ppermute(block, axis, route)]
    ppermute x1, starting transfers between devices: 14.1 us -> 7.56 us  [shards(): other = lax.ppermute(mine, 'wc', [(0, 1), (1, 0)])]
    all_to_all x3, starting transfers between devices: 19 us -> 13.6 us  [exchange(): return lax.all_to_all(pieces, AXES, 0, 0, axis_index_groups=groups)]
    ppermute x1, waiting for transfers between devices: 3.99 us -> 0.01 us  [shards(): received = lax.ppermute(send, 'wc', [(0, 1), (1, 0)])]
  transfers between devices with their start and end apart: 17 -> 17, of which waited for: 8 -> 6; matrix products, arithmetic and copies ran while one was open for 2% -> 5% of each run, Pallas kernels for 7% -> 12%
where the time goes in v1:
time: 168 us; the launch traced here: 167 us
  starting transfers between devices  63.4 us (38%)
  Pallas kernels  42.1 us (25%)
  local copies, waits for them, and re-layouts  31 us (18%)
  waiting for transfers between devices  21.3 us (13%)
  blocking collectives  7 us (4%)
    ppermute x12, starting transfers between devices, shift(): return lax.ppermute(block, axis, route)  42.3 us
    unnamed x40, local copies, waits for them, and re-layouts  19.9 us
    pallas_call x1, Pallas kernels, shards(): call(forward_kernel, (block, block, jax.ShapeDtypeStruct((3, 6, 18, 32, 2...  16.3 us
    ppermute x12, waiting for transfers between devices, shift(): return lax.ppermute(block, axis, route)  15.4 us
    all_to_all x3, starting transfers between devices, exchange(): return lax.all_to_all(pieces, AXES, 0, 0, axis_index_groups=groups)  13.6 us
    pallas_call x1, Pallas kernels, shards(): call(backward_kernel, block, (pltpu.VMEM((3, 6, 18, 32, 256), BF),), flop...  11.1 us
    ppermute x1, starting transfers between devices, shards(): other = lax.ppermute(mine, 'wc', [(0, 1), (1, 0)])  7.56 us
    all_to_all x1, blocking collectives, exchange(): return lax.all_to_all(pieces, AXES, 0, 0, axis_index_groups=groups)  7 us
  transfers between devices with their start and end apart: 17, of which 6 were waited for; matrix products, arithmetic and copies ran while one was open for 5% of the time, Pallas kernels for 12%

profile of v1, /device:TPU:1, one launch (start us, length us, event | category | flops | bytes accessed | tf_op | source)
XLA Modules:
  0.0 166.7 jit_solution(18199572140439428254)
XLA Ops:
  0.6 0.9 fusion.3
  1.5 3.9 %collective-permute-start = (bf16[4,1,32,256]{3,2,1,0:T(8,128)(2,1)S(1)}, bf16[4,1,32,256]{3,2,1,0:T(8,128)(2,1)S(1)}, u32[]{:S(2)}, u32[]{:S(2)}) collective-permute-start(bf16[4,1,32,256]{3,2,1,0:T(8,128)(2,1)S(1)} %get-tuple-element.63), channel_id=1, source_target_pairs={{0,4},{4,8},{8,12},{12,16},{16,20},{20,24},{24,28},{1,5},{5,9},{9,... | collective-permute-start | bytes 196616 | tf_op jit(solution)/shard_map/ppermute | solution.py:52
  5.5 1.3 collective-permute-start.1
  6.8 1.9 %slice.98 = bf16[2,16,32,256]{3,2,1,0:T(8,128)(2,1)} slice(bf16[4,16,32,256]{3,2,1,0:T(8,128)(2,1)} %refs_0_), slice={[2:4], [0:16], [0:32], [0:256]} | slice | bytes 1048576 | tf_op jit(solution)/shard_map/slice | solution.py:252
  8.6 4.0 %collective-permute-start.4 = (bf16[2,16,32,256]{3,2,1,0:T(8,128)(2,1)}, bf16[2,16,32,256]{3,2,1,0:T(8,128)(2,1)}, u32[]{:S(2)}, u32[]{:S(2)}) collective-permute-start(bf16[2,16,32,256]{3,2,1,0:T(8,128)(2,1)} %slice.98), channel_id=1, source_target_pairs={{0,32},{32,64},{64,96},{1,33},{33,65},{65,97},{2,34},{34,66},{66,9... | collective-permute-start | bytes 1572872 | tf_op jit(solution)/shard_map/ppermute | solution.py:52
  12.7 1.1 fusion.2
  13.8 0.0 collective-permute-done.1.refs_2_
  13.9 0.1 pad_maximum_fusion.2
  14.0 6.6 %collective-permute-start.2 = (bf16[4,18,1,256]{3,2,1,0:T(2,128)(2,1)S(1)}, bf16[4,18,1,256]{3,2,1,0:T(2,128)(2,1)S(1)}, u32[]{:S(2)}, u32[]{:S(2)}) collective-permute-start(bf16[4,18,1,256]{3,2,1,0:T(2,128)(2,1)S(1)} %pad_maximum_fusion.2), channel_id=1, source_target_pairs={{0,1},{1,2},{2,3},{4,5},{5,6},{6,7},{8,9},{9,10},{10,11},{12,13},{... | collective-permute-start | bytes 110600 | tf_op jit(solution)/shard_map/ppermute | solution.py:52
  20.6 0.1 pad_maximum_fusion.3
  20.8 1.9 %collective-permute-start.3 = (bf16[4,18,1,256]{3,2,1,0:T(2,128)(2,1)S(1)}, bf16[4,18,1,256]{3,2,1,0:T(2,128)(2,1)S(1)}, u32[]{:S(2)}, u32[]{:S(2)}) collective-permute-start(bf16[4,18,1,256]{3,2,1,0:T(2,128)(2,1)S(1)} %pad_maximum_fusion.3), channel_id=1, source_target_pairs={{1,0},{2,1},{3,2},{5,4},{6,5},{7,6},{9,8},{10,9},{11,10},{13,12},{... | collective-permute-start | bytes 110600 | tf_op jit(solution)/shard_map/ppermute | solution.py:52
  22.7 5.2 %collective-permute-done.3.refs_4_ = bf16[4,18,1,256]{3,2,1,0:T(2,128)(2,1)S(1)} collective-permute-done((bf16[4,18,1,256]{3,2,1,0:T(2,128)(2,1)S(1)}, bf16[4,18,1,256]{3,2,1,0:T(2,128)(2,1)S(1)}, u32[]{:S(2)}, u32[]{:S(2)}) %collective-permute-start.3) | collective-permute-done | bytes 36896 | tf_op jit(solution)/shard_map/ppermute | solution.py:52
  28.1 0.5 copy-done.14
  28.6 0.6 copy-done.12
  29.2 0.1 pad_maximum_fusion.8
  29.3 3.0 %collective-permute-start.5 = (bf16[200,256]{1,0:T(8,128)(2,1)S(1)}, bf16[200,256]{1,0:T(8,128)(2,1)}, u32[]{:S(2)}, u32[]{:S(2)}) collective-permute-start(bf16[200,256]{1,0:T(8,128)(2,1)S(1)} %pad_maximum_fusion), channel_id=1, source_target_pairs={{0,32},{32,64},{64,96},{1,33},{33,65},{65,97},{2,34},{34,66},{66,9... | collective-permute-start | bytes 307208 | tf_op jit(solution)/shard_map/ppermute | solution.py:52
  32.4 2.0 %copy-done = bf16[27,256,256]{2,1,0:T(8,128)(2,1)S(1)} copy-done((bf16[27,256,256]{2,1,0:T(8,128)(2,1)S(1)}, bf16[27,256,256]{2,1,0:T(8,128)(2,1)}, u32[]{:S(2)}) %copy-start) | copy-done | bytes 3538968
  34.4 2.8 %shard_map.75 = bf16[27,256,256]{2,1,0:T(8,128)(2,1)S(1)} custom-call(bf16[27,256,256]{2,1,0:T(8,128)(2,1)S(1)} %copy-done), custom_call_target="tpu_custom_call" | custom-call | flops 1811939328 | bytes 8388608 | tf_op jit(solution)/shard_map/pallas_call | solution.py:249
  37.2 1.7 %copy-done.2 = bf16[27,256,256]{2,1,0:T(8,128)(2,1)} copy-done((bf16[27,256,256]{2,1,0:T(8,128)(2,1)}, bf16[27,256,256]{2,1,0:T(8,128)(2,1)S(1)}, u32[]{:S(2)}) %copy-start.2) | copy-done | bytes 3538968
  39.0 1.4 slice.129
  40.4 1.4 reshape.70
  41.8 0.8 slice.128
  42.6 0.9 copy.35.refs_7_
  43.5 0.0 copy-start.4
  43.5 1.2 copy-done.4
  44.7 0.8 copy-done.9
  45.6 0.8 copy-done.11
  46.4 0.9 copy-done.13
  47.3 0.9 copy-done.15
  48.2 1.2 copy-done.16
  49.4 16.3 %shard_map.76 = (bf16[4,16,32,256]{3,2,1,0:T(8,128)(2,1)}, bf16[4,16,32,256]{3,2,1,0:T(8,128)(2,1)S(1)}, bf16[3,6,18,32,256]{4,3,2,1,0:T(8,128)(2,1)S(1)}, bf16[28,128,256]{2,1,0:T(8,128)(2,1)}) custom-call(bf16[4,16,32,256]{3,2,1,0:T(8,128)(2,1)S(1)} %copy-done.4, bf16[4,1,32,256]{3,2,1,0:T(8,128)(2,1)S(1)} %copy-done.9, ...), custom_call_target="tpu_custom_call" | custom-call | flops 10871635968 | bytes 8388608 | tf_op jit(solution)/shard_map/pallas_call | solution.py:254
  65.7 1.0 copy-done.5
  66.7 2.4 %copy-done.18 = bf16[3,6,18,32,256]{4,3,2,1,0:T(8,128)(2,1)} copy-done((bf16[3,6,18,32,256]{4,3,2,1,0:T(8,128)(2,1)}, bf16[3,6,18,32,256]{4,3,2,1,0:T(8,128)(2,1)S(1)}, u32[]{:S(2)}) %copy-start.18) | copy-done | bytes 5308440
  69.1 1.2 copy-done.6
  70.3 2.5 %copy-done.19 = bf16[3,6,18,32,256]{4,3,2,1,0:T(8,128)(2,1)S(1)} copy-done((bf16[3,6,18,32,256]{4,3,2,1,0:T(8,128)(2,1)S(1)}, bf16[3,6,18,32,256]{4,3,2,1,0:T(8,128)(2,1)}, u32[]{:S(2)}) %copy-start.19) | copy-done | bytes 5308440
  72.8 4.7 %shard_map.77.own = f32[28,128,256]{2,1,0:T(8,128)S(1)} custom-call(bf16[3,6,18,32,256]{4,3,2,1,0:T(8,128)(2,1)S(1)} %copy-done.19, bf16[4,16,32,256]{3,2,1,0:T(8,128)(2,1)S(1)} %copy-done.6), custom_call_target="tpu_custom_call" | custom-call | flops 3623878656 | bytes 8388608 | tf_op jit(solution)/shard_map/pallas_call | solution.py:267
  77.5 1.5 shard_map.78
  79.0 5.3 %all-to-all-start = ((bf16[8,448,256]{2,1,0:T(8,128)(2,1)}), bf16[8,448,256]{2,1,0:T(8,128)(2,1)S(1)}, u32[]{:S(2)}, u32[]{:S(2)}) async-start(bf16[8,448,256]{2,1,0:T(8,128)(2,1)} %bitcast.8), calls=%async_computation | async-start | bytes 3670016 | tf_op jit(solution)/shard_map/all_to_all | solution.py:43
  84.4 1.3 collective-permute-start.8
  85.7 0.1 fusion
  85.8 0.8 slice.113
  86.6 4.0 %collective-permute-start.7 = (bf16[4,1,32,256]{3,2,1,0:T(8,128)(2,1)S(1)}, bf16[4,1,32,256]{3,2,1,0:T(8,128)(2,1)S(1)}, u32[]{:S(2)}, u32[]{:S(2)}) collective-permute-start(bf16[4,1,32,256]{3,2,1,0:T(8,128)(2,1)S(1)} %get-tuple-element.59), channel_id=1, source_target_pairs={{0,4},{4,8},{8,12},{12,16},{16,20},{20,24},{24,28},{1,5},{5,9},{9,... | collective-permute-start | bytes 196616 | tf_op jit(solution)/shard_map/ppermute | solution.py:52
  90.6 1.3 collective-permute-start.11
  91.9 0.6 collective-permute-done.7.refs_1_
  92.6 0.1 pad_maximum_fusion.4
  92.7 11.7 %collective-permute-start.9 = (bf16[4,18,1,256]{3,2,1,0:T(2,128)(2,1)S(1)}, bf16[4,18,1,256]{3,2,1,0:T(2,128)(2,1)S(1)}, u32[]{:S(2)}, u32[]{:S(2)}) collective-permute-start(bf16[4,18,1,256]{3,2,1,0:T(2,128)(2,1)S(1)} %pad_maximum_fusion.4), channel_id=1, source_target_pairs={{0,1},{1,2},{2,3},{4,5},{5,6},{6,7},{8,9},{9,10},{10,11},{12,13},{... | collective-permute-start | bytes 110600 | tf_op jit(solution)/shard_map/ppermute | solution.py:52
  104.4 0.1 pad_maximum_fusion.5
  104.5 1.9 %collective-permute-start.10 = (bf16[4,18,1,256]{3,2,1,0:T(2,128)(2,1)S(1)}, bf16[4,18,1,256]{3,2,1,0:T(2,128)(2,1)S(1)}, u32[]{:S(2)}, u32[]{:S(2)}) collective-permute-start(bf16[4,18,1,256]{3,2,1,0:T(2,128)(2,1)S(1)} %pad_maximum_fusion.5), channel_id=1, source_target_pairs={{1,0},{2,1},{3,2},{5,4},{6,5},{7,6},{9,8},{10,9},{11,10},{13,12},{... | collective-permute-start | bytes 110600 | tf_op jit(solution)/shard_map/ppermute | solution.py:52
  106.5 5.2 %collective-permute-done.10.refs_4_ = bf16[4,18,1,256]{3,2,1,0:T(2,128)(2,1)S(1)} collective-permute-done((bf16[4,18,1,256]{3,2,1,0:T(2,128)(2,1)S(1)}, bf16[4,18,1,256]{3,2,1,0:T(2,128)(2,1)S(1)}, u32[]{:S(2)}, u32[]{:S(2)}) %collective-permute-start.10) | collective-permute-done | bytes 36896 | tf_op jit(solution)/shard_map/ppermute | solution.py:52
  111.9 0.1 pad_maximum_fusion.9
  112.0 0.9 shard_map.79
  112.9 4.7 %all-to-all-start.1 = ((bf16[8,56,256]{2,1,0:T(8,128)(2,1)}), bf16[8,56,256]{2,1,0:T(8,128)(2,1)S(1)}, u32[]{:S(2)}, u32[]{:S(2)}) async-start(bf16[8,56,256]{2,1,0:T(8,128)(2,1)} %bitcast.10), calls=%async_computation.1 | async-start | bytes 458752 | tf_op jit(solution)/shard_map/all_to_all | solution.py:43
  117.6 1.3 collective-permute-start.12
  118.9 4.4 %collective-permute-done.12 = bf16[200,256]{1,0:T(8,128)(2,1)S(1)} collective-permute-done((bf16[200,256]{1,0:T(8,128)(2,1)S(1)}, bf16[200,256]{1,0:T(8,128)(2,1)S(1)}, u32[]{:S(2)}, u32[]{:S(2)}) %collective-permute-start.12) | collective-permute-done | bytes 102432 | tf_op jit(solution)/shard_map/ppermute | solution.py:52
  123.4 7.0 %all_to_all.20 = bf16[8,56,256]{2,1,0:T(8,128)(2,1)S(1)} all-to-all(bf16[8,56,256]{2,1,0:T(8,128)(2,1)S(1)} %bitcast.44), channel_id=1, replica_groups={{0,18,96,114,12,30,108,126},{16,2,112,98,28,14,124,110},{32,50,64,82,44..., dimensions={0} | all-to-all | bytes 458752 | tf_op jit(solution)/shard_map/all_to_all | solution.py:43
  130.4 1.3 broadcast_in_dim.8
  131.7 3.6 %all-to-all-start.3 = ((bf16[8,448,256]{2,1,0:T(8,128)(2,1)}), bf16[8,448,256]{2,1,0:T(8,128)(2,1)S(1)}, u32[]{:S(2)}, u32[]{:S(2)}) async-start(bf16[8,448,256]{2,1,0:T(8,128)(2,1)} %broadcast_in_dim.8), calls=%async_computation.3 | async-start | bytes 3670016 | tf_op jit(solution)/shard_map/all_to_all | solution.py:43
  135.3 0.1 copy.39.refs_7_
  135.4 2.0 %copy-done.3 = bf16[27,256,256]{2,1,0:T(8,128)(2,1)S(1)} copy-done((bf16[27,256,256]{2,1,0:T(8,128)(2,1)S(1)}, bf16[27,256,256]{2,1,0:T(8,128)(2,1)}, u32[]{:S(2)}) %copy-start.3) | copy-done | bytes 3538968
  137.4 11.1 %shard_map.81 = bf16[4,16,32,256]{3,2,1,0:T(8,128)(2,1)} custom-call(bf16[4,16,32,256]{3,2,1,0:T(8,128)(2,1)S(1)} %copy-done.7, bf16[4,1,32,256]{3,2,1,0:T(8,128)(2,1)S(1)} %collective-permute-done.7.refs_1_, bf16[4,1,32,256]{3,2,1,0:T(8,128)(2,1)S(1)} %collective-permute-done.8.refs_2_, bf16[4,18,1,256]{3,2,1,0:T(2,128)(2,1)S(1)} %collective-permute-done.9.refs_3_, ...), custom_call_target="tpu_custom_call" | custom-call | flops 7247757312 | bytes 8388608 | tf_op jit(solution)/shard_map/pallas_call | solution.py:284
  148.5 2.5 %all-to-all-done.3 = bf16[8,448,256]{2,1,0:T(8,128)(2,1)S(1)} async-done(((bf16[8,448,256]{2,1,0:T(8,128)(2,1)}), bf16[8,448,256]{2,1,0:T(8,128)(2,1)S(1)}, u32[]{:S(2)}, u32[]{:S(2)}) %all-to-all-start.3) | async-done | bytes 1835040 | tf_op jit(solution)/shard_map/all_to_all | solution.py:43
  151.0 7.6 %collective-permute-start.13 = (bf16[28,128,256]{2,1,0:T(8,128)(2,1)S(1)}, bf16[28,128,256]{2,1,0:T(8,128)(2,1)S(1)}, u32[]{:S(2)}, u32[]{:S(2)}) collective-permute-start(bf16[28,128,256]{2,1,0:T(8,128)(2,1)S(1)} %bitcast.39), channel_id=1, source_target_pairs={{0,1},{1,0},{2,3},{3,2},{4,5},{5,4},{6,7},{7,6},{8,9},{9,8},{10,11... | collective-permute-start | bytes 5505032 | tf_op jit(solution)/shard_map/ppermute | solution.py:294
  158.6 3.4 %collective-permute-done.13.other = bf16[28,128,256]{2,1,0:T(8,128)(2,1)S(1)} collective-permute-done((bf16[28,128,256]{2,1,0:T(8,128)(2,1)S(1)}, bf16[28,128,256]{2,1,0:T(8,128)(2,1)S(1)}, u32[]{:S(2)}, u32[]{:S(2)}) %collective-permute-start.13) | collective-permute-done | bytes 1835040 | tf_op jit(solution)/shard_map/ppermute | solution.py:294
  162.0 4.7 %shard_map.82 = (f32[27,256,256]{2,1,0:T(8,128)}, f32[1,256]{1,0:T(1,128)}) custom-call(bf16[28,128,256]{2,1,0:T(8,128)(2,1)S(1)} %bitcast.40, bf16[28,128,256]{2,1,0:T(8,128)(2,1)S(1)} %collective-permute-done.13.other, bf16[28,128,256]{2,1,0:T(8,128)(2,1)S(1)} %bitcast.41), custom_call_target="tpu_custom_call" | custom-call | tf_op jit(solution)/shard_map/pallas_call | solution.py:297
  (64 shorter events, 0.5 us)
Async XLA Ops:
  1.5 12.3 %collective-permute-start = (bf16[4,1,32,256]{3,2,1,0:T(8,128)(2,1)S(1)}, bf16[4,1,32,256]{3,2,1,0:T(8,128)(2,1)S(1)}, u32[]{:S(2)}, u32[]{:S(2)}) collective-permute-start(bf16[4,1,32,256]{3,2,1,0:T(8,128)(2,1)S(1)} %get-tuple-element.63), channel_id=1, source_target_pairs={{0,4},{4,8},{8,12},{12,16},{16,20},{20,24},{24,28},{1,5},{5,9},{9,... | collective-permute-start | bytes 196616 | tf_op jit(solution)/shard_map/ppermute | solution.py:52
  5.5 8.3 %collective-permute-start.1 = (bf16[4,1,32,256]{3,2,1,0:T(8,128)(2,1)S(1)}, bf16[4,1,32,256]{3,2,1,0:T(8,128)(2,1)S(1)}, u32[]{:S(2)}, u32[]{:S(2)}) collective-permute-start(bf16[4,1,32,256]{3,2,1,0:T(8,128)(2,1)S(1)} %get-tuple-element.62), channel_id=1, source_target_pairs={{4,0},{8,4},{12,8},{16,12},{20,16},{24,20},{28,24},{5,1},{9,5},{13... | collective-permute-start | bytes 196616 | tf_op jit(solution)/shard_map/ppermute | solution.py:52
  8.6 34.0 %collective-permute-start.4 = (bf16[2,16,32,256]{3,2,1,0:T(8,128)(2,1)}, bf16[2,16,32,256]{3,2,1,0:T(8,128)(2,1)}, u32[]{:S(2)}, u32[]{:S(2)}) collective-permute-start(bf16[2,16,32,256]{3,2,1,0:T(8,128)(2,1)} %slice.98), channel_id=1, source_target_pairs={{0,32},{32,64},{64,96},{1,33},{33,65},{65,97},{2,34},{34,66},{66,9... | collective-permute-start | bytes 1572872 | tf_op jit(solution)/shard_map/ppermute | solution.py:52
  13.8 8.9 %copy-start.10 = (bf16[4,1,32,256]{3,2,1,0:T(8,128)(2,1)}, bf16[4,1,32,256]{3,2,1,0:T(8,128)(2,1)S(1)}, u32[]{:S(2)}) copy-start(bf16[4,1,32,256]{3,2,1,0:T(8,128)(2,1)S(1)} %collective-permute-done.1.refs_2_) | copy-start | bytes 196612
  13.8 8.9 %copy-start.8 = (bf16[4,1,32,256]{3,2,1,0:T(8,128)(2,1)}, bf16[4,1,32,256]{3,2,1,0:T(8,128)(2,1)S(1)}, u32[]{:S(2)}) copy-start(bf16[4,1,32,256]{3,2,1,0:T(8,128)(2,1)S(1)} %collective-permute-done.refs_1_) | copy-start | bytes 196612
  14.0 14.0 %collective-permute-start.2 = (bf16[4,18,1,256]{3,2,1,0:T(2,128)(2,1)S(1)}, bf16[4,18,1,256]{3,2,1,0:T(2,128)(2,1)S(1)}, u32[]{:S(2)}, u32[]{:S(2)}) collective-permute-start(bf16[4,18,1,256]{3,2,1,0:T(2,128)(2,1)S(1)} %pad_maximum_fusion.2), channel_id=1, source_target_pairs={{0,1},{1,2},{2,3},{4,5},{5,6},{6,7},{8,9},{9,10},{10,11},{12,13},{... | collective-permute-start | bytes 110600 | tf_op jit(solution)/shard_map/ppermute | solution.py:52
  20.8 7.2 %collective-permute-start.3 = (bf16[4,18,1,256]{3,2,1,0:T(2,128)(2,1)S(1)}, bf16[4,18,1,256]{3,2,1,0:T(2,128)(2,1)S(1)}, u32[]{:S(2)}, u32[]{:S(2)}) collective-permute-start(bf16[4,18,1,256]{3,2,1,0:T(2,128)(2,1)S(1)} %pad_maximum_fusion.3), channel_id=1, source_target_pairs={{1,0},{2,1},{3,2},{5,4},{6,5},{7,6},{9,8},{10,9},{11,10},{13,12},{... | collective-permute-start | bytes 110600 | tf_op jit(solution)/shard_map/ppermute | solution.py:52
  27.9 0.6 copy-start.14
  28.6 0.6 copy-start.12
  29.3 9.6 %collective-permute-start.5 = (bf16[200,256]{1,0:T(8,128)(2,1)S(1)}, bf16[200,256]{1,0:T(8,128)(2,1)}, u32[]{:S(2)}, u32[]{:S(2)}) collective-permute-start(bf16[200,256]{1,0:T(8,128)(2,1)S(1)} %pad_maximum_fusion), channel_id=1, source_target_pairs={{0,32},{32,64},{64,96},{1,33},{33,65},{65,97},{2,34},{34,66},{66,9... | collective-permute-start | bytes 307208 | tf_op jit(solution)/shard_map/ppermute | solution.py:52
  32.4 2.0 %copy-start = (bf16[27,256,256]{2,1,0:T(8,128)(2,1)S(1)}, bf16[27,256,256]{2,1,0:T(8,128)(2,1)}, u32[]{:S(2)}) copy-start(bf16[27,256,256]{2,1,0:T(8,128)(2,1)} %kernel.1) | copy-start | bytes 10616836
  34.4 9.1 %copy-start.1 = (bf16[27,256,256]{2,1,0:T(8,128)(2,1)S(1)}, bf16[27,256,256]{2,1,0:T(8,128)(2,1)}, u32[]{:S(2)}) copy-start(bf16[27,256,256]{2,1,0:T(8,128)(2,1)} %kernel.1) | copy-start | bytes 10616836
  34.4 9.1 %copy-start.17 = (f32[256]{0:T(256)S(1)}, f32[256]{0:T(256)}, u32[]{:S(2)}) copy-start(f32[256]{0:T(256)} %param.6) | copy-start | bytes 3076
  37.2 1.8 %copy-start.2 = (bf16[27,256,256]{2,1,0:T(8,128)(2,1)}, bf16[27,256,256]{2,1,0:T(8,128)(2,1)S(1)}, u32[]{:S(2)}) copy-start(bf16[27,256,256]{2,1,0:T(8,128)(2,1)S(1)} %shard_map.75) | copy-start | bytes 10616836
  43.5 1.2 copy-start.4
  44.7 0.8 copy-start.9
  45.6 0.8 copy-start.11
  46.4 0.9 copy-start.13
  47.3 0.9 copy-start.15
  48.2 1.2 copy-start.16
  65.7 1.0 copy-start.5
  66.7 2.4 %copy-start.18 = (bf16[3,6,18,32,256]{4,3,2,1,0:T(8,128)(2,1)}, bf16[3,6,18,32,256]{4,3,2,1,0:T(8,128)(2,1)S(1)}, u32[]{:S(2)}) copy-start(bf16[3,6,18,32,256]{4,3,2,1,0:T(8,128)(2,1)S(1)} %get-tuple-element.39.taps) | copy-start | bytes 15925252
  69.1 8.4 %collective-permute-start.6 = (bf16[28,128,256]{2,1,0:T(8,128)(2,1)}, bf16[28,128,256]{2,1,0:T(8,128)(2,1)S(1)}, u32[]{:S(2)}, u32[]{:S(2)}) collective-permute-start(bf16[28,128,256]{2,1,0:T(8,128)(2,1)} %get-tuple-element.41), channel_id=1, source_target_pairs={{0,1},{1,0},{2,3},{3,2},{4,5},{5,4},{6,7},{7,6},{8,9},{9,8},{10,11... | collective-permute-start | bytes 5505032 | tf_op jit(solution)/shard_map/ppermute | solution.py:266
  69.1 1.2 copy-start.6
  70.3 2.5 %copy-start.19 = (bf16[3,6,18,32,256]{4,3,2,1,0:T(8,128)(2,1)S(1)}, bf16[3,6,18,32,256]{4,3,2,1,0:T(8,128)(2,1)}, u32[]{:S(2)}) copy-start(bf16[3,6,18,32,256]{4,3,2,1,0:T(8,128)(2,1)} %copy-done.18) | copy-start | bytes 15925252
  79.0 5.3 %copy-start.7 = (bf16[4,16,32,256]{3,2,1,0:T(8,128)(2,1)S(1)}, bf16[4,16,32,256]{3,2,1,0:T(8,128)(2,1)}, u32[]{:S(2)}) copy-start(bf16[4,16,32,256]{3,2,1,0:T(8,128)(2,1)} %copy-done.5) | copy-start | bytes 3145732
  79.0 33.0 %all-to-all-start = ((bf16[8,448,256]{2,1,0:T(8,128)(2,1)}), bf16[8,448,256]{2,1,0:T(8,128)(2,1)S(1)}, u32[]{:S(2)}, u32[]{:S(2)}) async-start(bf16[8,448,256]{2,1,0:T(8,128)(2,1)} %bitcast.8), calls=%async_computation | async-start | bytes 3670016 | tf_op jit(solution)/shard_map/all_to_all | solution.py:43
  84.4 7.5 %collective-permute-start.8 = (bf16[4,1,32,256]{3,2,1,0:T(8,128)(2,1)S(1)}, bf16[4,1,32,256]{3,2,1,0:T(8,128)(2,1)S(1)}, u32[]{:S(2)}, u32[]{:S(2)}) collective-permute-start(bf16[4,1,32,256]{3,2,1,0:T(8,128)(2,1)S(1)} %get-tuple-element.58), channel_id=1, source_target_pairs={{4,0},{8,4},{12,8},{16,12},{20,16},{24,20},{28,24},{5,1},{9,5},{13... | collective-permute-start | bytes 196616 | tf_op jit(solution)/shard_map/ppermute | solution.py:52
  86.6 5.9 %collective-permute-start.7 = (bf16[4,1,32,256]{3,2,1,0:T(8,128)(2,1)S(1)}, bf16[4,1,32,256]{3,2,1,0:T(8,128)(2,1)S(1)}, u32[]{:S(2)}, u32[]{:S(2)}) collective-permute-start(bf16[4,1,32,256]{3,2,1,0:T(8,128)(2,1)S(1)} %get-tuple-element.59), channel_id=1, source_target_pairs={{0,4},{4,8},{8,12},{12,16},{16,20},{20,24},{24,28},{1,5},{5,9},{9,... | collective-permute-start | bytes 196616 | tf_op jit(solution)/shard_map/ppermute | solution.py:52
  90.6 32.8 %collective-permute-start.11 = (bf16[2,16,32,256]{3,2,1,0:T(8,128)(2,1)}, bf16[2,16,32,256]{3,2,1,0:T(8,128)(2,1)}, u32[]{:S(2)}, u32[]{:S(2)}) collective-permute-start(bf16[2,16,32,256]{3,2,1,0:T(8,128)(2,1)} %slice.113), channel_id=1, source_target_pairs={{32,0},{64,32},{96,64},{33,1},{65,33},{97,65},{34,2},{66,34},{98,6... | collective-permute-start | bytes 1572872 | tf_op jit(solution)/shard_map/ppermute | solution.py:52
  92.7 19.1 %collective-permute-start.9 = (bf16[4,18,1,256]{3,2,1,0:T(2,128)(2,1)S(1)}, bf16[4,18,1,256]{3,2,1,0:T(2,128)(2,1)S(1)}, u32[]{:S(2)}, u32[]{:S(2)}) collective-permute-start(bf16[4,18,1,256]{3,2,1,0:T(2,128)(2,1)S(1)} %pad_maximum_fusion.4), channel_id=1, source_target_pairs={{0,1},{1,2},{2,3},{4,5},{5,6},{6,7},{8,9},{9,10},{10,11},{12,13},{... | collective-permute-start | bytes 110600 | tf_op jit(solution)/shard_map/ppermute | solution.py:52
  104.5 7.2 %collective-permute-start.10 = (bf16[4,18,1,256]{3,2,1,0:T(2,128)(2,1)S(1)}, bf16[4,18,1,256]{3,2,1,0:T(2,128)(2,1)S(1)}, u32[]{:S(2)}, u32[]{:S(2)}) collective-permute-start(bf16[4,18,1,256]{3,2,1,0:T(2,128)(2,1)S(1)} %pad_maximum_fusion.5), channel_id=1, source_target_pairs={{1,0},{2,1},{3,2},{5,4},{6,5},{7,6},{9,8},{10,9},{11,10},{13,12},{... | collective-permute-start | bytes 110600 | tf_op jit(solution)/shard_map/ppermute | solution.py:52
  112.9 10.4 %all-to-all-start.1 = ((bf16[8,56,256]{2,1,0:T(8,128)(2,1)}), bf16[8,56,256]{2,1,0:T(8,128)(2,1)S(1)}, u32[]{:S(2)}, u32[]{:S(2)}) async-start(bf16[8,56,256]{2,1,0:T(8,128)(2,1)} %bitcast.10), calls=%async_computation.1 | async-start | bytes 458752 | tf_op jit(solution)/shard_map/all_to_all | solution.py:43
  117.6 5.7 %collective-permute-start.12 = (bf16[200,256]{1,0:T(8,128)(2,1)S(1)}, bf16[200,256]{1,0:T(8,128)(2,1)S(1)}, u32[]{:S(2)}, u32[]{:S(2)}) collective-permute-start(bf16[200,256]{1,0:T(8,128)(2,1)S(1)} %pad_maximum_fusion.1), channel_id=1, source_target_pairs={{32,0},{64,32},{96,64},{33,1},{65,33},{97,65},{34,2},{66,34},{98,6... | collective-permute-start | bytes 307208 | tf_op jit(solution)/shard_map/ppermute | solution.py:52
  131.7 19.3 %all-to-all-start.3 = ((bf16[8,448,256]{2,1,0:T(8,128)(2,1)}), bf16[8,448,256]{2,1,0:T(8,128)(2,1)S(1)}, u32[]{:S(2)}, u32[]{:S(2)}) async-start(bf16[8,448,256]{2,1,0:T(8,128)(2,1)} %broadcast_in_dim.8), calls=%async_computation.3 | async-start | bytes 3670016 | tf_op jit(solution)/shard_map/all_to_all | solution.py:43
  135.4 2.0 %copy-start.3 = (bf16[27,256,256]{2,1,0:T(8,128)(2,1)S(1)}, bf16[27,256,256]{2,1,0:T(8,128)(2,1)}, u32[]{:S(2)}) copy-start(bf16[27,256,256]{2,1,0:T(8,128)(2,1)} %copy-done.2) | copy-start | bytes 10616836
  151.0 11.0 %collective-permute-start.13 = (bf16[28,128,256]{2,1,0:T(8,128)(2,1)S(1)}, bf16[28,128,256]{2,1,0:T(8,128)(2,1)S(1)}, u32[]{:S(2)}, u32[]{:S(2)}) collective-permute-start(bf16[28,128,256]{2,1,0:T(8,128)(2,1)S(1)} %bitcast.39), channel_id=1, source_target_pairs={{0,1},{1,0},{2,3},{3,2},{4,5},{5,4},{6,7},{7,6},{8,9},{9,8},{10,11... | collective-permute-start | bytes 5505032 | tf_op jit(solution)/shard_map/ppermute | solution.py:294

commit v2 on v1

v2 whole, which is shorter than its diff:
```python
import functools
import itertools

import jax
import jax.numpy as jnp
import numpy as np
from jax import lax
from jax.experimental import pallas as pl
from jax.experimental.pallas import tpu as pltpu
from jax.sharding import Mesh
from jax.sharding import PartitionSpec as P

AXES = ("ta", "hz", "hx", "wz", "wc")
HA = ("hz", "hx")
WA = ("wz", "wc")
BF = jnp.bfloat16
F32 = jnp.float32
VMEM = pl.BlockSpec(memory_space=pltpu.VMEM)
ANY = pl.BlockSpec(memory_space=pl.ANY)
MIB = 1 << 20


def number(x, y, z, core):
    return (((y * 2 + z % 2) * 4 + x) * 2 + z // 2) * 2 + core


def cubes(pairs):
    out = []
    for core in (0, 1):
        for px, py, pz in itertools.product(pairs, repeat=3):
            cube = []
            for a, b, c in itertools.product(range(2), repeat=3):
                place = [(p + core) % 4 for p in (px[a], py[b], pz[c])]
                cube.append(number(*place, core))
            out.append(cube)
    return out


NEAR = cubes(((0, 1), (3, 2)))
FAR = cubes(((0, 3), (1, 2)))


def exchange(pieces, groups):
    return lax.all_to_all(pieces, AXES, 0, 0, axis_index_groups=groups)


def shift(block, axis, distance):
    names = axis if isinstance(axis, tuple) else (axis,)
    count = 1
    for name in names:
        count *= lax.axis_size(name)
    route = [(i, i + distance) for i in range(count) if 0 <= i + distance < count]
    return lax.ppermute(block, axis, route)


def transfers(sems, *pairs):
    copies = [pltpu.make_async_copy(s, d, sems.at[i]) for i, (s, d) in enumerate(pairs)]
    for copy in copies:
        copy.start()
    return copies


def one_hot(shape, hit):
    row = lax.broadcasted_iota(jnp.int32, shape, 0)
    lane = lax.broadcasted_iota(jnp.int32, shape, 1)
    return jnp.where(hit(row, lane), 1.0, 0.0).astype(BF)


def edge_rows_kernel(*refs):
    sems = refs[-1]
    field, outs = refs[0], refs[1:-1]
    pairs = [
        (field.at[:, pl.ds(0, 1)], outs[0]),
        (field.at[:, pl.ds(15, 1)], outs[1]),
        (field.at[pl.ds(2, 2)], outs[2]),
    ]
    for copy in transfers(sems, *pairs):
        copy.wait()


def more_rows_kernel(field, remote, top, bottom, sems):
    pairs = []
    for out, row in ((top, 0), (bottom, 15)):
        pairs.append((field.at[:, pl.ds(row, 1)], out.at[pl.ds(0, 4)]))
        pairs.append((remote.at[:, pl.ds(row, 1)], out.at[pl.ds(4, 2)]))
    for copy in transfers(sems, *pairs):
        copy.wait()


def columns_kernel(*refs):
    count = (len(refs) - 3) // 2
    sources, (first, last) = refs[:count], refs[count : count + 2]
    held, sems = refs[count + 2 : -1], refs[-1]
    copies = transfers(sems, *zip(sources, held))
    pick = one_hot((64, 576), lambda i, cell: cell == 32 * (i % 32) + 31 * (i // 32))
    for copy in copies:
        copy.wait()
    low, high = held[-2:]
    start = 0
    for field in held[:-2]:

        @pl.loop(0, field.shape[0])
        def _(t, field=field, start=start):
            block = jnp.concatenate([low[start + t], field[t], high[start + t]], axis=0)
            found = jnp.dot(pick, block.reshape(576, 256), preferred_element_type=F32)
            first[start + t] = found[0:32].astype(BF)
            last[start + t] = found[32:64].astype(BF)

        start += field.shape[0]


def place(taps, groups):
    west_at = one_hot((576, 32), lambda cell, r: cell == 32 * r)
    east_at = one_hot((576, 32), lambda cell, r: cell == 32 * r + 31)

    def put(at, middle, top, bottom, west, east):
        block = jnp.concatenate([top, middle, bottom], axis=0)
        taps[1, at] = block
        block = block.astype(F32)
        column = lax.broadcasted_iota(jnp.int32, block.shape, 1)
        side = jnp.dot(west_at, west, preferred_element_type=F32).reshape(18, 32, 256)
        taps[0, at] = jnp.where(column == 0, side, pltpu.roll(block, 1, 1)).astype(BF)
        side = jnp.dot(east_at, east, preferred_element_type=F32).reshape(18, 32, 256)
        taps[2, at] = jnp.where(column == 31, side, pltpu.roll(block, 31, 1)).astype(BF)

    for first, count, parts in groups:

        @pl.loop(0, count)
        def _(t, first=first, parts=parts):
            put(first + t, *parts(t))


def window(taps, c, frame, b):
    piece = taps[c, frame, pl.ds(b, 16)]
    return piece.reshape(-1, piece.shape[-1])


def weight_terms(taps, slope, half, emit, a):
    lanes = pl.ds(pl.multiple_of(half * 128, 128), 128)
    pieces = [
        taps[c, pl.ds(a, 4), b : b + 16, :, lanes].reshape(2048, 128)
        for b in range(3)
        for c in range(3)
    ]
    value = lax.dot_general(
        jnp.concatenate(pieces, axis=1),
        slope[...].reshape(2048, 256),
        (((0,), (0,)), ((), ())),
        preferred_element_type=F32,
    )
    emit(pl.ds(9 * a, 9), value.reshape(9, 128, 256))


def bias_rows(value):
    high = value.astype(BF).astype(F32)
    return jnp.concatenate([high, value - high, jnp.zeros((112, 256), F32)], axis=0)


def bias_term(slope):
    total = jnp.sum(slope[...].reshape(2048, 256).astype(F32), axis=0, keepdims=True)
    return jnp.broadcast_to(total, (8, 256))


def forward_kernel(*refs):
    sources, bias, outs, held = refs[:9], refs[9], refs[10:15], refs[15:24]
    act, slopes, taps, send, sems = refs[24:]
    copies = transfers(sems, *zip(sources, held))
    field, low, high, left, right, remote, edges, kernel, cotangent = held
    activation, dpre, front, taps_out, send_out = outs
    for copy in copies[:7]:
        copy.wait()
    own = (2, 4, lambda t: (field[t], low[t], high[t], left[t], right[t]))
    far = (
        0,
        2,
        lambda t: (remote[t], edges[t, 0:1], edges[t, 1:2], edges[t, 2], edges[t, 3]),
    )
    place(taps, (own, far))
    taps_copy = pltpu.make_async_copy(taps, taps_out, sems.at[9])
    taps_copy.start()
    for copy in copies[7:]:
        copy.wait()

    @pl.loop(0, 4)
    def _(t):
        total = jnp.broadcast_to(bias[...], (512, 256))
        for a in range(3):
            pieces = [window(taps, c, t + a, b) for b in range(3) for c in range(3)]
            total = total + jnp.dot(
                jnp.concatenate(pieces, axis=1), kernel[a], preferred_element_type=F32
            )
        sig = jax.nn.sigmoid(total)
        act[t] = (total * sig).astype(BF).reshape(16, 32, 256)
        cot = cotangent[t].reshape(512, 256).astype(F32)
        slope = cot * sig * (1.0 + total * (1.0 - sig))
        slopes[t] = slope.astype(BF).reshape(16, 32, 256)

    done = [
        pltpu.make_async_copy(act, activation, sems.at[10]),
        pltpu.make_async_copy(slopes, dpre, sems.at[11]),
        pltpu.make_async_copy(slopes.at[pl.ds(0, 2)], front, sems.at[12]),
    ]
    for copy in done:
        copy.start()

    def emit(at, value):
        send[at] = value.astype(BF)

    @pl.loop(0, 3)
    def _(a):
        weight_terms(taps, slopes, 1 - lax.axis_index("wc"), emit, a)

    send[27] = bias_rows(bias_term(slopes)).astype(BF)
    last = pltpu.make_async_copy(send, send_out, sems.at[13])
    last.start()
    for copy in (taps_copy, *done, last):
        copy.wait()


def weight_kernel(taps_in, dpre_in, own_out, taps, slopes, own, sems):
    pairs = [(dpre_in, slopes), (taps_in.at[:, pl.ds(0, 4)], taps.at[:, pl.ds(0, 4)])]
    pairs += [(taps_in.at[:, pl.ds(f, 1)], taps.at[:, pl.ds(f, 1)]) for f in (4, 5)]
    copies = transfers(sems, *pairs)

    def emit(at, value):
        own[at] = value

    outs = []
    copies[0].wait()
    for a in range(3):
        copies[1 + a].wait()
        weight_terms(taps, slopes, lax.axis_index("wc"), emit, a)
        part = pl.ds(9 * a, 9)
        outs.append(pltpu.make_async_copy(own.at[part], own_out.at[part], sems.at[4 + a]))
        outs[-1].start()
    own[27, 0:8] = bias_term(slopes)
    outs.append(pltpu.make_async_copy(own.at[27, 0:8], own_out.at[27, 0:8], sems.at[7]))
    outs[-1].start()
    for copy in outs:
        copy.wait()


def join_kernel(own_in, received_in, out, own, received, sems):
    copies = transfers(sems, (own_in, own), (received_in, received))
    for copy in copies:
        copy.wait()
    out[0:27] = (own[0:27] + received[0:27].astype(F32)).astype(BF)
    value = own[27, 0:8] + received[27, 0:8].astype(F32) + received[27, 8:16].astype(F32)
    out[27] = bias_rows(value).astype(BF)


def sum_kernel(pieces_in, flag, out, pieces, total, sems):
    copies = transfers(sems, *[(pieces_in.at[i], pieces.at[i]) for i in range(8)])
    for copy in copies:
        copy.wait()

    @pl.loop(0, 7)
    def _(part):
        at = pl.ds(pl.multiple_of(part * 64, 64), 64)
        value = pieces[0, at].astype(F32)
        for i in range(1, 8):
            value = value + pieces[i, at].astype(F32)
        total[at] = value.astype(BF)

    @pl.when(flag[0] == 1)
    def _():
        value = sum(pieces[i, 320:336].astype(F32) for i in range(8))
        total[320:336] = bias_rows(value[0:8] + value[8:16])[0:16].astype(BF)

    copies = transfers(sems, *[(total, out.at[i]) for i in range(8)])
    for copy in copies:
        copy.wait()


def backward_kernel(*refs):
    sources, latent_grad, held = refs[:7], refs[7], refs[8:15]
    grad, taps, sems = refs[15:]
    copies = transfers(sems, *zip(sources, held))
    field, remote, low, high, left, right, kernel = held
    for copy in copies:
        copy.wait()
    own = (0, 4, lambda t: (field[t], low[t], high[t], left[t], right[t]))
    far = (4, 2, lambda t: (remote[t], low[4 + t], high[4 + t], left[4 + t], right[4 + t]))
    place(taps, (own, far))

    @pl.loop(0, 4)
    def _(t):
        total = jnp.zeros((512, 256), F32)
        for a, b, c in itertools.product(range(3), repeat=3):
            total = total + lax.dot_general(
                window(taps, 2 - c, t + 2 - a, 2 - b),
                kernel[9 * a + 3 * b + c],
                (((1,), (1,)), ((), ())),
                preferred_element_type=F32,
            )
        grad[t] = total.astype(BF).reshape(16, 32, 256)

    copy = pltpu.make_async_copy(grad, latent_grad, sems.at[7])
    copy.start()
    copy.wait()


def finish_kernel(scale, turn, half_in, *refs):
    kernel_grad, half, wide, sems = refs[-4 - (turn == 0)], *refs[-3:]
    core = lax.axis_index("wc")
    rows = pl.ds(pl.multiple_of((core if turn == 0 else 1 - core) * 128, 128), 128)
    copies = []
    load = pltpu.make_async_copy(half_in, half, sems.at[9])
    load.start()
    load.wait()
    for k in range(9):
        at = pl.ds(3 * k, 3)
        wide[at] = half[at].astype(F32) * scale
        copies.append(pltpu.make_async_copy(wide.at[at], kernel_grad.at[at, rows], sems.at[k]))
        copies[-1].start()
    if turn == 0:
        bias_grad = refs[1]
        bias_grad[...] = (half[27, 0:1].astype(F32) + half[27, 8:9].astype(F32)) * scale
    for copy in copies:
        copy.wait()


def call(body, outs, n_in, scratch, sems, vmem=24, flops=0, specs=None, out_specs=None, **kwargs):
    return pl.pallas_call(
        body,
        out_shape=outs,
        in_specs=specs or [ANY] * n_in,
        out_specs=out_specs or jax.tree.map(lambda _: ANY, outs),
        scratch_shapes=[*scratch, pltpu.SemaphoreType.DMA((sems,))],
        compiler_params=pltpu.CompilerParams(vmem_limit_bytes=vmem * MIB),
        cost_estimate=pl.CostEstimate(flops=flops, bytes_accessed=4 * MIB, transcendentals=0),
        **kwargs,
    )


def shape(*dims, dtype=BF):
    return jax.ShapeDtypeStruct(dims, dtype)


def buffer(*dims, dtype=BF):
    return pltpu.VMEM(dims, dtype)


def columns_of(low, high, *fields):
    frames = low.shape[0]
    sources = (*fields, low, high)
    return call(
        columns_kernel,
        (shape(frames, 32, 256),) * 2,
        len(sources),
        [buffer(*x.shape) for x in sources],
        len(sources),
        vmem=8,
        out_specs=(VMEM, VMEM),
    )(*sources)


def sum_pieces(pieces, special):
    return call(
        sum_kernel,
        shape(8, 448, 256),
        2,
        [buffer(8, 448, 256), buffer(448, 256)],
        8,
        vmem=8,
        specs=(ANY, pl.BlockSpec(memory_space=pltpu.SMEM)),
    )(pieces, special.astype(jnp.int32).reshape(1))


def finish(scale, turn, half, *base):
    grad = shape(27, 256, 256, dtype=F32)
    outs = (grad, shape(1, 256, dtype=F32)) if turn == 0 else grad
    return call(
        functools.partial(finish_kernel, scale, turn),
        outs,
        1 + turn,
        [buffer(28, 128, 256), buffer(27, 128, 256, dtype=F32)],
        10,
        vmem=8,
        out_specs=(ANY, VMEM) if turn == 0 else ANY,
        input_output_aliases={1: 0} if turn else {},
    )(half, *base)


def shards(latent, kernel, bias, cotangent):
    frames, rows, columns, width = latent.shape
    cells = frames * rows * columns
    for name in AXES:
        cells *= lax.axis_size(name)
    scale = float(1.0 / np.sqrt(np.float32(cells)))
    conv_flops = 2 * 2048 * 27 * 256 * 256
    block, pair, half = (4, 16, 32, 256), (2, 16, 32, 256), (28, 128, 256)
    edge = (4, 1, 32, 256)
    bordered = (3, 6, 18, 32, 256)

    top, bottom, back = call(
        edge_rows_kernel, (shape(*edge), shape(*edge), shape(*pair)), 1, [], 3, vmem=4
    )(latent)
    low = shift(bottom, HA, 1)
    high = shift(top, HA, -1)
    remote = shift(back, "ta", 1)
    first, last = columns_of(low, high, latent)
    left = shift(last, WA, 1)
    right = shift(first, WA, -1)
    edges = jnp.concatenate([low[2:], high[2:], left[2:, None], right[2:, None]], axis=1)
    edges = shift(edges, "ta", 1)

    sources = (latent, low, high, left, right, remote, edges, kernel.reshape(3, 2304, 256))
    sources = (*sources, cotangent)
    activation, dpre, front, taps, send = call(
        forward_kernel,
        (shape(*block), shape(*block), shape(*pair), shape(*bordered), shape(*half)),
        10,
        [buffer(*x.shape) for x in sources]
        + [buffer(*block), buffer(*block), buffer(*bordered), buffer(*half)],
        14,
        vmem=32,
        flops=conv_flops * 3 // 2,
        specs=[ANY] * 9 + [VMEM],
    )(*sources, bias.reshape(1, 256))
    received = lax.ppermute(send, "wc", [(0, 1), (1, 0)])
    remote = shift(front, "ta", -1)
    own = call(
        weight_kernel,
        shape(*half, dtype=F32),
        2,
        [buffer(*bordered), buffer(*block), buffer(*half, dtype=F32)],
        8,
        vmem=24,
        flops=conv_flops // 2,
    )(taps, dpre)
    terms = call(
        join_kernel,
        shape(*half),
        2,
        [buffer(*half, dtype=F32), buffer(*half)],
        2,
        vmem=16,
        out_specs=VMEM,
    )(own, received)

    core = lax.axis_index("wc")
    z = 2 * lax.axis_index("wz") + lax.axis_index("hz")
    spot = [(p - core) % 4 for p in (lax.axis_index("hx"), lax.axis_index("ta"), z)]
    near = sum(w * ((p == 1) | (p == 2)) for w, p in zip((4, 2, 1), spot))
    pieces = exchange(terms.reshape(8, 448, 256), NEAR)
    top, bottom = call(
        more_rows_kernel, (shape(6, 1, 32, 256),) * 2, 2, [], 4, vmem=4
    )(dpre, remote)
    low = shift(bottom, HA, 1)
    high = shift(top, HA, -1)
    first, last = columns_of(low, high, dpre, remote)
    left = shift(last, WA, 1)
    right = shift(first, WA, -1)
    pieces, left, right = lax.optimization_barrier((pieces, left, right))
    pieces = exchange(sum_pieces(pieces, near == 7), FAR)
    sources = (dpre, remote, low, high, left, right, kernel)
    latent_grad = call(
        backward_kernel,
        shape(*block),
        7,
        [buffer(*x.shape) for x in sources] + [buffer(*block), buffer(*bordered)],
        8,
        vmem=32,
        flops=conv_flops,
    )(*sources)
    pieces, latent_grad = lax.optimization_barrier((pieces, latent_grad))
    mine = exchange(sum_pieces(pieces, near == 7), NEAR).reshape(half)
    other = lax.ppermute(mine, "wc", [(0, 1), (1, 0)])
    kernel_grad, bias_grad = finish(scale, 0, mine)
    kernel_grad = finish(scale, 1, other, kernel_grad)
    return (activation, latent_grad, kernel_grad, bias_grad.reshape(256))


def solution(mesh):
    split = Mesh(np.asarray(mesh.devices).reshape(4, 2, 4, 2, 2), AXES)
    placed = P("ta", HA, WA, None)
    return jax.shard_map(
        shards,
        mesh=split,
        in_specs=(placed, P(), P(), placed),
        out_specs=(placed, placed, P(), P()),
        check_vma=False,
    )
```

time: 168 us -> 180 us (1.071)
  local copies, waits for them, and re-layouts: 31 us -> 8 us
  waiting for transfers between devices: 21.3 us -> 39.9 us
  blocking collectives: 7 us -> 22.5 us
  Pallas kernels: 42.1 us -> 57.3 us
  starting transfers between devices: 63.4 us -> 50.5 us
    ppermute x12 -> x11, waiting for transfers between devices: 15.4 us -> 38.7 us  [shift(): return lax.ppermute(block, axis, route)]
    all_to_all x1, blocking collectives: 7 us -> 22.5 us  [exchange(): return lax.all_to_all(pieces, AXES, 0, 0, axis_index_groups=groups)]
    pallas_call x8 -> x12, Pallas kernels: 42.1 us -> 57.3 us  [the longest x1 16.7 us: shards(): call(forward_kernel, (shape(*block), shape(*block), shape(*pair), shape(*...]
    unnamed x40 -> x20, local copies, waits for them, and re-layouts: 19.9 us -> 7.98 us
    ppermute x1, starting transfers between devices: 7.56 us -> 0.01 us  [shards(): other = lax.ppermute(mine, 'wc', [(0, 1), (1, 0)])]
    slice x22 -> x2, local copies, waits for them, and re-layouts: 7.37 us -> 0.01 us  [the longest x1 0.01 us: shards(): high[2:]]
    ppermute x12 -> x11, starting transfers between devices: 42.3 us -> 37.4 us  [shift(): return lax.ppermute(block, axis, route)]
    all_to_all x3 -> x2, waiting for transfers between devices: 2.49 us -> 0.01 us  [exchange(): return lax.all_to_all(pieces, AXES, 0, 0, axis_index_groups=groups)]
  transfers between devices with their start and end apart: 17 -> 15, of which waited for: 6 -> 8; matrix products, arithmetic and copies ran while one was open for 5% -> 0% of each run, Pallas kernels for 12% -> 14%
where the time goes in v2:
time: 180 us; the launch traced here: 179 us
  Pallas kernels  57.3 us (32%)
  starting transfers between devices  50.5 us (28%)
  waiting for transfers between devices  39.9 us (22%)
  blocking collectives  22.5 us (12%)
  local copies, waits for them, and re-layouts  8 us (4%)
    ppermute x11, waiting for transfers between devices, shift(): return lax.ppermute(block, axis, route)  38.7 us
    ppermute x11, starting transfers between devices, shift(): return lax.ppermute(block, axis, route)  37.4 us
    all_to_all x1, blocking collectives, exchange(): return lax.all_to_all(pieces, AXES, 0, 0, axis_index_groups=groups)  22.5 us
    pallas_call x1, Pallas kernels, shards(): call(forward_kernel, (shape(*block), shape(*block), shape(*pair), shape(*...  16.7 us
    all_to_all x2, starting transfers between devices, exchange(): return lax.all_to_all(pieces, AXES, 0, 0, axis_index_groups=groups)  13 us
    pallas_call x1, Pallas kernels, shards(): call(backward_kernel, shape(*block), 7, [buffer(*x.shape) for x in source...  12.3 us
    pallas_call x2, Pallas kernels, sum_pieces(): call(sum_kernel, shape(8, 448, 256), 2, [buffer(8, 448, 256), buffer(448,...  10.2 us
    pallas_call x1, Pallas kernels, shards(): call(weight_kernel, shape(*half, dtype=F32), 2, [buffer(*bordered), buffe...  8.29 us
  transfers between devices with their start and end apart: 15, of which 8 were waited for; matrix products, arithmetic and copies ran while one was open for 0% of the time, Pallas kernels for 14%

profile of v2, /device:TPU:1, one launch (start us, length us, event | category | flops | bytes accessed | tf_op | source)
XLA Modules:
  0.0 179.4 jit_solution(17011798657537188040)
XLA Ops:
  0.6 0.0 copy-start.1
  0.6 1.2 copy-done.1
  1.9 0.0 copy-start.2
  1.9 0.0 copy-start.7
  1.9 0.0 copy-start.9
  1.9 0.1 shard_map.75
  2.0 4.1 %collective-permute-start = (bf16[4,1,32,256]{3,2,1,0:T(8,128)(2,1)S(1)}, bf16[4,1,32,256]{3,2,1,0:T(8,128)(2,1)S(1)}, u32[]{:S(2)}, u32[]{:S(2)}) collective-permute-start(bf16[4,1,32,256]{3,2,1,0:T(8,128)(2,1)S(1)} %get-tuple-element.25), channel_id=1, source_target_pairs={{0,4},{4,8},{8,12},{12,16},{16,20},{20,24},{24,28},{1,5},{5,9},{9,... | collective-permute-start | bytes 196616 | tf_op jit(solution)/shard_map/ppermute | solution.py:53
  6.1 1.3 collective-permute-start.1
  7.4 0.0 collective-permute-done.refs_1_
  7.4 3.7 %collective-permute-done.1.refs_2_ = bf16[4,1,32,256]{3,2,1,0:T(8,128)(2,1)S(1)} collective-permute-done((bf16[4,1,32,256]{3,2,1,0:T(8,128)(2,1)S(1)}, bf16[4,1,32,256]{3,2,1,0:T(8,128)(2,1)S(1)}, u32[]{:S(2)}, u32[]{:S(2)}) %collective-permute-start.1) | collective-permute-done | bytes 65568 | tf_op jit(solution)/shard_map/ppermute | solution.py:53
  11.1 1.0 shard_map.76
  12.1 7.5 %collective-permute-start.2 = (bf16[4,32,256]{2,1,0:T(8,128)(2,1)S(1)}, bf16[4,32,256]{2,1,0:T(8,128)(2,1)S(1)}, u32[]{:S(2)}, u32[]{:S(2)}) collective-permute-start(bf16[4,32,256]{2,1,0:T(8,128)(2,1)S(1)} %get-tuple-element.27), channel_id=1, source_target_pairs={{0,1},{1,2},{2,3},{4,5},{5,6},{6,7},{8,9},{9,10},{10,11},{12,13},{... | collective-permute-start | bytes 196616 | tf_op jit(solution)/shard_map/ppermute | solution.py:53
  19.6 3.2 %collective-permute-start.4 = (bf16[2,16,32,256]{3,2,1,0:T(8,128)(2,1)S(1)}, bf16[2,16,32,256]{3,2,1,0:T(8,128)(2,1)S(1)}, u32[]{:S(2)}, u32[]{:S(2)}) collective-permute-start(bf16[2,16,32,256]{3,2,1,0:T(8,128)(2,1)S(1)} %get-tuple-element.29), channel_id=1, source_target_pairs={{0,32},{32,64},{64,96},{1,33},{33,65},{65,97},{2,34},{34,66},{66,9... | collective-permute-start | bytes 1572872 | tf_op jit(solution)/shard_map/ppermute | solution.py:53
  22.8 1.9 %collective-permute-start.3 = (bf16[4,32,256]{2,1,0:T(8,128)(2,1)S(1)}, bf16[4,32,256]{2,1,0:T(8,128)(2,1)S(1)}, u32[]{:S(2)}, u32[]{:S(2)}) collective-permute-start(bf16[4,32,256]{2,1,0:T(8,128)(2,1)S(1)} %get-tuple-element.28), channel_id=1, source_target_pairs={{1,0},{2,1},{3,2},{5,4},{6,5},{7,6},{9,8},{10,9},{11,10},{13,12},{... | collective-permute-start | bytes 196616 | tf_op jit(solution)/shard_map/ppermute | solution.py:53
  24.8 0.0 collective-permute-done.2.refs_3_
  24.8 5.1 %collective-permute-done.3.refs_4_ = bf16[4,32,256]{2,1,0:T(8,128)(2,1)S(1)} collective-permute-done((bf16[4,32,256]{2,1,0:T(8,128)(2,1)S(1)}, bf16[4,32,256]{2,1,0:T(8,128)(2,1)S(1)}, u32[]{:S(2)}, u32[]{:S(2)}) %collective-permute-start.3) | collective-permute-done | bytes 65568 | tf_op jit(solution)/shard_map/ppermute | solution.py:53
  30.0 3.2 %collective-permute-start.5 = (bf16[2,4,32,256]{3,2,1,0:T(8,128)(2,1)S(1)}, bf16[2,4,32,256]{3,2,1,0:T(8,128)(2,1)S(1)}, u32[]{:S(2)}, u32[]{:S(2)}) collective-permute-start(bf16[2,4,32,256]{3,2,1,0:T(8,128)(2,1)S(1)} %pad_maximum_fusion), channel_id=1, source_target_pairs={{0,32},{32,64},{64,96},{1,33},{33,65},{65,97},{2,34},{34,66},{66,9... | collective-permute-start | bytes 393224 | tf_op jit(solution)/shard_map/ppermute | solution.py:53
  33.2 1.9 %collective-permute-done.5.refs_6_ = bf16[2,4,32,256]{3,2,1,0:T(8,128)(2,1)S(1)} collective-permute-done((bf16[2,4,32,256]{3,2,1,0:T(8,128)(2,1)S(1)}, bf16[2,4,32,256]{3,2,1,0:T(8,128)(2,1)S(1)}, u32[]{:S(2)}, u32[]{:S(2)}) %collective-permute-start.5) | collective-permute-done | bytes 131104 | tf_op jit(solution)/shard_map/ppermute | solution.py:53
  35.1 0.0 collective-permute-done.4.refs_5_
  35.1 0.0 copy-done.2
  35.1 0.0 copy-done.7
  35.1 0.0 copy-done.9
  35.1 0.0 copy-start.5
  35.1 2.0 %copy-done.5 = bf16[27,256,256]{2,1,0:T(8,128)(2,1)S(1)} copy-done((bf16[27,256,256]{2,1,0:T(8,128)(2,1)S(1)}, bf16[27,256,256]{2,1,0:T(8,128)(2,1)}, u32[]{:S(2)}) %copy-start.5) | copy-done | bytes 3538968
  37.1 16.7 %shard_map.77 = (bf16[4,16,32,256]{3,2,1,0:T(8,128)(2,1)}, bf16[4,16,32,256]{3,2,1,0:T(8,128)(2,1)S(1)}, bf16[2,16,32,256]{3,2,1,0:T(8,128)(2,1)S(1)}, bf16[3,6,...) custom-call(bf16[4,16,32,256]{3,2,1,0:T(8,128)(2,1)S(1)} %copy-done.2, ...), custom_call_target="tpu_custom_call" | custom-call | flops 10871635968 | bytes 4194304 | tf_op jit(solution)/shard_map/pallas_call | solution.py:410
  53.8 0.0 copy-start.8
  53.8 0.1 collective-permute-start.6
  53.9 8.3 %shard_map.78.own_in = f32[28,128,256]{2,1,0:T(8,128)S(1)} custom-call(bf16[3,6,18,32,256]{4,3,2,1,0:T(8,128)(2,1)S(1)} %get-tuple-element.31.taps_in, bf16[4,16,32,256]{3,2,1,0:T(8,128)(2,1)S(1)} %get-tuple-element.32.dpre_in.field.refs_0_), custom_call_target="tpu_custom_call" | custom-call | flops 3623878656 | bytes 4194304 | tf_op jit(solution)/shard_map/pallas_call | solution.py:423
  62.2 0.0 copy-done.8
  62.2 0.0 collective-permute-done.6.received_in
  62.2 1.9 %shard_map.79 = bf16[28,128,256]{2,1,0:T(8,128)(2,1)} custom-call(f32[28,128,256]{2,1,0:T(8,128)S(1)} %shard_map.78.own_in, bf16[28,128,256]{2,1,0:T(8,128)(2,1)S(1)} %collective-permute-done.6.received_in), custom_call_target="tpu_custom_call" | custom-call | bytes 4194304 | tf_op jit(solution)/shard_map/pallas_call | solution.py:432
  64.1 7.9 %all-to-all-start = ((bf16[8,448,256]{2,1,0:T(8,128)(2,1)}), bf16[8,448,256]{2,1,0:T(8,128)(2,1)S(1)}, u32[]{:S(2)}, u32[]{:S(2)}) async-start(bf16[8,448,256]{2,1,0:T(8,128)(2,1)} %bitcast.4), calls=%async_computation | async-start | bytes 3670016 | tf_op jit(solution)/shard_map/all_to_all | solution.py:44
  72.0 1.3 collective-permute-start.7
  73.3 16.7 %collective-permute-done.7.remote.refs_1_ = bf16[2,16,32,256]{3,2,1,0:T(8,128)(2,1)S(1)} collective-permute-done((bf16[2,16,32,256]{3,2,1,0:T(8,128)(2,1)}, bf16[2,16,32,256]{3,2,1,0:T(8,128)(2,1)S(1)}, u32[]{:S(2)}, u32[]{:S(2)}) %collective-permute-start.7) | collective-permute-done | bytes 524320 | tf_op jit(solution)/shard_map/ppermute | solution.py:53
  90.0 0.1 shard_map.80
  90.2 2.1 %collective-permute-start.8 = (bf16[6,1,32,256]{3,2,1,0:T(8,128)(2,1)S(1)}, bf16[6,1,32,256]{3,2,1,0:T(8,128)(2,1)S(1)}, u32[]{:S(2)}, u32[]{:S(2)}) collective-permute-start(bf16[6,1,32,256]{3,2,1,0:T(8,128)(2,1)S(1)} %get-tuple-element.35), channel_id=1, source_target_pairs={{0,4},{4,8},{8,12},{12,16},{16,20},{20,24},{24,28},{1,5},{5,9},{9,... | collective-permute-start | bytes 294920 | tf_op jit(solution)/shard_map/ppermute | solution.py:53
  92.3 1.3 collective-permute-start.9
  93.6 0.3 collective-permute-done.8.refs_2_
  93.9 5.1 %collective-permute-done.9.refs_3_ = bf16[6,1,32,256]{3,2,1,0:T(8,128)(2,1)S(1)} collective-permute-done((bf16[6,1,32,256]{3,2,1,0:T(8,128)(2,1)S(1)}, bf16[6,1,32,256]{3,2,1,0:T(8,128)(2,1)S(1)}, u32[]{:S(2)}, u32[]{:S(2)}) %collective-permute-start.9) | collective-permute-done | bytes 98336 | tf_op jit(solution)/shard_map/ppermute | solution.py:53
  99.0 2.2 %shard_map.81 = (bf16[6,32,256]{2,1,0:T(8,128)(2,1)}, bf16[6,32,256]{2,1,0:T(8,128)(2,1)}) custom-call(bf16[4,16,32,256]{3,2,1,0:T(8,128)(2,1)S(1)} %get-tuple-element.32.dpre_in.field.refs_0_, bf16[2,16,32,256]{3,2,1,0:T(8,128)(2,1)S(1)} %collective-permute-done.7.remote.refs_1_, bf16[6,1,32,256]{3,2,1,0:T(8,128)(2,1)S(1)} %collective-permute-done.8.refs_2_, ...), custom_call_target="tpu_custom_call" | custom-call | bytes 4194304 | tf_op jit(solution)/shard_map/pallas_call | solution.py:347
  101.3 0.0 copy-start.3
  101.3 0.6 copy-done.3
  101.9 9.6 %collective-permute-start.10 = (bf16[6,32,256]{2,1,0:T(8,128)(2,1)}, bf16[6,32,256]{2,1,0:T(8,128)(2,1)}, u32[]{:S(2)}, u32[]{:S(2)}) collective-permute-start(bf16[6,32,256]{2,1,0:T(8,128)(2,1)} %get-tuple-element.37), channel_id=1, source_target_pairs={{0,1},{1,2},{2,3},{4,5},{5,6},{6,7},{8,9},{9,10},{10,11},{12,13},{... | collective-permute-start | bytes 294920 | tf_op jit(solution)/shard_map/ppermute | solution.py:53
  111.5 1.9 %collective-permute-start.11 = (bf16[6,32,256]{2,1,0:T(8,128)(2,1)}, bf16[6,32,256]{2,1,0:T(8,128)(2,1)}, u32[]{:S(2)}, u32[]{:S(2)}) collective-permute-start(bf16[6,32,256]{2,1,0:T(8,128)(2,1)} %get-tuple-element.38), channel_id=1, source_target_pairs={{1,0},{2,1},{3,2},{5,4},{6,5},{7,6},{9,8},{10,9},{11,10},{13,12},{... | collective-permute-start | bytes 294920 | tf_op jit(solution)/shard_map/ppermute | solution.py:53
  113.5 0.0 collective-permute-done.10.refs_4_
  113.5 5.7 %collective-permute-done.11.refs_5_ = bf16[6,32,256]{2,1,0:T(8,128)(2,1)} collective-permute-done((bf16[6,32,256]{2,1,0:T(8,128)(2,1)}, bf16[6,32,256]{2,1,0:T(8,128)(2,1)}, u32[]{:S(2)}, u32[]{:S(2)}) %collective-permute-start.11) | collective-permute-done | bytes 98336 | tf_op jit(solution)/shard_map/ppermute | solution.py:53
  119.2 0.0 all-to-all-done.pieces_in
  119.2 5.1 %shard_map.82 = bf16[8,448,256]{2,1,0:T(8,128)(2,1)S(1)} custom-call(bf16[8,448,256]{2,1,0:T(8,128)(2,1)S(1)} %all-to-all-done.pieces_in, s32[1]{0:T(128)} %bitcast.5.flag), custom_call_target="tpu_custom_call" | custom-call | bytes 4194304 | tf_op jit(solution)/shard_map/pallas_call | solution.py:359
  124.3 0.0 copy-start
  124.3 1.2 copy-done
  125.5 5.1 %all-to-all-start.1 = ((bf16[8,448,256]{2,1,0:T(8,128)(2,1)}), bf16[8,448,256]{2,1,0:T(8,128)(2,1)S(1)}, u32[]{:S(2)}, u32[]{:S(2)}) async-start(bf16[8,448,256]{2,1,0:T(8,128)(2,1)} %copy-done), calls=%async_computation.1 | async-start | bytes 3670016 | tf_op jit(solution)/shard_map/all_to_all | solution.py:44
  130.6 0.0 copy-start.4
  130.6 0.9 copy-done.4
  131.5 0.0 copy-start.6
  131.5 2.0 %copy-done.6 = bf16[27,256,256]{2,1,0:T(8,128)(2,1)S(1)} copy-done((bf16[27,256,256]{2,1,0:T(8,128)(2,1)S(1)}, bf16[27,256,256]{2,1,0:T(8,128)(2,1)}, u32[]{:S(2)}) %copy-start.6) | copy-done | bytes 3538968
  133.5 12.3 %shard_map.83 = bf16[4,16,32,256]{3,2,1,0:T(8,128)(2,1)} custom-call(bf16[4,16,32,256]{3,2,1,0:T(8,128)(2,1)S(1)} %get-tuple-element.32.dpre_in.field.refs_0_, bf16[2,16,32,256]{3,2,1,0:T(8,128)(2,1)S(1)} %collective-permute-done.7.remote.refs_1_, bf16[6,1,32,256]{3,2,1,0:T(8,128)(2,1)S(1)} %collective-permute-done.8.refs_2_, ...), custom_call_target="tpu_custom_call" | custom-call | flops 7247757312 | bytes 4194304 | tf_op jit(solution)/shard_map/pallas_call | solution.py:458
  145.8 0.0 all-to-all-done.1.pieces_in
  145.8 5.1 %shard_map.84 = bf16[8,448,256]{2,1,0:T(8,128)(2,1)S(1)} custom-call(bf16[8,448,256]{2,1,0:T(8,128)(2,1)S(1)} %all-to-all-done.1.pieces_in, s32[1]{0:T(128)} %bitcast.5.flag), custom_call_target="tpu_custom_call" | custom-call | bytes 4194304 | tf_op jit(solution)/shard_map/pallas_call | solution.py:359
  150.9 22.5 %all_to_all.15 = bf16[8,448,256]{2,1,0:T(8,128)(2,1)S(1)} all-to-all(bf16[8,448,256]{2,1,0:T(8,128)(2,1)S(1)} %shard_map.84), channel_id=1, replica_groups={{0,16,32,48,4,20,36,52},{18,2,50,34,22,6,54,38},{96,112,64,80,100,116,6..., dimensions={0} | all-to-all | bytes 3670016 | tf_op jit(solution)/shard_map/all_to_all | solution.py:44
  173.4 0.0 collective-permute-start.12
  173.4 2.6 %shard_map.85 = (f32[27,256,256]{2,1,0:T(8,128)}, f32[1,256]{1,0:T(1,128)}) custom-call(bf16[28,128,256]{2,1,0:T(8,128)(2,1)S(1)} %bitcast.11), custom_call_target="tpu_custom_call" | custom-call | bytes 4194304 | tf_op jit(solution)/shard_map/pallas_call | solution.py:373
  176.0 1.2 collective-permute-done.12.half_in
  177.2 2.0 %shard_map.86 = f32[27,256,256]{2,1,0:T(8,128)} custom-call(bf16[28,128,256]{2,1,0:T(8,128)(2,1)S(1)} %collective-permute-done.12.half_in, f32[27,256,256]{2,1,0:T(8,128)} %get-tuple-element.44.refs_0_), custom_call_target="tpu_custom_call", output_to_operand_aliasing={{}: (1, {})} | custom-call | bytes 4194304 | tf_op jit(solution)/shard_map/pallas_call | solution.py:373
  (5 shorter events, 0.0 us)
Async XLA Ops:
  0.6 1.2 copy-start.1
  1.9 33.2 %copy-start.2 = (bf16[4,16,32,256]{3,2,1,0:T(8,128)(2,1)S(1)}, bf16[4,16,32,256]{3,2,1,0:T(8,128)(2,1)}, u32[]{:S(2)}) copy-start(bf16[4,16,32,256]{3,2,1,0:T(8,128)(2,1)} %refs_0_.5) | copy-start | bytes 3145732
  1.9 33.2 %copy-start.7 = (bf16[4,16,32,256]{3,2,1,0:T(8,128)(2,1)S(1)}, bf16[4,16,32,256]{3,2,1,0:T(8,128)(2,1)}, u32[]{:S(2)}) copy-start(bf16[4,16,32,256]{3,2,1,0:T(8,128)(2,1)} %refs_8_.1) | copy-start | bytes 3145732
  1.9 33.2 %copy-start.9 = (f32[256]{0:T(256)S(1)}, f32[256]{0:T(256)}, u32[]{:S(2)}) copy-start(f32[256]{0:T(256)} %param.6) | copy-start | bytes 3076
  2.0 5.4 %collective-permute-start = (bf16[4,1,32,256]{3,2,1,0:T(8,128)(2,1)S(1)}, bf16[4,1,32,256]{3,2,1,0:T(8,128)(2,1)S(1)}, u32[]{:S(2)}, u32[]{:S(2)}) collective-permute-start(bf16[4,1,32,256]{3,2,1,0:T(8,128)(2,1)S(1)} %get-tuple-element.25), channel_id=1, source_target_pairs={{0,4},{4,8},{8,12},{12,16},{16,20},{20,24},{24,28},{1,5},{5,9},{9,... | collective-permute-start | bytes 196616 | tf_op jit(solution)/shard_map/ppermute | solution.py:53
  6.1 5.0 %collective-permute-start.1 = (bf16[4,1,32,256]{3,2,1,0:T(8,128)(2,1)S(1)}, bf16[4,1,32,256]{3,2,1,0:T(8,128)(2,1)S(1)}, u32[]{:S(2)}, u32[]{:S(2)}) collective-permute-start(bf16[4,1,32,256]{3,2,1,0:T(8,128)(2,1)S(1)} %get-tuple-element.26), channel_id=1, source_target_pairs={{4,0},{8,4},{12,8},{16,12},{20,16},{24,20},{28,24},{5,1},{9,5},{13... | collective-permute-start | bytes 196616 | tf_op jit(solution)/shard_map/ppermute | solution.py:53
  12.1 12.7 %collective-permute-start.2 = (bf16[4,32,256]{2,1,0:T(8,128)(2,1)S(1)}, bf16[4,32,256]{2,1,0:T(8,128)(2,1)S(1)}, u32[]{:S(2)}, u32[]{:S(2)}) collective-permute-start(bf16[4,32,256]{2,1,0:T(8,128)(2,1)S(1)} %get-tuple-element.27), channel_id=1, source_target_pairs={{0,1},{1,2},{2,3},{4,5},{5,6},{6,7},{8,9},{9,10},{10,11},{12,13},{... | collective-permute-start | bytes 196616 | tf_op jit(solution)/shard_map/ppermute | solution.py:53
  19.6 15.5 %collective-permute-start.4 = (bf16[2,16,32,256]{3,2,1,0:T(8,128)(2,1)S(1)}, bf16[2,16,32,256]{3,2,1,0:T(8,128)(2,1)S(1)}, u32[]{:S(2)}, u32[]{:S(2)}) collective-permute-start(bf16[2,16,32,256]{3,2,1,0:T(8,128)(2,1)S(1)} %get-tuple-element.29), channel_id=1, source_target_pairs={{0,32},{32,64},{64,96},{1,33},{33,65},{65,97},{2,34},{34,66},{66,9... | collective-permute-start | bytes 1572872 | tf_op jit(solution)/shard_map/ppermute | solution.py:53
  22.8 7.1 %collective-permute-start.3 = (bf16[4,32,256]{2,1,0:T(8,128)(2,1)S(1)}, bf16[4,32,256]{2,1,0:T(8,128)(2,1)S(1)}, u32[]{:S(2)}, u32[]{:S(2)}) collective-permute-start(bf16[4,32,256]{2,1,0:T(8,128)(2,1)S(1)} %get-tuple-element.28), channel_id=1, source_target_pairs={{1,0},{2,1},{3,2},{5,4},{6,5},{7,6},{9,8},{10,9},{11,10},{13,12},{... | collective-permute-start | bytes 196616 | tf_op jit(solution)/shard_map/ppermute | solution.py:53
  30.0 5.1 %collective-permute-start.5 = (bf16[2,4,32,256]{3,2,1,0:T(8,128)(2,1)S(1)}, bf16[2,4,32,256]{3,2,1,0:T(8,128)(2,1)S(1)}, u32[]{:S(2)}, u32[]{:S(2)}) collective-permute-start(bf16[2,4,32,256]{3,2,1,0:T(8,128)(2,1)S(1)} %pad_maximum_fusion), channel_id=1, source_target_pairs={{0,32},{32,64},{64,96},{1,33},{33,65},{65,97},{2,34},{34,66},{66,9... | collective-permute-start | bytes 393224 | tf_op jit(solution)/shard_map/ppermute | solution.py:53
  35.1 2.0 %copy-start.5 = (bf16[27,256,256]{2,1,0:T(8,128)(2,1)S(1)}, bf16[27,256,256]{2,1,0:T(8,128)(2,1)}, u32[]{:S(2)}) copy-start(bf16[27,256,256]{2,1,0:T(8,128)(2,1)} %refs_6_.1) | copy-start | bytes 10616836
  53.8 8.4 %copy-start.8 = (bf16[2,16,32,256]{3,2,1,0:T(8,128)(2,1)}, bf16[2,16,32,256]{3,2,1,0:T(8,128)(2,1)S(1)}, u32[]{:S(2)}) copy-start(bf16[2,16,32,256]{3,2,1,0:T(8,128)(2,1)S(1)} %get-tuple-element.34) | copy-start | bytes 1572868
  53.8 8.4 %collective-permute-start.6 = (bf16[28,128,256]{2,1,0:T(8,128)(2,1)S(1)}, bf16[28,128,256]{2,1,0:T(8,128)(2,1)S(1)}, u32[]{:S(2)}, u32[]{:S(2)}) collective-permute-start(bf16[28,128,256]{2,1,0:T(8,128)(2,1)S(1)} %get-tuple-element.33), channel_id=1, source_target_pairs={{0,1},{1,0},{2,3},{3,2},{4,5},{5,4},{6,7},{7,6},{8,9},{9,8},{10,11... | collective-permute-start | bytes 5505032 | tf_op jit(solution)/shard_map/ppermute | solution.py:421
  64.1 55.1 %all-to-all-start = ((bf16[8,448,256]{2,1,0:T(8,128)(2,1)}), bf16[8,448,256]{2,1,0:T(8,128)(2,1)S(1)}, u32[]{:S(2)}, u32[]{:S(2)}) async-start(bf16[8,448,256]{2,1,0:T(8,128)(2,1)} %bitcast.4), calls=%async_computation | async-start | bytes 3670016 | tf_op jit(solution)/shard_map/all_to_all | solution.py:44
  72.0 18.0 %collective-permute-start.7 = (bf16[2,16,32,256]{3,2,1,0:T(8,128)(2,1)}, bf16[2,16,32,256]{3,2,1,0:T(8,128)(2,1)S(1)}, u32[]{:S(2)}, u32[]{:S(2)}) collective-permute-start(bf16[2,16,32,256]{3,2,1,0:T(8,128)(2,1)} %copy-done.8), channel_id=1, source_target_pairs={{32,0},{64,32},{96,64},{33,1},{65,33},{97,65},{34,2},{66,34},{98,6... | collective-permute-start | bytes 1572872 | tf_op jit(solution)/shard_map/ppermute | solution.py:53
  90.2 3.7 %collective-permute-start.8 = (bf16[6,1,32,256]{3,2,1,0:T(8,128)(2,1)S(1)}, bf16[6,1,32,256]{3,2,1,0:T(8,128)(2,1)S(1)}, u32[]{:S(2)}, u32[]{:S(2)}) collective-permute-start(bf16[6,1,32,256]{3,2,1,0:T(8,128)(2,1)S(1)} %get-tuple-element.35), channel_id=1, source_target_pairs={{0,4},{4,8},{8,12},{12,16},{16,20},{20,24},{24,28},{1,5},{5,9},{9,... | collective-permute-start | bytes 294920 | tf_op jit(solution)/shard_map/ppermute | solution.py:53
  92.3 6.8 %collective-permute-start.9 = (bf16[6,1,32,256]{3,2,1,0:T(8,128)(2,1)S(1)}, bf16[6,1,32,256]{3,2,1,0:T(8,128)(2,1)S(1)}, u32[]{:S(2)}, u32[]{:S(2)}) collective-permute-start(bf16[6,1,32,256]{3,2,1,0:T(8,128)(2,1)S(1)} %get-tuple-element.36), channel_id=1, source_target_pairs={{4,0},{8,4},{12,8},{16,12},{20,16},{24,20},{28,24},{5,1},{9,5},{13... | collective-permute-start | bytes 294920 | tf_op jit(solution)/shard_map/ppermute | solution.py:53
  101.3 0.6 copy-start.3
  101.9 11.6 %collective-permute-start.10 = (bf16[6,32,256]{2,1,0:T(8,128)(2,1)}, bf16[6,32,256]{2,1,0:T(8,128)(2,1)}, u32[]{:S(2)}, u32[]{:S(2)}) collective-permute-start(bf16[6,32,256]{2,1,0:T(8,128)(2,1)} %get-tuple-element.37), channel_id=1, source_target_pairs={{0,1},{1,2},{2,3},{4,5},{5,6},{6,7},{8,9},{9,10},{10,11},{12,13},{... | collective-permute-start | bytes 294920 | tf_op jit(solution)/shard_map/ppermute | solution.py:53
  111.5 7.8 %collective-permute-start.11 = (bf16[6,32,256]{2,1,0:T(8,128)(2,1)}, bf16[6,32,256]{2,1,0:T(8,128)(2,1)}, u32[]{:S(2)}, u32[]{:S(2)}) collective-permute-start(bf16[6,32,256]{2,1,0:T(8,128)(2,1)} %get-tuple-element.38), channel_id=1, source_target_pairs={{1,0},{2,1},{3,2},{5,4},{6,5},{7,6},{9,8},{10,9},{11,10},{13,12},{... | collective-permute-start | bytes 294920 | tf_op jit(solution)/shard_map/ppermute | solution.py:53
  124.3 1.2 copy-start
  125.5 20.3 %all-to-all-start.1 = ((bf16[8,448,256]{2,1,0:T(8,128)(2,1)}), bf16[8,448,256]{2,1,0:T(8,128)(2,1)S(1)}, u32[]{:S(2)}, u32[]{:S(2)}) async-start(bf16[8,448,256]{2,1,0:T(8,128)(2,1)} %copy-done), calls=%async_computation.1 | async-start | bytes 3670016 | tf_op jit(solution)/shard_map/all_to_all | solution.py:44
  130.6 0.9 copy-start.4
  131.5 2.0 %copy-start.6 = (bf16[27,256,256]{2,1,0:T(8,128)(2,1)S(1)}, bf16[27,256,256]{2,1,0:T(8,128)(2,1)}, u32[]{:S(2)}) copy-start(bf16[27,256,256]{2,1,0:T(8,128)(2,1)} %refs_6_.1) | copy-start | bytes 10616836
  173.4 3.8 %collective-permute-start.12 = (bf16[28,128,256]{2,1,0:T(8,128)(2,1)S(1)}, bf16[28,128,256]{2,1,0:T(8,128)(2,1)S(1)}, u32[]{:S(2)}, u32[]{:S(2)}) collective-permute-start(bf16[28,128,256]{2,1,0:T(8,128)(2,1)S(1)} %bitcast.10), channel_id=1, source_target_pairs={{0,1},{1,0},{2,3},{3,2},{4,5},{5,4},{6,7},{7,6},{8,9},{9,8},{10,11... | collective-permute-start | bytes 5505032 | tf_op jit(solution)/shard_map/ppermute | solution.py:469

commit v3 on v2

v3 whole, which is shorter than its diff:
```python
import functools
import itertools

import jax
import jax.numpy as jnp
import numpy as np
from jax import lax
from jax.experimental import pallas as pl
from jax.experimental.pallas import tpu as pltpu
from jax.sharding import Mesh
from jax.sharding import PartitionSpec as P

AXES = ("ta", "hz", "hx", "wz", "wc")
HA = ("hz", "hx")
WA = ("wz", "wc")
BF = jnp.bfloat16
F32 = jnp.float32
VMEM = pl.BlockSpec(memory_space=pltpu.VMEM)
HBM = pl.BlockSpec(memory_space=pltpu.HBM)
MIB = 1 << 20


def number(x, y, z, core):
    return (((y * 2 + z % 2) * 4 + x) * 2 + z // 2) * 2 + core


def cubes(pairs):
    out = []
    for core in (0, 1):
        for px, py, pz in itertools.product(pairs, repeat=3):
            cube = []
            for a, b, c in itertools.product(range(2), repeat=3):
                place = [(p + core) % 4 for p in (px[a], py[b], pz[c])]
                cube.append(number(*place, core))
            out.append(cube)
    return out


NEAR = cubes(((0, 1), (3, 2)))
FAR = cubes(((0, 3), (1, 2)))


def exchange(pieces, groups):
    return lax.all_to_all(pieces, AXES, 0, 0, axis_index_groups=groups)


def shift(block, axis, distance):
    names = axis if isinstance(axis, tuple) else (axis,)
    count = 1
    for name in names:
        count *= lax.axis_size(name)
    route = [(i, i + distance) for i in range(count) if 0 <= i + distance < count]
    return lax.ppermute(block, axis, route)


def transfers(sems, *pairs):
    copies = [pltpu.make_async_copy(s, d, sems.at[i]) for i, (s, d) in enumerate(pairs)]
    for copy in copies:
        copy.start()
    return copies


def one_hot(shape, hit):
    row = lax.broadcasted_iota(jnp.int32, shape, 0)
    lane = lax.broadcasted_iota(jnp.int32, shape, 1)
    return jnp.where(hit(row, lane), 1.0, 0.0).astype(BF)


def edge_rows_kernel(start, field, top, bottom, frames, sems):
    pairs = [
        (field.at[:, pl.ds(0, 1)], top),
        (field.at[:, pl.ds(15, 1)], bottom),
        (field.at[pl.ds(start, 2)], frames),
    ]
    for copy in transfers(sems, *pairs):
        copy.wait()


def columns_kernel(field, low, high, first, last):
    pick = one_hot((64, 576), lambda i, cell: cell == 32 * (i % 32) + 31 * (i // 32))
    for t in range(4):
        block = jnp.concatenate([low[t], field[t], high[t]], axis=0).reshape(576, 256)
        found = jnp.dot(pick, block, preferred_element_type=F32)
        first[t] = found[0:32].astype(BF)
        last[t] = found[32:64].astype(BF)


def placer(taps):
    west_at = one_hot((576, 32), lambda cell, r: cell == 32 * r)
    east_at = one_hot((576, 32), lambda cell, r: cell == 32 * r + 31)

    def put(at, middle, top, bottom, west, east):
        block = jnp.concatenate([top, middle, bottom], axis=0)
        taps[1, at] = block
        block = block.astype(F32)
        column = lax.broadcasted_iota(jnp.int32, block.shape, 1)
        side = jnp.dot(west_at, west, preferred_element_type=F32).reshape(18, 32, 256)
        taps[0, at] = jnp.where(column == 0, side, pltpu.roll(block, 1, 1)).astype(BF)
        side = jnp.dot(east_at, east, preferred_element_type=F32).reshape(18, 32, 256)
        taps[2, at] = jnp.where(column == 31, side, pltpu.roll(block, 31, 1)).astype(BF)

    return put


def window(taps, c, frame, b):
    piece = taps[c, frame, pl.ds(b, 16)]
    return piece.reshape(-1, piece.shape[-1])


def weight_terms(far, own, slope, half, emit, a):
    lanes = pl.ds(pl.multiple_of(half * 128, 128), 128)

    def block(c, b):
        parts = [own[c, max(a - 2, 0) : a + 2, b : b + 16, :, lanes]]
        if a < 2:
            parts.insert(0, far[c, a:2, b : b + 16, :, lanes])
        return jnp.concatenate(parts, axis=0).reshape(2048, 128)

    value = lax.dot_general(
        jnp.concatenate([block(c, b) for b in range(3) for c in range(3)], axis=1),
        slope[...].reshape(2048, 256),
        (((0,), (0,)), ((), ())),
        preferred_element_type=F32,
    )
    emit(pl.ds(9 * a, 9), value.reshape(9, 128, 256))


def bias_rows(value):
    high = value.astype(BF).astype(F32)
    return jnp.concatenate([high, value - high, jnp.zeros((112, 256), F32)], axis=0)


def bias_term(slope):
    total = jnp.sum(slope[...].reshape(2048, 256).astype(F32), axis=0, keepdims=True)
    return jnp.broadcast_to(total, (8, 256))


def forward(frames, kernel, bias, cot):
    total = jnp.broadcast_to(bias[...], (512, 256))
    for a, (taps, at) in enumerate(frames):
        pieces = [window(taps, c, at, b) for b in range(3) for c in range(3)]
        total = total + jnp.dot(
            jnp.concatenate(pieces, axis=1), kernel[a], preferred_element_type=F32
        )
    sig = jax.nn.sigmoid(total)
    cot = cot.reshape(512, 256).astype(F32)
    slope = cot * sig * (1.0 + total * (1.0 - sig))
    field = (16, 32, 256)
    return (total * sig).astype(BF).reshape(field), slope.astype(BF).reshape(field)


def late_frames_kernel(
    field, low, high, left, right, kernel, cot, bias, activation, slopes, own, act, sems
):
    put = placer(own)

    def put_own(t):
        put(t, field[t], low[t], high[t], left[t], right[t])

    for t in range(3):
        put_own(t)
    for t in range(2):
        act[t], slopes[t] = forward([(own, t + a) for a in range(3)], kernel, bias, cot[t + 2])
        if t == 0:
            put_own(3)
        copy = pltpu.make_async_copy(act.at[t], activation.at[t + 2], sems.at[t])
        copy.start()
    for t in range(2):
        pltpu.make_async_copy(act.at[t], activation.at[t + 2], sems.at[t]).wait()


def early_frames_kernel(*refs):
    remote, edges, own, late, kernel, cot, bias = refs[:7]
    activation, top, bottom, front, slopes, far, act, sems = refs[8:]
    put = placer(far)
    for t in (1, 0):
        put(t, remote[t], edges[t, 0:1], edges[t, 1:2], edges[t, 2], edges[t, 3])
    slopes[2:4] = late[...]
    for t in (1, 0):
        frames = [(far, t + a) if t + a < 2 else (own, t + a - 2) for a in range(3)]
        act[t], slopes[t] = forward(frames, kernel, bias, cot[t])
    pairs = [
        (act, activation.at[pl.ds(0, 2)]),
        (slopes.at[pl.ds(0, 2)], front),
        (slopes.at[:, pl.ds(0, 1)], top),
        (slopes.at[:, pl.ds(15, 1)], bottom),
    ]
    for copy in transfers(sems, *pairs):
        copy.wait()


def weight_kernel(mine, far, own, slopes, out):
    core = lax.axis_index("wc")

    def emit(at, value):
        out[at] = value.astype(out.dtype)

    for a in range(3):
        weight_terms(far, own, slopes, core if mine else 1 - core, emit, a)
    if mine:
        out[27, 0:8] = bias_term(slopes)
    else:
        out[27] = bias_rows(bias_term(slopes)).astype(BF)


def join_kernel(own, received, out):
    out[0:27] = (own[0:27] + received[0:27].astype(F32)).astype(BF)
    value = own[27, 0:8] + received[27, 0:8].astype(F32) + received[27, 8:16].astype(F32)
    out[27] = bias_rows(value).astype(BF)


def sum_kernel(pieces, flag, out, total):
    for part in range(7):
        at = slice(64 * part, 64 * part + 64)
        value = pieces[0, at].astype(F32)
        for i in range(1, 8):
            value = value + pieces[i, at].astype(F32)
        total[at] = value.astype(BF)

    @pl.when(flag[0] == 1)
    def _():
        value = sum(pieces[i, 320:336].astype(F32) for i in range(8))
        total[320:336] = bias_rows(value[0:8] + value[8:16])[0:16].astype(BF)

    for i in range(8):
        out[i] = total[...]


def backward_kernel(
    field, low, high, left, right, remote, edges, kernel, latent_grad, taps
):
    put = placer(taps)

    def put_own(t):
        put(t, field[t], low[t], high[t], left[t], right[t])

    for t in (1, 0):
        put(4 + t, remote[t], edges[t, 0:1], edges[t, 1:2], edges[t, 2], edges[t, 3])
    put_own(3)

    def one(t):
        total = jnp.zeros((512, 256), F32)
        for a, b, c in itertools.product(range(3), repeat=3):
            total = total + lax.dot_general(
                window(taps, 2 - c, t + 2 - a, 2 - b),
                kernel[9 * a + 3 * b + c],
                (((1,), (1,)), ((), ())),
                preferred_element_type=F32,
            )
        latent_grad[t] = total.astype(BF).reshape(16, 32, 256)

    @pl.loop(0, 3)
    def _(i):
        put_own(2 - i)
        one(3 - i)

    one(0)


def finish_kernel(scale, turn, half, *refs):
    kernel_grad, wide, sems = refs[-3 - (turn == 0)], *refs[-2:]
    core = lax.axis_index("wc")
    rows = pl.ds(pl.multiple_of((core if turn == 0 else 1 - core) * 128, 128), 128)
    copies = []
    for k in range(9):
        at = pl.ds(3 * k, 3)
        wide[at] = half[at].astype(F32) * scale
        copies.append(pltpu.make_async_copy(wide.at[at], kernel_grad.at[at, rows], sems.at[k]))
        copies[-1].start()
    if turn == 0:
        bias_grad = refs[1]
        bias_grad[...] = (half[27, 0:1].astype(F32) + half[27, 8:9].astype(F32)) * scale
    for copy in copies:
        copy.wait()


def call(body, outs, n_in, scratch, sems, vmem=24, flops=0, specs=None, out_specs=None, moved=4 << 20, **kwargs):
    return pl.pallas_call(
        body,
        out_shape=outs,
        in_specs=specs or [HBM] * n_in,
        out_specs=out_specs or jax.tree.map(lambda _: HBM, outs),
        scratch_shapes=[*scratch] + [pltpu.SemaphoreType.DMA((sems,))] * (sems > 0),
        compiler_params=pltpu.CompilerParams(vmem_limit_bytes=int(vmem * MIB)),
        cost_estimate=pl.CostEstimate(flops=flops, bytes_accessed=moved, transcendentals=0),
        **kwargs,
    )


def shape(*dims, dtype=BF):
    return jax.ShapeDtypeStruct(dims, dtype)


def buffer(*dims, dtype=BF):
    return pltpu.VMEM(dims, dtype)


def columns_of(*sources):
    outs = (shape(4, 32, 256),) * 2
    return call(columns_kernel, outs, 3, [], 0, vmem=6, moved=1 << 10, specs=[VMEM] * 3, out_specs=(VMEM, VMEM))(*sources)


def edges_of(frames, *parts):
    low, high, left, right = (x[frames] for x in parts)
    return jnp.concatenate([low, high, left[:, None], right[:, None]], axis=1)


def sum_pieces(pieces, special):
    return call(
        sum_kernel,
        shape(8, 448, 256),
        2,
        [buffer(448, 256)],
        0,
        vmem=12,
        specs=(VMEM, pl.BlockSpec(memory_space=pltpu.SMEM)),
        out_specs=VMEM,
    )(pieces, special.astype(jnp.int32).reshape(1))


def finish(scale, turn, half, *base):
    grad = shape(27, 256, 256, dtype=F32)
    outs = (grad, shape(1, 256, dtype=F32)) if turn == 0 else grad
    return call(
        functools.partial(finish_kernel, scale, turn),
        outs,
        1 + turn,
        [buffer(27, 128, 256, dtype=F32)],
        9,
        vmem=8,
        specs=[VMEM] + [HBM] * turn,
        out_specs=(HBM, VMEM) if turn == 0 else HBM,
        input_output_aliases={1: 0} if turn else {},
    )(half, *base)


def shards(latent, kernel, bias, cotangent):
    frames, rows, columns, width = latent.shape
    cells = frames * rows * columns
    for name in AXES:
        cells *= lax.axis_size(name)
    scale = float(1.0 / np.sqrt(np.float32(cells)))
    conv_flops = 2 * 2048 * 27 * 256 * 256
    block, pair, half = (4, 16, 32, 256), (2, 16, 32, 256), (28, 128, 256)
    edge = (4, 1, 32, 256)
    bordered = (3, 6, 18, 32, 256)

    top, bottom, back = call(
        functools.partial(edge_rows_kernel, 2),
        (shape(*edge), shape(*edge), shape(*pair)),
        1,
        [],
        3,
        vmem=4,
    )(latent)
    low = shift(bottom, HA, 1)
    high = shift(top, HA, -1)
    remote = shift(back, "ta", 1)
    first, last = columns_of(latent, low, high)
    left = shift(last, WA, 1)
    right = shift(first, WA, -1)
    edges = shift(edges_of(slice(2, 4), low, high, left, right), "ta", 1)

    grouped, bias = kernel.reshape(3, 2304, 256), bias.reshape(1, 256)
    activation, late, own = call(
        late_frames_kernel,
        (shape(*block), shape(*pair), shape(3, 4, 18, 32, 256)),
        8,
        [buffer(*pair)],
        2,
        vmem=8,
        flops=conv_flops // 2,
        specs=[VMEM] * 8,
        out_specs=(HBM, VMEM, VMEM),
    )(latent, low, high, left, right, grouped, cotangent, bias)
    activation, top, bottom, front, dpre, far = call(
        early_frames_kernel,
        tuple(shape(*x) for x in (block, edge, edge, pair, block, (3, 2, 18, 32, 256))),
        8,
        [buffer(*pair)],
        4,
        vmem=8,
        flops=conv_flops // 2,
        specs=[VMEM] * 7 + [HBM],
        out_specs=(HBM,) * 4 + (VMEM,) * 2,
        input_output_aliases={7: 0},
    )(remote, edges, own, late, grouped, cotangent, bias, activation)
    remote = shift(front, "ta", -1)

    def weight_half(mine):
        return call(
            functools.partial(weight_kernel, mine),
            shape(*half, dtype=F32 if mine else BF),
            3,
            [],
            0,
            vmem=24,
            moved=1 << 10,
            specs=(VMEM, VMEM, VMEM),
            out_specs=VMEM,
        )(far, own, dpre)

    received = lax.ppermute(weight_half(False), "wc", [(0, 1), (1, 0)])
    mine = weight_half(True)
    terms = call(
        join_kernel, shape(*half), 2, [], 0, vmem=16, moved=1 << 10, specs=[VMEM] * 2, out_specs=VMEM
    )(mine, received)

    core = lax.axis_index("wc")
    z = 2 * lax.axis_index("wz") + lax.axis_index("hz")
    spot = [(p - core) % 4 for p in (lax.axis_index("hx"), lax.axis_index("ta"), z)]
    near = sum(w * ((p == 1) | (p == 2)) for w, p in zip((4, 2, 1), spot))
    terms, remote = lax.optimization_barrier((terms, remote))
    pieces = exchange(terms.reshape(8, 448, 256), NEAR)
    low = shift(bottom, HA, 1)
    high = shift(top, HA, -1)
    pieces, low, high = lax.optimization_barrier((pieces, low, high))
    total = sum_pieces(pieces, near == 7)
    first, last = columns_of(dpre, low, high)
    total, first, last = lax.optimization_barrier((total, first, last))
    pieces = exchange(total, FAR)
    left = shift(last, WA, 1)
    right = shift(first, WA, -1)
    edges = shift(edges_of(slice(0, 2), low, high, left, right), "ta", -1)
    pieces, edges = lax.optimization_barrier((pieces, edges))
    total = sum_pieces(pieces, near == 7)
    mine = exchange(total, NEAR).reshape(half)
    sources = (dpre, low, high, left, right, remote, edges, kernel)
    latent_grad = call(
        backward_kernel,
        shape(*block),
        8,
        [buffer(*bordered)],
        0,
        vmem=16,
        flops=conv_flops,
        specs=[VMEM] * 8,
        out_specs=VMEM,
    )(*sources)
    mine, latent_grad = lax.optimization_barrier((mine, latent_grad))
    other = lax.ppermute(mine, "wc", [(0, 1), (1, 0)])
    kernel_grad, bias_grad = finish(scale, 0, mine)
    kernel_grad = finish(scale, 1, other, kernel_grad)
    return (activation, latent_grad, kernel_grad, bias_grad.reshape(256))


def solution(mesh):
    split = Mesh(np.asarray(mesh.devices).reshape(4, 2, 4, 2, 2), AXES)
    placed = P("ta", HA, WA, None)
    return jax.shard_map(
        shards,
        mesh=split,
        in_specs=(placed, P(), P(), placed),
        out_specs=(placed, placed, P(), P()),
        check_vma=False,
    )
```

time: 180 us -> 140 us (0.78)
  blocking collectives: 22.5 us -> 0 us
  Pallas kernels: 57.3 us -> 36.6 us
  waiting for transfers between devices: 39.9 us -> 44.1 us
  starting transfers between devices: 50.5 us -> 47.4 us
    all_to_all x1 -> x0, blocking collectives: 22.5 us -> none  [exchange(): return lax.all_to_all(pieces, AXES, 0, 0, axis_index_groups=groups)]
    pallas_call x10 -> x11, Pallas kernels: 52.7 us -> 32.3 us  [the longest x1 10.7 us: shards(): call(backward_kernel, shape(*block), 8, [buffer(*bordered)], 0, vmem=16,...]
    all_to_all x2 -> x3, waiting for transfers between devices: 0.01 us -> 10.4 us  [exchange(): return lax.all_to_all(pieces, AXES, 0, 0, axis_index_groups=groups)]
    ppermute x11 -> x12, waiting for transfers between devices: 38.7 us -> 32.4 us  [shift(): return lax.ppermute(block, axis, route)]
    ppermute x11 -> x12, starting transfers between devices: 37.4 us -> 32.8 us  [shift(): return lax.ppermute(block, axis, route)]
    unnamed x20 -> x18, local copies, waits for them, and re-layouts: 7.98 us -> 9.5 us
    all_to_all x2 -> x3, starting transfers between devices: 13 us -> 14.5 us  [exchange(): return lax.all_to_all(pieces, AXES, 0, 0, axis_index_groups=groups)]
  transfers between devices with their start and end apart: 15 -> 17, of which waited for: 8 -> 11; matrix products, arithmetic and copies ran while one was open for 0% -> 0% of each run, Pallas kernels for 14% -> 17%
where the time goes in v3:
time: 140 us; the launch traced here: 139 us
  starting transfers between devices  47.4 us (34%)
  waiting for transfers between devices  44.1 us (32%)
  Pallas kernels  36.6 us (26%)
  local copies, waits for them, and re-layouts  9.53 us (7%)
    ppermute x12, starting transfers between devices, shift(): return lax.ppermute(block, axis, route)  32.8 us
    ppermute x12, waiting for transfers between devices, shift(): return lax.ppermute(block, axis, route)  32.4 us
    all_to_all x3, starting transfers between devices, exchange(): return lax.all_to_all(pieces, AXES, 0, 0, axis_index_groups=groups)  14.5 us
    pallas_call x1, Pallas kernels, shards(): call(backward_kernel, shape(*block), 8, [buffer(*bordered)], 0, vmem=16,...  10.7 us
    all_to_all x3, waiting for transfers between devices, exchange(): return lax.all_to_all(pieces, AXES, 0, 0, axis_index_groups=groups)  10.4 us
    unnamed x18, local copies, waits for them, and re-layouts  9.5 us
    pallas_call x2, Pallas kernels, weight_half(): call(functools.partial(weight_kernel, mine), shape(*half, dtype=F32 if mi...  7.82 us
    pallas_call x1, Pallas kernels, shards(): call(late_frames_kernel, (shape(*block), shape(*pair), shape(3, 4, 18, 32...  5.5 us
  transfers between devices with their start and end apart: 17, of which 11 were waited for; matrix products, arithmetic and copies ran while one was open for 0% of the time, Pallas kernels for 17%

profile of v3, /device:TPU:1, one launch (start us, length us, event | category | flops | bytes accessed | tf_op | source)
XLA Modules:
  0.0 138.9 jit_solution(13411497485492479613)
XLA Ops:
  0.6 0.0 copy-start.2
  0.6 1.2 copy-done.2
  1.9 0.0 copy-start.5
  1.9 0.0 copy-start.8
  1.9 0.1 shard_map.75
  2.0 4.1 %collective-permute-start.1 = (bf16[4,1,32,256]{3,2,1,0:T(8,128)(2,1)S(1)}, bf16[4,1,32,256]{3,2,1,0:T(8,128)(2,1)S(1)}, u32[]{:S(2)}, u32[]{:S(2)}) collective-permute-start(bf16[4,1,32,256]{3,2,1,0:T(8,128)(2,1)S(1)} %get-tuple-element.35), channel_id=1, source_target_pairs={{0,4},{4,8},{8,12},{12,16},{16,20},{20,24},{24,28},{1,5},{5,9},{9,... | collective-permute-start | bytes 196616 | tf_op jit(solution)/shard_map/ppermute | solution.py:53
  6.1 1.3 collective-permute-start.2
  7.4 0.0 collective-permute-done.1.low
  7.4 3.7 %collective-permute-done.2.high = bf16[4,1,32,256]{3,2,1,0:T(8,128)(2,1)S(1)} collective-permute-done((bf16[4,1,32,256]{3,2,1,0:T(8,128)(2,1)S(1)}, bf16[4,1,32,256]{3,2,1,0:T(8,128)(2,1)S(1)}, u32[]{:S(2)}, u32[]{:S(2)}) %collective-permute-start.2) | collective-permute-done | bytes 65568 | tf_op jit(solution)/shard_map/ppermute | solution.py:53
  11.1 0.3 shard_map.76
  11.4 7.5 %collective-permute-start.3 = (bf16[4,32,256]{2,1,0:T(8,128)(2,1)S(1)}, bf16[4,32,256]{2,1,0:T(8,128)(2,1)S(1)}, u32[]{:S(2)}, u32[]{:S(2)}) collective-permute-start(bf16[4,32,256]{2,1,0:T(8,128)(2,1)S(1)} %get-tuple-element.37), channel_id=1, source_target_pairs={{0,1},{1,2},{2,3},{4,5},{5,6},{6,7},{8,9},{9,10},{10,11},{12,13},{... | collective-permute-start | bytes 196616 | tf_op jit(solution)/shard_map/ppermute | solution.py:53
  18.9 3.2 %collective-permute-start = (bf16[2,16,32,256]{3,2,1,0:T(8,128)(2,1)S(1)}, bf16[2,16,32,256]{3,2,1,0:T(8,128)(2,1)S(1)}, u32[]{:S(2)}, u32[]{:S(2)}) collective-permute-start(bf16[2,16,32,256]{3,2,1,0:T(8,128)(2,1)S(1)} %get-tuple-element.34), channel_id=1, source_target_pairs={{0,32},{32,64},{64,96},{1,33},{33,65},{65,97},{2,34},{34,66},{66,9... | collective-permute-start | bytes 1572872 | tf_op jit(solution)/shard_map/ppermute | solution.py:53
  22.2 1.9 %collective-permute-start.4 = (bf16[4,32,256]{2,1,0:T(8,128)(2,1)S(1)}, bf16[4,32,256]{2,1,0:T(8,128)(2,1)S(1)}, u32[]{:S(2)}, u32[]{:S(2)}) collective-permute-start(bf16[4,32,256]{2,1,0:T(8,128)(2,1)S(1)} %get-tuple-element.38), channel_id=1, source_target_pairs={{1,0},{2,1},{3,2},{5,4},{6,5},{7,6},{9,8},{10,9},{11,10},{13,12},{... | collective-permute-start | bytes 196616 | tf_op jit(solution)/shard_map/ppermute | solution.py:53
  24.1 0.0 collective-permute-done.3.left
  24.1 5.1 %collective-permute-done.4.right = bf16[4,32,256]{2,1,0:T(8,128)(2,1)S(1)} collective-permute-done((bf16[4,32,256]{2,1,0:T(8,128)(2,1)S(1)}, bf16[4,32,256]{2,1,0:T(8,128)(2,1)S(1)}, u32[]{:S(2)}, u32[]{:S(2)}) %collective-permute-start.4) | collective-permute-done | bytes 65568 | tf_op jit(solution)/shard_map/ppermute | solution.py:53
  29.3 3.2 %collective-permute-start.5 = (bf16[2,4,32,256]{3,2,1,0:T(8,128)(2,1)S(1)}, bf16[2,4,32,256]{3,2,1,0:T(8,128)(2,1)S(1)}, u32[]{:S(2)}, u32[]{:S(2)}) collective-permute-start(bf16[2,4,32,256]{3,2,1,0:T(8,128)(2,1)S(1)} %pad_maximum_fusion), channel_id=1, source_target_pairs={{0,32},{32,64},{64,96},{1,33},{33,65},{65,97},{2,34},{34,66},{66,9... | collective-permute-start | bytes 393224 | tf_op jit(solution)/shard_map/ppermute | solution.py:53
  32.5 0.0 copy-done.5
  32.5 0.0 copy-done.8
  32.5 0.0 copy-start.3
  32.5 2.0 %copy-done.3 = bf16[27,256,256]{2,1,0:T(8,128)(2,1)S(1)} copy-done((bf16[27,256,256]{2,1,0:T(8,128)(2,1)S(1)}, bf16[27,256,256]{2,1,0:T(8,128)(2,1)}, u32[]{:S(2)}) %copy-start.3) | copy-done | bytes 3538968
  34.5 5.5 %shard_map.77 = (bf16[4,16,32,256]{3,2,1,0:T(8,128)(2,1)}, bf16[2,16,32,256]{3,2,1,0:T(8,128)(2,1)S(1)}, bf16[3,4,18,32,256]{4,3,2,1,0:T(8,128)(2,1)S(1)}) custom-call(bf16[4,16,32,256]{3,2,1,0:T(8,128)(2,1)S(1)} %copy-done.2, bf16[4,1,32,256]{3,2,1,0:T(8,128)(2,1)S(1)} %collective-permute-done.1.low, ...), custom_call_target="tpu_custom_call" | custom-call | flops 3623878656 | bytes 4194304 | tf_op jit(solution)/shard_map/pallas_call | solution.py:365
  40.0 0.0 collective-permute-done.5.refs_1_
  40.0 0.0 collective-permute-done.refs_0_
  40.0 5.2 %shard_map.78 = (bf16[4,16,32,256]{3,2,1,0:T(8,128)(2,1)}, bf16[4,1,32,256]{3,2,1,0:T(8,128)(2,1)S(1)}, bf16[4,1,32,256]{3,2,1,0:T(8,128)(2,1)S(1)}, bf16[2,16,3...) custom-call(bf16[2,16,32,256]{3,2,1,0:T(8,128)(2,1)S(1)} %collective, ...), custom_call_target="tpu_custom_call", output_to_operand_aliasing={{0}: (7, {})} | custom-call | flops 3623878656 | bytes 4194304 | tf_op jit(solution)/shard_map/pallas_call | solution.py:376
  45.3 3.9 %shard_map.80 = bf16[28,128,256]{2,1,0:T(8,128)(2,1)S(1)} custom-call(bf16[3,2,18,32,256]{4,3,2,1,0:T(8,128)(2,1)S(1)} %get-tuple-element.43.far, bf16[3,4,18,32,256]{4,3,2,1,0:T(8,128)(2,1)S(1)} %get-tuple-element.39.refs_2_.own, bf16[4,16,32,256]{3,2,1,0:T(8,128)(2,1)S(1)} %get-tuple-element.44.slopes.field), custom_call_target="tpu_custom_call" | custom-call | bytes 1024 | tf_op jit(solution)/shard_map/pallas_call | solution.py:391
  49.2 0.1 collective-permute-start.6
  49.3 1.5 %collective-permute-start.7 = (bf16[2,16,32,256]{3,2,1,0:T(8,128)(2,1)S(1)}, bf16[2,16,32,256]{3,2,1,0:T(8,128)(2,1)S(1)}, u32[]{:S(2)}, u32[]{:S(2)}) collective-permute-start(bf16[2,16,32,256]{3,2,1,0:T(8,128)(2,1)S(1)} %get-tuple-element.45), channel_id=1, source_target_pairs={{32,0},{64,32},{96,64},{33,1},{65,33},{97,65},{34,2},{66,34},{98,6... | collective-permute-start | bytes 1572872 | tf_op jit(solution)/shard_map/ppermute | solution.py:53
  50.7 3.9 %shard_map.79.own = f32[28,128,256]{2,1,0:T(8,128)S(1)} custom-call(bf16[3,2,18,32,256]{4,3,2,1,0:T(8,128)(2,1)S(1)} %get-tuple-element.43.far, bf16[3,4,18,32,256]{4,3,2,1,0:T(8,128)(2,1)S(1)} %get-tuple-element.39.refs_2_.own, bf16[4,16,32,256]{3,2,1,0:T(8,128)(2,1)S(1)} %get-tuple-element.44.slopes.field), custom_call_target="tpu_custom_call" | custom-call | bytes 1024 | tf_op jit(solution)/shard_map/pallas_call | solution.py:391
  54.7 0.0 collective-permute-done.6.received
  54.7 1.5 %shard_map.81 = bf16[28,128,256]{2,1,0:T(8,128)(2,1)} custom-call(f32[28,128,256]{2,1,0:T(8,128)S(1)} %shard_map.79.own, bf16[28,128,256]{2,1,0:T(8,128)(2,1)S(1)} %collective-permute-done.6.received), custom_call_target="tpu_custom_call" | custom-call | bytes 1024 | tf_op jit(solution)/shard_map/pallas_call | solution.py:405
  56.2 8.0 %collective-permute-done.7.remote = bf16[2,16,32,256]{3,2,1,0:T(8,128)(2,1)S(1)} collective-permute-done((bf16[2,16,32,256]{3,2,1,0:T(8,128)(2,1)S(1)}, bf16[2,16,32,256]{3,2,1,0:T(8,128)(2,1)S(1)}, u32[]{:S(2)}, u32[]{:S(2)}) %collective-permute-start.7) | collective-permute-done | bytes 524320 | tf_op jit(solution)/shard_map/ppermute | solution.py:53
  64.2 0.0 copy-start.6
  64.2 0.8 copy-done.6
  65.0 5.9 %all-to-all-start = ((bf16[8,448,256]{2,1,0:T(8,128)(2,1)}), bf16[8,448,256]{2,1,0:T(8,128)(2,1)S(1)}, u32[]{:S(2)}, u32[]{:S(2)}) async-start(bf16[8,448,256]{2,1,0:T(8,128)(2,1)} %bitcast.4), calls=%async_computation | async-start | bytes 3670016 | tf_op jit(solution)/shard_map/all_to_all | solution.py:44
  70.9 1.3 collective-permute-start.8
  72.2 1.3 collective-permute-start.9
  73.5 0.6 collective-permute-done.8.low
  74.1 4.1 %collective-permute-done.9.high = bf16[4,1,32,256]{3,2,1,0:T(8,128)(2,1)S(1)} collective-permute-done((bf16[4,1,32,256]{3,2,1,0:T(8,128)(2,1)S(1)}, bf16[4,1,32,256]{3,2,1,0:T(8,128)(2,1)S(1)}, u32[]{:S(2)}, u32[]{:S(2)}) %collective-permute-start.9) | collective-permute-done | bytes 65568 | tf_op jit(solution)/shard_map/ppermute | solution.py:53
  78.2 8.4 %all-to-all-done.pieces = bf16[8,448,256]{2,1,0:T(8,128)(2,1)S(1)} async-done(((bf16[8,448,256]{2,1,0:T(8,128)(2,1)}), bf16[8,448,256]{2,1,0:T(8,128)(2,1)S(1)}, u32[]{:S(2)}, u32[]{:S(2)}) %all-to-all-start) | async-done | bytes 1835040 | tf_op jit(solution)/shard_map/all_to_all | solution.py:44
  86.6 0.4 shard_map.82
  87.0 0.0 copy-start
  87.0 1.2 copy-done
  88.2 0.3 shard_map.83
  88.6 4.6 %all-to-all-start.1 = ((bf16[8,448,256]{2,1,0:T(8,128)(2,1)}), bf16[8,448,256]{2,1,0:T(8,128)(2,1)S(1)}, u32[]{:S(2)}, u32[]{:S(2)}) async-start(bf16[8,448,256]{2,1,0:T(8,128)(2,1)} %copy-done), calls=%async_computation.1 | async-start | bytes 3670016 | tf_op jit(solution)/shard_map/all_to_all | solution.py:44
  93.1 4.4 %collective-permute-start.10 = (bf16[4,32,256]{2,1,0:T(8,128)(2,1)S(1)}, bf16[4,32,256]{2,1,0:T(8,128)(2,1)S(1)}, u32[]{:S(2)}, u32[]{:S(2)}) collective-permute-start(bf16[4,32,256]{2,1,0:T(8,128)(2,1)S(1)} %get-tuple-element.55), channel_id=1, source_target_pairs={{0,1},{1,2},{2,3},{4,5},{5,6},{6,7},{8,9},{9,10},{10,11},{12,13},{... | collective-permute-start | bytes 196616 | tf_op jit(solution)/shard_map/ppermute | solution.py:53
  97.5 1.9 %collective-permute-start.11 = (bf16[4,32,256]{2,1,0:T(8,128)(2,1)S(1)}, bf16[4,32,256]{2,1,0:T(8,128)(2,1)S(1)}, u32[]{:S(2)}, u32[]{:S(2)}) collective-permute-start(bf16[4,32,256]{2,1,0:T(8,128)(2,1)S(1)} %get-tuple-element.56), channel_id=1, source_target_pairs={{1,0},{2,1},{3,2},{5,4},{6,5},{7,6},{9,8},{10,9},{11,10},{13,12},{... | collective-permute-start | bytes 196616 | tf_op jit(solution)/shard_map/ppermute | solution.py:53
  99.4 4.9 %collective-permute-done.10.left = bf16[4,32,256]{2,1,0:T(8,128)(2,1)S(1)} collective-permute-done((bf16[4,32,256]{2,1,0:T(8,128)(2,1)S(1)}, bf16[4,32,256]{2,1,0:T(8,128)(2,1)S(1)}, u32[]{:S(2)}, u32[]{:S(2)}) %collective-permute-start.10) | collective-permute-done | bytes 65568 | tf_op jit(solution)/shard_map/ppermute | solution.py:53
  104.4 1.6 %collective-permute-done.11.right = bf16[4,32,256]{2,1,0:T(8,128)(2,1)S(1)} collective-permute-done((bf16[4,32,256]{2,1,0:T(8,128)(2,1)S(1)}, bf16[4,32,256]{2,1,0:T(8,128)(2,1)S(1)}, u32[]{:S(2)}, u32[]{:S(2)}) %collective-permute-start.11) | collective-permute-done | bytes 65568 | tf_op jit(solution)/shard_map/ppermute | solution.py:53
  106.0 1.3 collective-permute-start.12
  107.3 4.4 %collective-permute-done.12.edges = bf16[2,4,32,256]{3,2,1,0:T(8,128)(2,1)S(1)} collective-permute-done((bf16[2,4,32,256]{3,2,1,0:T(8,128)(2,1)S(1)}, bf16[2,4,32,256]{3,2,1,0:T(8,128)(2,1)S(1)}, u32[]{:S(2)}, u32[]{:S(2)}) %collective-permute-start.12) | collective-permute-done | bytes 131104 | tf_op jit(solution)/shard_map/ppermute | solution.py:53
  111.7 0.0 all-to-all-done.1.pieces
  111.7 0.4 shard_map.84
  112.0 0.0 copy-start.1
  112.1 1.2 copy-done.1
  113.3 4.0 %all-to-all-start.2 = ((bf16[8,448,256]{2,1,0:T(8,128)(2,1)}), bf16[8,448,256]{2,1,0:T(8,128)(2,1)S(1)}, u32[]{:S(2)}, u32[]{:S(2)}) async-start(bf16[8,448,256]{2,1,0:T(8,128)(2,1)} %copy-done.1), calls=%async_computation.2 | async-start | bytes 3670016 | tf_op jit(solution)/shard_map/all_to_all | solution.py:44
  117.3 0.0 copy-start.4
  117.3 2.0 %copy-done.4 = bf16[27,256,256]{2,1,0:T(8,128)(2,1)S(1)} copy-done((bf16[27,256,256]{2,1,0:T(8,128)(2,1)S(1)}, bf16[27,256,256]{2,1,0:T(8,128)(2,1)}, u32[]{:S(2)}) %copy-start.4) | copy-done | bytes 3538968
  119.3 1.0 copy-done.7
  120.3 10.7 %shard_map.85 = bf16[4,16,32,256]{3,2,1,0:T(8,128)(2,1)} custom-call(bf16[4,16,32,256]{3,2,1,0:T(8,128)(2,1)S(1)} %get-tuple-element.44.slopes.field, bf16[4,1,32,256]{3,2,1,0:T(8,128)(2,1)S(1)} %collective-permute-done.8.low, bf16[4,1,32,256]{3,2,1,0:T(8,128)(2,1)S(1)} %collective-permute-done.9.high, bf16[4,32,256]{2,1,0:T(8,128)(2,1)S(1)} %collective-permute-done.10.left, ...), custom_call_target="tpu_custom_call" | custom-call | flops 7247757312 | bytes 4194304 | tf_op jit(solution)/shard_map/pallas_call | solution.py:429
  131.0 2.0 %all-to-all-done.2 = bf16[8,448,256]{2,1,0:T(8,128)(2,1)S(1)} async-done(((bf16[8,448,256]{2,1,0:T(8,128)(2,1)}), bf16[8,448,256]{2,1,0:T(8,128)(2,1)S(1)}, u32[]{:S(2)}, u32[]{:S(2)}) %all-to-all-start.2) | async-done | bytes 1835040 | tf_op jit(solution)/shard_map/all_to_all | solution.py:44
  133.0 0.0 collective-permute-start.13
  133.0 2.4 %shard_map.86 = (f32[27,256,256]{2,1,0:T(8,128)}, f32[1,256]{1,0:T(1,128)}) custom-call(bf16[28,128,256]{2,1,0:T(8,128)(2,1)S(1)} %bitcast.15), custom_call_target="tpu_custom_call" | custom-call | bytes 4194304 | tf_op jit(solution)/shard_map/pallas_call | solution.py:324
  135.5 1.3 collective-permute-done.13.half
  136.8 1.9 %shard_map.87 = f32[27,256,256]{2,1,0:T(8,128)} custom-call(bf16[28,128,256]{2,1,0:T(8,128)(2,1)S(1)} %collective-permute-done.13.half, f32[27,256,256]{2,1,0:T(8,128)} %get-tuple-element.62.refs_0_), custom_call_target="tpu_custom_call", output_to_operand_aliasing={{}: (1, {})} | custom-call | bytes 4194304 | tf_op jit(solution)/shard_map/pallas_call | solution.py:324
  (11 shorter events, 0.1 us)
Async XLA Ops:
  0.6 1.2 copy-start.2
  1.9 30.6 %copy-start.5 = (bf16[4,16,32,256]{3,2,1,0:T(8,128)(2,1)S(1)}, bf16[4,16,32,256]{3,2,1,0:T(8,128)(2,1)}, u32[]{:S(2)}) copy-start(bf16[4,16,32,256]{3,2,1,0:T(8,128)(2,1)} %refs_5_.1) | copy-start | bytes 3145732
  1.9 30.6 %copy-start.8 = (f32[256]{0:T(256)S(1)}, f32[256]{0:T(256)}, u32[]{:S(2)}) copy-start(f32[256]{0:T(256)} %param.6) | copy-start | bytes 3076
  2.0 5.4 %collective-permute-start.1 = (bf16[4,1,32,256]{3,2,1,0:T(8,128)(2,1)S(1)}, bf16[4,1,32,256]{3,2,1,0:T(8,128)(2,1)S(1)}, u32[]{:S(2)}, u32[]{:S(2)}) collective-permute-start(bf16[4,1,32,256]{3,2,1,0:T(8,128)(2,1)S(1)} %get-tuple-element.35), channel_id=1, source_target_pairs={{0,4},{4,8},{8,12},{12,16},{16,20},{20,24},{24,28},{1,5},{5,9},{9,... | collective-permute-start | bytes 196616 | tf_op jit(solution)/shard_map/ppermute | solution.py:53
  6.1 5.0 %collective-permute-start.2 = (bf16[4,1,32,256]{3,2,1,0:T(8,128)(2,1)S(1)}, bf16[4,1,32,256]{3,2,1,0:T(8,128)(2,1)S(1)}, u32[]{:S(2)}, u32[]{:S(2)}) collective-permute-start(bf16[4,1,32,256]{3,2,1,0:T(8,128)(2,1)S(1)} %get-tuple-element.36), channel_id=1, source_target_pairs={{4,0},{8,4},{12,8},{16,12},{20,16},{24,20},{28,24},{5,1},{9,5},{13... | collective-permute-start | bytes 196616 | tf_op jit(solution)/shard_map/ppermute | solution.py:53
  11.4 12.7 %collective-permute-start.3 = (bf16[4,32,256]{2,1,0:T(8,128)(2,1)S(1)}, bf16[4,32,256]{2,1,0:T(8,128)(2,1)S(1)}, u32[]{:S(2)}, u32[]{:S(2)}) collective-permute-start(bf16[4,32,256]{2,1,0:T(8,128)(2,1)S(1)} %get-tuple-element.37), channel_id=1, source_target_pairs={{0,1},{1,2},{2,3},{4,5},{5,6},{6,7},{8,9},{9,10},{10,11},{12,13},{... | collective-permute-start | bytes 196616 | tf_op jit(solution)/shard_map/ppermute | solution.py:53
  18.9 21.1 %collective-permute-start = (bf16[2,16,32,256]{3,2,1,0:T(8,128)(2,1)S(1)}, bf16[2,16,32,256]{3,2,1,0:T(8,128)(2,1)S(1)}, u32[]{:S(2)}, u32[]{:S(2)}) collective-permute-start(bf16[2,16,32,256]{3,2,1,0:T(8,128)(2,1)S(1)} %get-tuple-element.34), channel_id=1, source_target_pairs={{0,32},{32,64},{64,96},{1,33},{33,65},{65,97},{2,34},{34,66},{66,9... | collective-permute-start | bytes 1572872 | tf_op jit(solution)/shard_map/ppermute | solution.py:53
  22.2 7.1 %collective-permute-start.4 = (bf16[4,32,256]{2,1,0:T(8,128)(2,1)S(1)}, bf16[4,32,256]{2,1,0:T(8,128)(2,1)S(1)}, u32[]{:S(2)}, u32[]{:S(2)}) collective-permute-start(bf16[4,32,256]{2,1,0:T(8,128)(2,1)S(1)} %get-tuple-element.38), channel_id=1, source_target_pairs={{1,0},{2,1},{3,2},{5,4},{6,5},{7,6},{9,8},{10,9},{11,10},{13,12},{... | collective-permute-start | bytes 196616 | tf_op jit(solution)/shard_map/ppermute | solution.py:53
  29.3 10.7 %collective-permute-start.5 = (bf16[2,4,32,256]{3,2,1,0:T(8,128)(2,1)S(1)}, bf16[2,4,32,256]{3,2,1,0:T(8,128)(2,1)S(1)}, u32[]{:S(2)}, u32[]{:S(2)}) collective-permute-start(bf16[2,4,32,256]{3,2,1,0:T(8,128)(2,1)S(1)} %pad_maximum_fusion), channel_id=1, source_target_pairs={{0,32},{32,64},{64,96},{1,33},{33,65},{65,97},{2,34},{34,66},{66,9... | collective-permute-start | bytes 393224 | tf_op jit(solution)/shard_map/ppermute | solution.py:53
  32.5 2.0 %copy-start.3 = (bf16[27,256,256]{2,1,0:T(8,128)(2,1)S(1)}, bf16[27,256,256]{2,1,0:T(8,128)(2,1)}, u32[]{:S(2)}) copy-start(bf16[27,256,256]{2,1,0:T(8,128)(2,1)} %kernel.1) | copy-start | bytes 10616836
  49.2 5.5 %collective-permute-start.6 = (bf16[28,128,256]{2,1,0:T(8,128)(2,1)S(1)}, bf16[28,128,256]{2,1,0:T(8,128)(2,1)S(1)}, u32[]{:S(2)}, u32[]{:S(2)}) collective-permute-start(bf16[28,128,256]{2,1,0:T(8,128)(2,1)S(1)} %shard_map.80), channel_id=1, source_target_pairs={{0,1},{1,0},{2,3},{3,2},{4,5},{5,4},{6,7},{7,6},{8,9},{9,8},{10,11... | collective-permute-start | bytes 5505032 | tf_op jit(solution)/shard_map/ppermute | solution.py:403
  49.3 14.9 %collective-permute-start.7 = (bf16[2,16,32,256]{3,2,1,0:T(8,128)(2,1)S(1)}, bf16[2,16,32,256]{3,2,1,0:T(8,128)(2,1)S(1)}, u32[]{:S(2)}, u32[]{:S(2)}) collective-permute-start(bf16[2,16,32,256]{3,2,1,0:T(8,128)(2,1)S(1)} %get-tuple-element.45), channel_id=1, source_target_pairs={{32,0},{64,32},{96,64},{33,1},{65,33},{97,65},{34,2},{66,34},{98,6... | collective-permute-start | bytes 1572872 | tf_op jit(solution)/shard_map/ppermute | solution.py:53
  64.2 0.8 copy-start.6
  65.0 21.7 %all-to-all-start = ((bf16[8,448,256]{2,1,0:T(8,128)(2,1)}), bf16[8,448,256]{2,1,0:T(8,128)(2,1)S(1)}, u32[]{:S(2)}, u32[]{:S(2)}) async-start(bf16[8,448,256]{2,1,0:T(8,128)(2,1)} %bitcast.4), calls=%async_computation | async-start | bytes 3670016 | tf_op jit(solution)/shard_map/all_to_all | solution.py:44
  70.9 3.2 %collective-permute-start.8 = (bf16[4,1,32,256]{3,2,1,0:T(8,128)(2,1)S(1)}, bf16[4,1,32,256]{3,2,1,0:T(8,128)(2,1)S(1)}, u32[]{:S(2)}, u32[]{:S(2)}) collective-permute-start(bf16[4,1,32,256]{3,2,1,0:T(8,128)(2,1)S(1)} %get-tuple-element.47), channel_id=1, source_target_pairs={{0,4},{4,8},{8,12},{12,16},{16,20},{20,24},{24,28},{1,5},{5,9},{9,... | collective-permute-start | bytes 196616 | tf_op jit(solution)/shard_map/ppermute | solution.py:53
  72.2 6.1 %collective-permute-start.9 = (bf16[4,1,32,256]{3,2,1,0:T(8,128)(2,1)S(1)}, bf16[4,1,32,256]{3,2,1,0:T(8,128)(2,1)S(1)}, u32[]{:S(2)}, u32[]{:S(2)}) collective-permute-start(bf16[4,1,32,256]{3,2,1,0:T(8,128)(2,1)S(1)} %get-tuple-element.48), channel_id=1, source_target_pairs={{4,0},{8,4},{12,8},{16,12},{20,16},{24,20},{28,24},{5,1},{9,5},{13... | collective-permute-start | bytes 196616 | tf_op jit(solution)/shard_map/ppermute | solution.py:53
  87.0 1.2 copy-start
  88.6 23.1 %all-to-all-start.1 = ((bf16[8,448,256]{2,1,0:T(8,128)(2,1)}), bf16[8,448,256]{2,1,0:T(8,128)(2,1)S(1)}, u32[]{:S(2)}, u32[]{:S(2)}) async-start(bf16[8,448,256]{2,1,0:T(8,128)(2,1)} %copy-done), calls=%async_computation.1 | async-start | bytes 3670016 | tf_op jit(solution)/shard_map/all_to_all | solution.py:44
  93.1 11.2 %collective-permute-start.10 = (bf16[4,32,256]{2,1,0:T(8,128)(2,1)S(1)}, bf16[4,32,256]{2,1,0:T(8,128)(2,1)S(1)}, u32[]{:S(2)}, u32[]{:S(2)}) collective-permute-start(bf16[4,32,256]{2,1,0:T(8,128)(2,1)S(1)} %get-tuple-element.55), channel_id=1, source_target_pairs={{0,1},{1,2},{2,3},{4,5},{5,6},{6,7},{8,9},{9,10},{10,11},{12,13},{... | collective-permute-start | bytes 196616 | tf_op jit(solution)/shard_map/ppermute | solution.py:53
  97.5 8.4 %collective-permute-start.11 = (bf16[4,32,256]{2,1,0:T(8,128)(2,1)S(1)}, bf16[4,32,256]{2,1,0:T(8,128)(2,1)S(1)}, u32[]{:S(2)}, u32[]{:S(2)}) collective-permute-start(bf16[4,32,256]{2,1,0:T(8,128)(2,1)S(1)} %get-tuple-element.56), channel_id=1, source_target_pairs={{1,0},{2,1},{3,2},{5,4},{6,5},{7,6},{9,8},{10,9},{11,10},{13,12},{... | collective-permute-start | bytes 196616 | tf_op jit(solution)/shard_map/ppermute | solution.py:53
  106.0 5.7 %collective-permute-start.12 = (bf16[2,4,32,256]{3,2,1,0:T(8,128)(2,1)S(1)}, bf16[2,4,32,256]{3,2,1,0:T(8,128)(2,1)S(1)}, u32[]{:S(2)}, u32[]{:S(2)}) collective-permute-start(bf16[2,4,32,256]{3,2,1,0:T(8,128)(2,1)S(1)} %pad_maximum_fusion.1), channel_id=1, source_target_pairs={{32,0},{64,32},{96,64},{33,1},{65,33},{97,65},{34,2},{66,34},{98,6... | collective-permute-start | bytes 393224 | tf_op jit(solution)/shard_map/ppermute | solution.py:53
  112.0 1.2 copy-start.1
  113.3 19.8 %all-to-all-start.2 = ((bf16[8,448,256]{2,1,0:T(8,128)(2,1)}), bf16[8,448,256]{2,1,0:T(8,128)(2,1)S(1)}, u32[]{:S(2)}, u32[]{:S(2)}) async-start(bf16[8,448,256]{2,1,0:T(8,128)(2,1)} %copy-done.1), calls=%async_computation.2 | async-start | bytes 3670016 | tf_op jit(solution)/shard_map/all_to_all | solution.py:44
  117.3 2.0 %copy-start.4 = (bf16[27,256,256]{2,1,0:T(8,128)(2,1)S(1)}, bf16[27,256,256]{2,1,0:T(8,128)(2,1)}, u32[]{:S(2)}) copy-start(bf16[27,256,256]{2,1,0:T(8,128)(2,1)} %kernel.1) | copy-start | bytes 10616836
  119.3 1.0 copy-start.7
  133.0 3.8 %collective-permute-start.13 = (bf16[28,128,256]{2,1,0:T(8,128)(2,1)S(1)}, bf16[28,128,256]{2,1,0:T(8,128)(2,1)S(1)}, u32[]{:S(2)}, u32[]{:S(2)}) collective-permute-start(bf16[28,128,256]{2,1,0:T(8,128)(2,1)S(1)} %bitcast.14), channel_id=1, source_target_pairs={{0,1},{1,0},{2,3},{3,2},{4,5},{5,4},{6,7},{7,6},{8,9},{9,8},{10,11... | collective-permute-start | bytes 5505032 | tf_op jit(solution)/shard_map/ppermute | solution.py:441

commit v4 on v3

--- a/solution.py
+++ b/solution.py
@@ -17,6 +17,7 @@
 F32 = jnp.float32
 VMEM = pl.BlockSpec(memory_space=pltpu.VMEM)
 HBM = pl.BlockSpec(memory_space=pltpu.HBM)
+ANY = pl.BlockSpec(memory_space=pl.ANY)
 MIB = 1 << 20
 
 
@@ -150,8 +151,10 @@
 
 
 def late_frames_kernel(
-    field, low, high, left, right, kernel, cot, bias, activation, slopes, own, act, sems
+    field, low, high, left, right, source, cot, bias, activation, slopes, own, kernel, act, sems
 ):
+    load = pltpu.make_async_copy(source, kernel, sems.at[2])
+    load.start()
     put = placer(own)
 
     def put_own(t):
@@ -159,6 +162,7 @@
 
     for t in range(3):
         put_own(t)
+    load.wait()
     for t in range(2):
         act[t], slopes[t] = forward([(own, t + a) for a in range(3)], kernel, bias, cot[t + 2])
         if t == 0:
@@ -226,9 +230,12 @@
         out[i] = total[...]
 
 
-def backward_kernel(
-    field, low, high, left, right, remote, edges, kernel, latent_grad, taps
-):
+def backward_kernel(field, low, high, *refs):
+    kernel, latent_grad, taps, held, sems = refs[4], refs[5], refs[6], refs[7:11], refs[11]
+    copies = transfers(sems, *zip(refs[:4], held))
+    left, right, remote, edges = held
+    for copy in copies:
+        copy.wait()
     put = placer(taps)
 
     def put_own(t):
@@ -274,17 +281,36 @@
         copy.wait()
 
 
-def call(body, outs, n_in, scratch, sems, vmem=24, flops=0, specs=None, out_specs=None, moved=4 << 20, **kwargs):
-    return pl.pallas_call(
-        body,
+def call(
+    body,
+    outs,
+    n_in,
+    scratch,
+    sems,
+    vmem=24,
+    flops=0,
+    moved=4 << 20,
+    specs=None,
+    out_specs=None,
+    after=(),
+    **kwargs,
+):
+    specs = list(specs or [HBM] * n_in) + [ANY] * len(after)
+
+    def trimmed(*refs):
+        body(*refs[:n_in], *refs[n_in + len(after) :])
+
+    run = pl.pallas_call(
+        trimmed,
         out_shape=outs,
-        in_specs=specs or [HBM] * n_in,
+        in_specs=specs,
         out_specs=out_specs or jax.tree.map(lambda _: HBM, outs),
         scratch_shapes=[*scratch] + [pltpu.SemaphoreType.DMA((sems,))] * (sems > 0),
         compiler_params=pltpu.CompilerParams(vmem_limit_bytes=int(vmem * MIB)),
         cost_estimate=pl.CostEstimate(flops=flops, bytes_accessed=moved, transcendentals=0),
         **kwargs,
     )
+    return lambda *operands: run(*operands, *after)
 
 
 def shape(*dims, dtype=BF):
@@ -295,9 +321,23 @@
     return pltpu.VMEM(dims, dtype)
 
 
-def columns_of(*sources):
-    outs = (shape(4, 32, 256),) * 2
-    return call(columns_kernel, outs, 3, [], 0, vmem=6, moved=1 << 10, specs=[VMEM] * 3, out_specs=(VMEM, VMEM))(*sources)
+def columns_of(*sources, after=()):
+    return call(
+        columns_kernel,
+        (shape(4, 32, 256),) * 2,
+        3,
+        [],
+        0,
+        vmem=6,
+        moved=1 << 10,
+        specs=[VMEM] * 3,
+        out_specs=(VMEM, VMEM),
+        after=after,
+    )(*sources)
+
+
+def in_hbm(x):
+    return pltpu.with_memory_space_constraint(x, pltpu.HBM)
 
 
 def edges_of(frames, *parts):
@@ -361,17 +401,17 @@
     right = shift(first, WA, -1)
     edges = shift(edges_of(slice(2, 4), low, high, left, right), "ta", 1)
 
-    grouped, bias = kernel.reshape(3, 2304, 256), bias.reshape(1, 256)
-    activation, late, own = call(
+    grouped, bias = in_hbm(kernel.reshape(3, 2304, 256)), bias.reshape(1, 256)
+    activation, late, own, grouped = call(
         late_frames_kernel,
-        (shape(*block), shape(*pair), shape(3, 4, 18, 32, 256)),
+        (shape(*block), shape(*pair), shape(3, 4, 18, 32, 256), shape(*grouped.shape)),
         8,
         [buffer(*pair)],
-        2,
+        3,
         vmem=8,
         flops=conv_flops // 2,
-        specs=[VMEM] * 8,
-        out_specs=(HBM, VMEM, VMEM),
+        specs=[VMEM] * 5 + [HBM] + [VMEM] * 2,
+        out_specs=(HBM, VMEM, VMEM, VMEM),
     )(latent, low, high, left, right, grouped, cotangent, bias)
     activation, top, bottom, front, dpre, far = call(
         early_frames_kernel,
@@ -410,14 +450,13 @@
     z = 2 * lax.axis_index("wz") + lax.axis_index("hz")
     spot = [(p - core) % 4 for p in (lax.axis_index("hx"), lax.axis_index("ta"), z)]
     near = sum(w * ((p == 1) | (p == 2)) for w, p in zip((4, 2, 1), spot))
-    terms, remote = lax.optimization_barrier((terms, remote))
     pieces = exchange(terms.reshape(8, 448, 256), NEAR)
     low = shift(bottom, HA, 1)
     high = shift(top, HA, -1)
     pieces, low, high = lax.optimization_barrier((pieces, low, high))
     total = sum_pieces(pieces, near == 7)
-    first, last = columns_of(dpre, low, high)
-    total, first, last = lax.optimization_barrier((total, first, last))
+    first, last = columns_of(dpre, low, high, after=(total,))
+    total, remote = lax.optimization_barrier((total, remote))
     pieces = exchange(total, FAR)
     left = shift(last, WA, 1)
     right = shift(first, WA, -1)
@@ -430,13 +469,13 @@
         backward_kernel,
         shape(*block),
         8,
-        [buffer(*bordered)],
-        0,
-        vmem=16,
+        [buffer(*bordered)] + [buffer(*x.shape) for x in sources[3:7]],
+        4,
+        vmem=20,
         flops=conv_flops,
-        specs=[VMEM] * 8,
+        specs=[VMEM] * 3 + [HBM] * 4 + [VMEM],
         out_specs=VMEM,
-    )(*sources)
+    )(*sources[:3], *[in_hbm(x) for x in sources[3:7]], kernel)
     mine, latent_grad = lax.optimization_barrier((mine, latent_grad))
     other = lax.ppermute(mine, "wc", [(0, 1), (1, 0)])
     kernel_grad, bias_grad = finish(scale, 0, mine)

time: 140 us -> 137 us (0.979)
  waiting for transfers between devices: 44.1 us -> 35.6 us
  starting transfers between devices: 47.4 us -> 53.8 us
  local copies, waits for them, and re-layouts: 9.53 us -> 4.76 us
  Pallas kernels: 36.6 us -> 40.4 us
    ppermute x12, waiting for transfers between devices: 32.4 us -> 25.5 us  [shift(): return lax.ppermute(block, axis, route)]
    unnamed x18, local copies, waits for them, and re-layouts: 9.5 us -> 4.73 us
    all_to_all x3, starting transfers between devices: 14.5 us -> 19 us  [exchange(): return lax.all_to_all(pieces, AXES, 0, 0, axis_index_groups=groups)]
    pallas_call x13, Pallas kernels: 36.6 us -> 40.4 us  [call(): return lambda *operands: run(*operands, *after)]
    ppermute x12, starting transfers between devices: 32.8 us -> 34.6 us  [shift(): return lax.ppermute(block, axis, route)]
    all_to_all x3, waiting for transfers between devices: 10.4 us -> 8.78 us  [exchange(): return lax.all_to_all(pieces, AXES, 0, 0, axis_index_groups=groups)]
  transfers between devices with their start and end apart: 17 -> 17, of which waited for: 11 -> 11; matrix products, arithmetic and copies ran while one was open for 0% -> 0% of each run, Pallas kernels for 17% -> 20%
where the time goes in v4:
time: 137 us; the launch traced here: 136 us
  starting transfers between devices  53.8 us (39%)
  Pallas kernels  40.4 us (29%)
  waiting for transfers between devices  35.6 us (26%)
  local copies, waits for them, and re-layouts  4.76 us (3%)
    pallas_call x13, Pallas kernels, call(): return lambda *operands: run(*operands, *after)  40.4 us
    ppermute x12, starting transfers between devices, shift(): return lax.ppermute(block, axis, route)  34.6 us
    ppermute x12, waiting for transfers between devices, shift(): return lax.ppermute(block, axis, route)  25.5 us
    all_to_all x3, starting transfers between devices, exchange(): return lax.all_to_all(pieces, AXES, 0, 0, axis_index_groups=groups)  19 us
    all_to_all x3, waiting for transfers between devices, exchange(): return lax.all_to_all(pieces, AXES, 0, 0, axis_index_groups=groups)  8.78 us
    unnamed x18, local copies, waits for them, and re-layouts  4.73 us
  transfers between devices with their start and end apart: 17, of which 11 were waited for; matrix products, arithmetic and copies ran while one was open for 0% of the time, Pallas kernels for 20%

profile of v4, /device:TPU:1, one launch (start us, length us, event | category | flops | bytes accessed | tf_op | source)
XLA Modules:
  0.0 135.9 jit_solution(12064892717076895275)
XLA Ops:
  0.6 0.0 copy-start.1
  0.6 1.2 copy-done.1
  1.9 0.0 copy-start.3
  1.9 0.0 copy-start.5
  1.9 0.1 shard_map.75
  2.0 4.1 %collective-permute-start.1 = (bf16[4,1,32,256]{3,2,1,0:T(8,128)(2,1)S(1)}, bf16[4,1,32,256]{3,2,1,0:T(8,128)(2,1)S(1)}, u32[]{:S(2)}, u32[]{:S(2)}) collective-permute-start(bf16[4,1,32,256]{3,2,1,0:T(8,128)(2,1)S(1)} %get-tuple-element.33), channel_id=1, source_target_pairs={{0,4},{4,8},{8,12},{12,16},{16,20},{20,24},{24,28},{1,5},{5,9},{9,... | collective-permute-start | bytes 196616 | tf_op jit(solution)/shard_map/ppermute | solution.py:54
  6.1 1.3 collective-permute-start.2
  7.4 0.0 collective-permute-done.1.refs_1_
  7.4 3.7 %collective-permute-done.2.refs_2_ = bf16[4,1,32,256]{3,2,1,0:T(8,128)(2,1)S(1)} collective-permute-done((bf16[4,1,32,256]{3,2,1,0:T(8,128)(2,1)S(1)}, bf16[4,1,32,256]{3,2,1,0:T(8,128)(2,1)S(1)}, u32[]{:S(2)}, u32[]{:S(2)}) %collective-permute-start.2) | collective-permute-done | bytes 65568 | tf_op jit(solution)/shard_map/ppermute | solution.py:54
  11.1 0.3 shard_map.76
  11.4 7.5 %collective-permute-start.3 = (bf16[4,32,256]{2,1,0:T(8,128)(2,1)S(1)}, bf16[4,32,256]{2,1,0:T(8,128)(2,1)S(1)}, u32[]{:S(2)}, u32[]{:S(2)}) collective-permute-start(bf16[4,32,256]{2,1,0:T(8,128)(2,1)S(1)} %get-tuple-element.35), channel_id=1, source_target_pairs={{0,1},{1,2},{2,3},{4,5},{5,6},{6,7},{8,9},{9,10},{10,11},{12,13},{... | collective-permute-start | bytes 196616 | tf_op jit(solution)/shard_map/ppermute | solution.py:54
  18.9 3.2 %collective-permute-start = (bf16[2,16,32,256]{3,2,1,0:T(8,128)(2,1)S(1)}, bf16[2,16,32,256]{3,2,1,0:T(8,128)(2,1)S(1)}, u32[]{:S(2)}, u32[]{:S(2)}) collective-permute-start(bf16[2,16,32,256]{3,2,1,0:T(8,128)(2,1)S(1)} %get-tuple-element.32), channel_id=1, source_target_pairs={{0,32},{32,64},{64,96},{1,33},{33,65},{65,97},{2,34},{34,66},{66,9... | collective-permute-start | bytes 1572872 | tf_op jit(solution)/shard_map/ppermute | solution.py:54
  22.2 1.9 %collective-permute-start.4 = (bf16[4,32,256]{2,1,0:T(8,128)(2,1)S(1)}, bf16[4,32,256]{2,1,0:T(8,128)(2,1)S(1)}, u32[]{:S(2)}, u32[]{:S(2)}) collective-permute-start(bf16[4,32,256]{2,1,0:T(8,128)(2,1)S(1)} %get-tuple-element.36), channel_id=1, source_target_pairs={{1,0},{2,1},{3,2},{5,4},{6,5},{7,6},{9,8},{10,9},{11,10},{13,12},{... | collective-permute-start | bytes 196616 | tf_op jit(solution)/shard_map/ppermute | solution.py:54
  24.1 0.0 collective-permute-done.3.refs_3_
  24.1 5.1 %collective-permute-done.4.refs_4_ = bf16[4,32,256]{2,1,0:T(8,128)(2,1)S(1)} collective-permute-done((bf16[4,32,256]{2,1,0:T(8,128)(2,1)S(1)}, bf16[4,32,256]{2,1,0:T(8,128)(2,1)S(1)}, u32[]{:S(2)}, u32[]{:S(2)}) %collective-permute-start.4) | collective-permute-done | bytes 65568 | tf_op jit(solution)/shard_map/ppermute | solution.py:54
  29.3 3.2 %collective-permute-start.5 = (bf16[2,4,32,256]{3,2,1,0:T(8,128)(2,1)S(1)}, bf16[2,4,32,256]{3,2,1,0:T(8,128)(2,1)S(1)}, u32[]{:S(2)}, u32[]{:S(2)}) collective-permute-start(bf16[2,4,32,256]{3,2,1,0:T(8,128)(2,1)S(1)} %pad_maximum_fusion), channel_id=1, source_target_pairs={{0,32},{32,64},{64,96},{1,33},{33,65},{65,97},{2,34},{34,66},{66,9... | collective-permute-start | bytes 393224 | tf_op jit(solution)/shard_map/ppermute | solution.py:54
  32.5 0.0 copy-done.3
  32.5 0.0 copy-done.5
  32.5 6.9 %shard_map.77 = (bf16[4,16,32,256]{3,2,1,0:T(8,128)(2,1)}, bf16[2,16,32,256]{3,2,1,0:T(8,128)(2,1)S(1)}, bf16[3,4,18,32,256]{4,3,2,1,0:T(8,128)(2,1)S(1)}, bf16[3,2304,256]{2,1,0:T(8,128)(2,1)S(1)}) custom-call(bf16[4,16,32,256]{3,2,1,0:T(8,128)(2,1)S(1)} %copy-done.1, bf16[4,1,32,256]{3,2,1,0:T(8,128)(2,1)S(1)} %collective-permute-done.1.refs_1_, ...), custom_call_target="tpu_custom_call" | custom-call | flops 3623878656 | bytes 4194304 | tf_op jit(solution)/shard_map/pallas_call | solution.py:313
  39.4 0.0 collective-permute-done.5.refs_1_
  39.4 0.0 collective-permute-done.refs_0_
  39.4 5.3 %shard_map.78 = (bf16[4,16,32,256]{3,2,1,0:T(8,128)(2,1)}, bf16[4,1,32,256]{3,2,1,0:T(8,128)(2,1)S(1)}, bf16[4,1,32,256]{3,2,1,0:T(8,128)(2,1)}, bf16[2,16,32,25...) custom-call(bf16[2,16,32,256]{3,2,1,0:T(8,128)(2,1)S(1)} %collective, ...), custom_call_target="tpu_custom_call", output_to_operand_aliasing={{0}: (7, {})} | custom-call | flops 3623878656 | bytes 4194304 | tf_op jit(solution)/shard_map/pallas_call | solution.py:313
  44.7 0.0 copy-start.4
  44.7 3.9 %shard_map.80 = bf16[28,128,256]{2,1,0:T(8,128)(2,1)S(1)} custom-call(bf16[3,2,18,32,256]{4,3,2,1,0:T(8,128)(2,1)S(1)} %get-tuple-element.42.refs_0_, bf16[3,4,18,32,256]{4,3,2,1,0:T(8,128)(2,1)S(1)} %get-tuple-element.37.refs_2_.refs_1_, bf16[4,16,32,256]{3,2,1,0:T(8,128)(2,1)S(1)} %get-tuple-element.43.refs_2_.refs_0_), custom_call_target="tpu_custom_call" | custom-call | bytes 1024 | tf_op jit(solution)/shard_map/pallas_call | solution.py:313
  48.6 0.0 copy-done.4
  48.6 0.3 collective-permute-start.6
  48.9 3.9 %shard_map.79.refs_0_ = f32[28,128,256]{2,1,0:T(8,128)S(1)} custom-call(bf16[3,2,18,32,256]{4,3,2,1,0:T(8,128)(2,1)S(1)} %get-tuple-element.42.refs_0_, bf16[3,4,18,32,256]{4,3,2,1,0:T(8,128)(2,1)S(1)} %get-tuple-element.37.refs_2_.refs_1_, bf16[4,16,32,256]{3,2,1,0:T(8,128)(2,1)S(1)} %get-tuple-element.43.refs_2_.refs_0_), custom_call_target="tpu_custom_call" | custom-call | bytes 1024 | tf_op jit(solution)/shard_map/pallas_call | solution.py:313
  52.8 0.0 collective-permute-done.6.refs_1_
  52.8 1.5 %shard_map.81 = bf16[28,128,256]{2,1,0:T(8,128)(2,1)} custom-call(f32[28,128,256]{2,1,0:T(8,128)S(1)} %shard_map.79.refs_0_, bf16[28,128,256]{2,1,0:T(8,128)(2,1)S(1)} %collective-permute-done.6.refs_1_), custom_call_target="tpu_custom_call" | custom-call | bytes 1024 | tf_op jit(solution)/shard_map/pallas_call | solution.py:313
  54.4 5.9 %all-to-all-start = ((bf16[8,448,256]{2,1,0:T(8,128)(2,1)}), bf16[8,448,256]{2,1,0:T(8,128)(2,1)S(1)}, u32[]{:S(2)}, u32[]{:S(2)}) async-start(bf16[8,448,256]{2,1,0:T(8,128)(2,1)} %bitcast.4), calls=%async_computation | async-start | bytes 3670016 | tf_op jit(solution)/shard_map/all_to_all | solution.py:45
  60.3 1.3 collective-permute-start.9
  61.6 1.3 collective-permute-start.7
  62.9 1.3 collective-permute-start.8
  64.2 0.9 collective-permute-done.7.refs_1_
  65.1 4.0 %collective-permute-done.8.refs_2_ = bf16[4,1,32,256]{3,2,1,0:T(8,128)(2,1)S(1)} collective-permute-done((bf16[4,1,32,256]{3,2,1,0:T(8,128)(2,1)}, bf16[4,1,32,256]{3,2,1,0:T(8,128)(2,1)S(1)}, u32[]{:S(2)}, u32[]{:S(2)}) %collective-permute-start.8) | collective-permute-done | bytes 65568 | tf_op jit(solution)/shard_map/ppermute | solution.py:54
  69.1 6.9 %all-to-all-done.refs_0_ = bf16[8,448,256]{2,1,0:T(8,128)(2,1)S(1)} async-done(((bf16[8,448,256]{2,1,0:T(8,128)(2,1)}), bf16[8,448,256]{2,1,0:T(8,128)(2,1)S(1)}, u32[]{:S(2)}, u32[]{:S(2)}) %all-to-all-start) | async-done | bytes 1835040 | tf_op jit(solution)/shard_map/all_to_all | solution.py:45
  76.0 1.6 %shard_map.82.refs_3_ = bf16[8,448,256]{2,1,0:T(8,128)(2,1)} custom-call(bf16[8,448,256]{2,1,0:T(8,128)(2,1)S(1)} %all-to-all-done.refs_0_, s32[1]{0:T(128)} %bitcast.5.refs_1_), custom_call_target="tpu_custom_call" | custom-call | bytes 4194304 | tf_op jit(solution)/shard_map/pallas_call | solution.py:313
  77.6 1.9 %collective-permute-done.9.refs_5_ = bf16[2,16,32,256]{3,2,1,0:T(8,128)(2,1)} collective-permute-done((bf16[2,16,32,256]{3,2,1,0:T(8,128)(2,1)S(1)}, bf16[2,16,32,256]{3,2,1,0:T(8,128)(2,1)}, u32[]{:S(2)}, u32[]{:S(2)}) %collective-permute-start.9) | collective-permute-done | bytes 524320 | tf_op jit(solution)/shard_map/ppermute | solution.py:54
  79.5 8.9 %all-to-all-start.1 = ((bf16[8,448,256]{2,1,0:T(8,128)(2,1)}), bf16[8,448,256]{2,1,0:T(8,128)(2,1)S(1)}, u32[]{:S(2)}, u32[]{:S(2)}) async-start(bf16[8,448,256]{2,1,0:T(8,128)(2,1)} %shard_map.82.refs_3_), calls=%async_computation.1 | async-start | bytes 3670016 | tf_op jit(solution)/shard_map/all_to_all | solution.py:45
  88.5 0.3 shard_map.83
  88.8 6.3 %collective-permute-start.10 = (bf16[4,32,256]{2,1,0:T(8,128)(2,1)S(1)}, bf16[4,32,256]{2,1,0:T(8,128)(2,1)S(1)}, u32[]{:S(2)}, u32[]{:S(2)}) collective-permute-start(bf16[4,32,256]{2,1,0:T(8,128)(2,1)S(1)} %get-tuple-element.51), channel_id=1, source_target_pairs={{0,1},{1,2},{2,3},{4,5},{5,6},{6,7},{8,9},{9,10},{10,11},{12,13},{... | collective-permute-start | bytes 196616 | tf_op jit(solution)/shard_map/ppermute | solution.py:54
  95.2 1.9 %collective-permute-start.11 = (bf16[4,32,256]{2,1,0:T(8,128)(2,1)S(1)}, bf16[4,32,256]{2,1,0:T(8,128)(2,1)S(1)}, u32[]{:S(2)}, u32[]{:S(2)}) collective-permute-start(bf16[4,32,256]{2,1,0:T(8,128)(2,1)S(1)} %get-tuple-element.52), channel_id=1, source_target_pairs={{1,0},{2,1},{3,2},{5,4},{6,5},{7,6},{9,8},{10,9},{11,10},{13,12},{... | collective-permute-start | bytes 196616 | tf_op jit(solution)/shard_map/ppermute | solution.py:54
  97.1 2.6 %collective-permute-done.10.refs_3_ = bf16[4,32,256]{2,1,0:T(8,128)(2,1)S(1)} collective-permute-done((bf16[4,32,256]{2,1,0:T(8,128)(2,1)S(1)}, bf16[4,32,256]{2,1,0:T(8,128)(2,1)S(1)}, u32[]{:S(2)}, u32[]{:S(2)}) %collective-permute-start.10) | collective-permute-done | bytes 65568 | tf_op jit(solution)/shard_map/ppermute | solution.py:54
  99.7 0.0 copy-start.6
  99.7 2.8 %collective-permute-done.11.refs_4_ = bf16[4,32,256]{2,1,0:T(8,128)(2,1)S(1)} collective-permute-done((bf16[4,32,256]{2,1,0:T(8,128)(2,1)S(1)}, bf16[4,32,256]{2,1,0:T(8,128)(2,1)S(1)}, u32[]{:S(2)}, u32[]{:S(2)}) %collective-permute-start.11) | collective-permute-done | bytes 65568 | tf_op jit(solution)/shard_map/ppermute | solution.py:54
  102.5 0.0 copy-start.7
  102.6 1.3 collective-permute-start.12
  103.9 4.4 %collective-permute-done.12.refs_6_ = bf16[2,4,32,256]{3,2,1,0:T(8,128)(2,1)S(1)} collective-permute-done((bf16[2,4,32,256]{3,2,1,0:T(8,128)(2,1)S(1)}, bf16[2,4,32,256]{3,2,1,0:T(8,128)(2,1)S(1)}, u32[]{:S(2)}, u32[]{:S(2)}) %collective-permute-start.12) | collective-permute-done | bytes 131104 | tf_op jit(solution)/shard_map/ppermute | solution.py:54
  108.3 0.0 copy-start.8
  108.3 0.0 all-to-all-done.1.refs_0_
  108.3 0.4 shard_map.84
  108.6 0.0 copy-done.6
  108.7 0.0 copy-done.7
  108.7 0.3 copy-done.8
  108.9 0.0 copy-start
  108.9 1.2 copy-done
  110.2 4.1 %all-to-all-start.2 = ((bf16[8,448,256]{2,1,0:T(8,128)(2,1)}), bf16[8,448,256]{2,1,0:T(8,128)(2,1)S(1)}, u32[]{:S(2)}, u32[]{:S(2)}) async-start(bf16[8,448,256]{2,1,0:T(8,128)(2,1)} %copy-done), calls=%async_computation.2 | async-start | bytes 3670016 | tf_op jit(solution)/shard_map/all_to_all | solution.py:45
  114.3 2.0 %copy-done.2 = bf16[27,256,256]{2,1,0:T(8,128)(2,1)S(1)} copy-done((bf16[27,256,256]{2,1,0:T(8,128)(2,1)S(1)}, bf16[27,256,256]{2,1,0:T(8,128)(2,1)}, u32[]{:S(2)}) %copy-start.2) | copy-done | bytes 3538968
  116.3 11.9 %shard_map.85 = bf16[4,16,32,256]{3,2,1,0:T(8,128)(2,1)} custom-call(bf16[4,16,32,256]{3,2,1,0:T(8,128)(2,1)S(1)} %get-tuple-element.43.refs_2_.refs_0_, bf16[4,1,32,256]{3,2,1,0:T(8,128)(2,1)S(1)} %collective-permute-done.7.refs_1_, bf16[4,1,32,256]{3,2,1,0:T(8,128)(2,1)S(1)} %collective-permute-done.8.refs_2_, bf16[4,32,256]{2,1,0:T(8,128)(2,1)} %copy-done.6, ...), custom_call_target="tpu_custom_call" | custom-call | flops 7247757312 | bytes 4194304 | tf_op jit(solution)/shard_map/pallas_call | solution.py:313
  128.2 1.9 %all-to-all-done.2 = bf16[8,448,256]{2,1,0:T(8,128)(2,1)S(1)} async-done(((bf16[8,448,256]{2,1,0:T(8,128)(2,1)}), bf16[8,448,256]{2,1,0:T(8,128)(2,1)S(1)}, u32[]{:S(2)}, u32[]{:S(2)}) %all-to-all-start.2) | async-done | bytes 1835040 | tf_op jit(solution)/shard_map/all_to_all | solution.py:45
  130.0 0.0 collective-permute-start.13
  130.0 2.4 %shard_map.86 = (f32[27,256,256]{2,1,0:T(8,128)}, f32[1,256]{1,0:T(1,128)}) custom-call(bf16[28,128,256]{2,1,0:T(8,128)(2,1)S(1)} %bitcast.15), custom_call_target="tpu_custom_call" | custom-call | bytes 4194304 | tf_op jit(solution)/shard_map/pallas_call | solution.py:313
  132.5 1.3 collective-permute-done.13.refs_0_
  133.8 1.9 %shard_map.87 = f32[27,256,256]{2,1,0:T(8,128)} custom-call(bf16[28,128,256]{2,1,0:T(8,128)(2,1)S(1)} %collective-permute-done.13.refs_0_, f32[27,256,256]{2,1,0:T(8,128)} %get-tuple-element.58.refs_1_), custom_call_target="tpu_custom_call", output_to_operand_aliasing={{}: (1, {})} | custom-call | bytes 4194304 | tf_op jit(solution)/shard_map/pallas_call | solution.py:313
  (11 shorter events, 0.1 us)
Async XLA Ops:
  0.6 1.2 copy-start.1
  1.9 30.6 %copy-start.3 = (bf16[4,16,32,256]{3,2,1,0:T(8,128)(2,1)S(1)}, bf16[4,16,32,256]{3,2,1,0:T(8,128)(2,1)}, u32[]{:S(2)}) copy-start(bf16[4,16,32,256]{3,2,1,0:T(8,128)(2,1)} %refs_5_.1) | copy-start | bytes 3145732
  1.9 30.6 %copy-start.5 = (f32[256]{0:T(256)S(1)}, f32[256]{0:T(256)}, u32[]{:S(2)}) copy-start(f32[256]{0:T(256)} %param.6) | copy-start | bytes 3076
  2.0 5.4 %collective-permute-start.1 = (bf16[4,1,32,256]{3,2,1,0:T(8,128)(2,1)S(1)}, bf16[4,1,32,256]{3,2,1,0:T(8,128)(2,1)S(1)}, u32[]{:S(2)}, u32[]{:S(2)}) collective-permute-start(bf16[4,1,32,256]{3,2,1,0:T(8,128)(2,1)S(1)} %get-tuple-element.33), channel_id=1, source_target_pairs={{0,4},{4,8},{8,12},{12,16},{16,20},{20,24},{24,28},{1,5},{5,9},{9,... | collective-permute-start | bytes 196616 | tf_op jit(solution)/shard_map/ppermute | solution.py:54
  6.1 5.0 %collective-permute-start.2 = (bf16[4,1,32,256]{3,2,1,0:T(8,128)(2,1)S(1)}, bf16[4,1,32,256]{3,2,1,0:T(8,128)(2,1)S(1)}, u32[]{:S(2)}, u32[]{:S(2)}) collective-permute-start(bf16[4,1,32,256]{3,2,1,0:T(8,128)(2,1)S(1)} %get-tuple-element.34), channel_id=1, source_target_pairs={{4,0},{8,4},{12,8},{16,12},{20,16},{24,20},{28,24},{5,1},{9,5},{13... | collective-permute-start | bytes 196616 | tf_op jit(solution)/shard_map/ppermute | solution.py:54
  11.4 12.7 %collective-permute-start.3 = (bf16[4,32,256]{2,1,0:T(8,128)(2,1)S(1)}, bf16[4,32,256]{2,1,0:T(8,128)(2,1)S(1)}, u32[]{:S(2)}, u32[]{:S(2)}) collective-permute-start(bf16[4,32,256]{2,1,0:T(8,128)(2,1)S(1)} %get-tuple-element.35), channel_id=1, source_target_pairs={{0,1},{1,2},{2,3},{4,5},{5,6},{6,7},{8,9},{9,10},{10,11},{12,13},{... | collective-permute-start | bytes 196616 | tf_op jit(solution)/shard_map/ppermute | solution.py:54
  18.9 20.5 %collective-permute-start = (bf16[2,16,32,256]{3,2,1,0:T(8,128)(2,1)S(1)}, bf16[2,16,32,256]{3,2,1,0:T(8,128)(2,1)S(1)}, u32[]{:S(2)}, u32[]{:S(2)}) collective-permute-start(bf16[2,16,32,256]{3,2,1,0:T(8,128)(2,1)S(1)} %get-tuple-element.32), channel_id=1, source_target_pairs={{0,32},{32,64},{64,96},{1,33},{33,65},{65,97},{2,34},{34,66},{66,9... | collective-permute-start | bytes 1572872 | tf_op jit(solution)/shard_map/ppermute | solution.py:54
  22.2 7.1 %collective-permute-start.4 = (bf16[4,32,256]{2,1,0:T(8,128)(2,1)S(1)}, bf16[4,32,256]{2,1,0:T(8,128)(2,1)S(1)}, u32[]{:S(2)}, u32[]{:S(2)}) collective-permute-start(bf16[4,32,256]{2,1,0:T(8,128)(2,1)S(1)} %get-tuple-element.36), channel_id=1, source_target_pairs={{1,0},{2,1},{3,2},{5,4},{6,5},{7,6},{9,8},{10,9},{11,10},{13,12},{... | collective-permute-start | bytes 196616 | tf_op jit(solution)/shard_map/ppermute | solution.py:54
  29.3 10.1 %collective-permute-start.5 = (bf16[2,4,32,256]{3,2,1,0:T(8,128)(2,1)S(1)}, bf16[2,4,32,256]{3,2,1,0:T(8,128)(2,1)S(1)}, u32[]{:S(2)}, u32[]{:S(2)}) collective-permute-start(bf16[2,4,32,256]{3,2,1,0:T(8,128)(2,1)S(1)} %pad_maximum_fusion), channel_id=1, source_target_pairs={{0,32},{32,64},{64,96},{1,33},{33,65},{65,97},{2,34},{34,66},{66,9... | collective-permute-start | bytes 393224 | tf_op jit(solution)/shard_map/ppermute | solution.py:54
  44.7 3.9 %copy-start.4 = (bf16[4,1,32,256]{3,2,1,0:T(8,128)(2,1)}, bf16[4,1,32,256]{3,2,1,0:T(8,128)(2,1)S(1)}, u32[]{:S(2)}) copy-start(bf16[4,1,32,256]{3,2,1,0:T(8,128)(2,1)S(1)} %get-tuple-element.45) | copy-start | bytes 196612
  48.6 4.2 %collective-permute-start.6 = (bf16[28,128,256]{2,1,0:T(8,128)(2,1)S(1)}, bf16[28,128,256]{2,1,0:T(8,128)(2,1)S(1)}, u32[]{:S(2)}, u32[]{:S(2)}) collective-permute-start(bf16[28,128,256]{2,1,0:T(8,128)(2,1)S(1)} %shard_map.80), channel_id=1, source_target_pairs={{0,1},{1,0},{2,3},{3,2},{4,5},{5,4},{6,7},{7,6},{8,9},{9,8},{10,11... | collective-permute-start | bytes 5505032 | tf_op jit(solution)/shard_map/ppermute | solution.py:443
  54.4 21.7 %all-to-all-start = ((bf16[8,448,256]{2,1,0:T(8,128)(2,1)}), bf16[8,448,256]{2,1,0:T(8,128)(2,1)S(1)}, u32[]{:S(2)}, u32[]{:S(2)}) async-start(bf16[8,448,256]{2,1,0:T(8,128)(2,1)} %bitcast.4), calls=%async_computation | async-start | bytes 3670016 | tf_op jit(solution)/shard_map/all_to_all | solution.py:45
  60.3 19.2 %collective-permute-start.9 = (bf16[2,16,32,256]{3,2,1,0:T(8,128)(2,1)S(1)}, bf16[2,16,32,256]{3,2,1,0:T(8,128)(2,1)}, u32[]{:S(2)}, u32[]{:S(2)}) collective-permute-start(bf16[2,16,32,256]{3,2,1,0:T(8,128)(2,1)S(1)} %get-tuple-element.47), channel_id=1, source_target_pairs={{32,0},{64,32},{96,64},{33,1},{65,33},{97,65},{34,2},{66,34},{98,6... | collective-permute-start | bytes 1572872 | tf_op jit(solution)/shard_map/ppermute | solution.py:54
  61.6 3.6 %collective-permute-start.7 = (bf16[4,1,32,256]{3,2,1,0:T(8,128)(2,1)}, bf16[4,1,32,256]{3,2,1,0:T(8,128)(2,1)S(1)}, u32[]{:S(2)}, u32[]{:S(2)}) collective-permute-start(bf16[4,1,32,256]{3,2,1,0:T(8,128)(2,1)} %get-tuple-element.44), channel_id=1, source_target_pairs={{0,4},{4,8},{8,12},{12,16},{16,20},{20,24},{24,28},{1,5},{5,9},{9,... | collective-permute-start | bytes 196616 | tf_op jit(solution)/shard_map/ppermute | solution.py:54
  62.9 6.3 %collective-permute-start.8 = (bf16[4,1,32,256]{3,2,1,0:T(8,128)(2,1)}, bf16[4,1,32,256]{3,2,1,0:T(8,128)(2,1)S(1)}, u32[]{:S(2)}, u32[]{:S(2)}) collective-permute-start(bf16[4,1,32,256]{3,2,1,0:T(8,128)(2,1)} %copy-done.4), channel_id=1, source_target_pairs={{4,0},{8,4},{12,8},{16,12},{20,16},{24,20},{28,24},{5,1},{9,5},{13... | collective-permute-start | bytes 196616 | tf_op jit(solution)/shard_map/ppermute | solution.py:54
  79.5 28.8 %all-to-all-start.1 = ((bf16[8,448,256]{2,1,0:T(8,128)(2,1)}), bf16[8,448,256]{2,1,0:T(8,128)(2,1)S(1)}, u32[]{:S(2)}, u32[]{:S(2)}) async-start(bf16[8,448,256]{2,1,0:T(8,128)(2,1)} %shard_map.82.refs_3_), calls=%async_computation.1 | async-start | bytes 3670016 | tf_op jit(solution)/shard_map/all_to_all | solution.py:45
  88.8 10.9 %collective-permute-start.10 = (bf16[4,32,256]{2,1,0:T(8,128)(2,1)S(1)}, bf16[4,32,256]{2,1,0:T(8,128)(2,1)S(1)}, u32[]{:S(2)}, u32[]{:S(2)}) collective-permute-start(bf16[4,32,256]{2,1,0:T(8,128)(2,1)S(1)} %get-tuple-element.51), channel_id=1, source_target_pairs={{0,1},{1,2},{2,3},{4,5},{5,6},{6,7},{8,9},{9,10},{10,11},{12,13},{... | collective-permute-start | bytes 196616 | tf_op jit(solution)/shard_map/ppermute | solution.py:54
  95.2 7.4 %collective-permute-start.11 = (bf16[4,32,256]{2,1,0:T(8,128)(2,1)S(1)}, bf16[4,32,256]{2,1,0:T(8,128)(2,1)S(1)}, u32[]{:S(2)}, u32[]{:S(2)}) collective-permute-start(bf16[4,32,256]{2,1,0:T(8,128)(2,1)S(1)} %get-tuple-element.52), channel_id=1, source_target_pairs={{1,0},{2,1},{3,2},{5,4},{6,5},{7,6},{9,8},{10,9},{11,10},{13,12},{... | collective-permute-start | bytes 196616 | tf_op jit(solution)/shard_map/ppermute | solution.py:54
  99.7 8.9 %copy-start.6 = (bf16[4,32,256]{2,1,0:T(8,128)(2,1)}, bf16[4,32,256]{2,1,0:T(8,128)(2,1)S(1)}, u32[]{:S(2)}) copy-start(bf16[4,32,256]{2,1,0:T(8,128)(2,1)S(1)} %collective-permute-done.10.refs_3_) | copy-start | bytes 196612
  102.5 6.1 %copy-start.7 = (bf16[4,32,256]{2,1,0:T(8,128)(2,1)}, bf16[4,32,256]{2,1,0:T(8,128)(2,1)S(1)}, u32[]{:S(2)}) copy-start(bf16[4,32,256]{2,1,0:T(8,128)(2,1)S(1)} %collective-permute-done.11.refs_4_) | copy-start | bytes 196612
  102.6 5.7 %collective-permute-start.12 = (bf16[2,4,32,256]{3,2,1,0:T(8,128)(2,1)S(1)}, bf16[2,4,32,256]{3,2,1,0:T(8,128)(2,1)S(1)}, u32[]{:S(2)}, u32[]{:S(2)}) collective-permute-start(bf16[2,4,32,256]{3,2,1,0:T(8,128)(2,1)S(1)} %pad_maximum_fusion.1), channel_id=1, source_target_pairs={{32,0},{64,32},{96,64},{33,1},{65,33},{97,65},{34,2},{66,34},{98,6... | collective-permute-start | bytes 393224 | tf_op jit(solution)/shard_map/ppermute | solution.py:54
  108.3 0.7 copy-start.8
  108.9 1.2 copy-start
  110.2 19.9 %all-to-all-start.2 = ((bf16[8,448,256]{2,1,0:T(8,128)(2,1)}), bf16[8,448,256]{2,1,0:T(8,128)(2,1)S(1)}, u32[]{:S(2)}, u32[]{:S(2)}) async-start(bf16[8,448,256]{2,1,0:T(8,128)(2,1)} %copy-done), calls=%async_computation.2 | async-start | bytes 3670016 | tf_op jit(solution)/shard_map/all_to_all | solution.py:45
  114.3 2.0 %copy-start.2 = (bf16[27,256,256]{2,1,0:T(8,128)(2,1)S(1)}, bf16[27,256,256]{2,1,0:T(8,128)(2,1)}, u32[]{:S(2)}) copy-start(bf16[27,256,256]{2,1,0:T(8,128)(2,1)} %refs_7_.1) | copy-start | bytes 10616836
  130.0 3.8 %collective-permute-start.13 = (bf16[28,128,256]{2,1,0:T(8,128)(2,1)S(1)}, bf16[28,128,256]{2,1,0:T(8,128)(2,1)S(1)}, u32[]{:S(2)}, u32[]{:S(2)}) collective-permute-start(bf16[28,128,256]{2,1,0:T(8,128)(2,1)S(1)} %bitcast.14), channel_id=1, source_target_pairs={{0,1},{1,0},{2,3},{3,2},{4,5},{5,4},{6,7},{7,6},{8,9},{9,8},{10,11... | collective-permute-start | bytes 5505032 | tf_op jit(solution)/shard_map/ppermute | solution.py:480

commit v5 on v4

--- a/solution.py
+++ b/solution.py
@@ -150,11 +150,15 @@
     return (total * sig).astype(BF).reshape(field), slope.astype(BF).reshape(field)
 
 
+def load_kernel(source, held, sems):
+    copy = pltpu.make_async_copy(source, held, sems.at[0])
+    copy.start()
+    copy.wait()
+
+
 def late_frames_kernel(
-    field, low, high, left, right, source, cot, bias, activation, slopes, own, kernel, act, sems
+    field, low, high, left, right, kernel, cot, bias, activation, slopes, own, act, sems
 ):
-    load = pltpu.make_async_copy(source, kernel, sems.at[2])
-    load.start()
     put = placer(own)
 
     def put_own(t):
@@ -162,7 +166,6 @@
 
     for t in range(3):
         put_own(t)
-    load.wait()
     for t in range(2):
         act[t], slopes[t] = forward([(own, t + a) for a in range(3)], kernel, bias, cot[t + 2])
         if t == 0:
@@ -402,16 +405,19 @@
     edges = shift(edges_of(slice(2, 4), low, high, left, right), "ta", 1)
 
     grouped, bias = in_hbm(kernel.reshape(3, 2304, 256)), bias.reshape(1, 256)
-    activation, late, own, grouped = call(
+    grouped = call(
+        load_kernel, shape(*grouped.shape), 1, [], 1, vmem=4, flops=conv_flops // 4, out_specs=VMEM
+    )(grouped)
+    activation, late, own = call(
         late_frames_kernel,
-        (shape(*block), shape(*pair), shape(3, 4, 18, 32, 256), shape(*grouped.shape)),
+        (shape(*block), shape(*pair), shape(3, 4, 18, 32, 256)),
         8,
         [buffer(*pair)],
-        3,
+        2,
         vmem=8,
         flops=conv_flops // 2,
-        specs=[VMEM] * 5 + [HBM] + [VMEM] * 2,
-        out_specs=(HBM, VMEM, VMEM, VMEM),
+        specs=[VMEM] * 8,
+        out_specs=(HBM, VMEM, VMEM),
     )(latent, low, high, left, right, grouped, cotangent, bias)
     activation, top, bottom, front, dpre, far = call(
         early_frames_kernel,

time: 137 us -> 134 us (0.978)
  waiting for transfers between devices: 35.6 us -> 32.8 us
    ppermute x12, waiting for transfers between devices: 25.5 us -> 22.4 us  [shift(): return lax.ppermute(block, axis, route)]
    pallas_call x13 -> x14, Pallas kernels: 40.4 us -> 41.1 us  [call(): return lambda *operands: run(*operands, *after)]
  transfers between devices with their start and end apart: 17 -> 17, of which waited for: 11 -> 11; matrix products, arithmetic and copies ran while one was open for 0% -> 0% of each run, Pallas kernels for 20% -> 21%
where the time goes in v5:
time: 134 us
  starting transfers between devices  53.8 us (40%)
  Pallas kernels  41.1 us (31%)
  waiting for transfers between devices  32.8 us (24%)
  local copies, waits for them, and re-layouts  4.77 us (4%)
    pallas_call x14, Pallas kernels, call(): return lambda *operands: run(*operands, *after)  41.1 us
    ppermute x12, starting transfers between devices, shift(): return lax.ppermute(block, axis, route)  34 us
    ppermute x12, waiting for transfers between devices, shift(): return lax.ppermute(block, axis, route)  22.4 us
    all_to_all x3, starting transfers between devices, exchange(): return lax.all_to_all(pieces, AXES, 0, 0, axis_index_groups=groups)  19.5 us
    all_to_all x3, waiting for transfers between devices, exchange(): return lax.all_to_all(pieces, AXES, 0, 0, axis_index_groups=groups)  9.08 us
    unnamed x18, local copies, waits for them, and re-layouts  4.74 us
  transfers between devices with their start and end apart: 17, of which 11 were waited for; matrix products, arithmetic and copies ran while one was open for 0% of the time, Pallas kernels for 21%

profile of v5, /device:TPU:1, one launch (start us, length us, event | category | flops | bytes accessed | tf_op | source)
XLA Modules:
  0.0 133.8 jit_solution(631607585135120048)
XLA Ops:
  0.6 0.0 copy-start.1
  0.6 1.2 copy-done.1
  1.9 0.1 shard_map.75
  2.0 3.9 %collective-permute-start.1 = (bf16[4,1,32,256]{3,2,1,0:T(8,128)(2,1)S(1)}, bf16[4,1,32,256]{3,2,1,0:T(8,128)(2,1)S(1)}, u32[]{:S(2)}, u32[]{:S(2)}) collective-permute-start(bf16[4,1,32,256]{3,2,1,0:T(8,128)(2,1)S(1)} %get-tuple-element.32), channel_id=1, source_target_pairs={{0,4},{4,8},{8,12},{12,16},{16,20},{20,24},{24,28},{1,5},{5,9},{9,... | collective-permute-start | bytes 196616 | tf_op jit(solution)/shard_map/ppermute | solution.py:54
  5.9 1.3 collective-permute-start.2
  7.2 3.2 %collective-permute-start = (bf16[2,16,32,256]{3,2,1,0:T(8,128)(2,1)S(1)}, bf16[2,16,32,256]{3,2,1,0:T(8,128)(2,1)S(1)}, u32[]{:S(2)}, u32[]{:S(2)}) collective-permute-start(bf16[2,16,32,256]{3,2,1,0:T(8,128)(2,1)S(1)} %get-tuple-element.31), channel_id=1, source_target_pairs={{0,32},{32,64},{64,96},{1,33},{33,65},{65,97},{2,34},{34,66},{66,9... | collective-permute-start | bytes 1572872 | tf_op jit(solution)/shard_map/ppermute | solution.py:54
  10.5 0.0 collective-permute-done.1.refs_1_
  10.5 0.5 collective-permute-done.2.refs_2_
  10.9 0.3 shard_map.76
  11.3 7.5 %collective-permute-start.3 = (bf16[4,32,256]{2,1,0:T(8,128)(2,1)S(1)}, bf16[4,32,256]{2,1,0:T(8,128)(2,1)S(1)}, u32[]{:S(2)}, u32[]{:S(2)}) collective-permute-start(bf16[4,32,256]{2,1,0:T(8,128)(2,1)S(1)} %get-tuple-element.34), channel_id=1, source_target_pairs={{0,1},{1,2},{2,3},{4,5},{5,6},{6,7},{8,9},{9,10},{10,11},{12,13},{... | collective-permute-start | bytes 196616 | tf_op jit(solution)/shard_map/ppermute | solution.py:54
  18.8 0.0 copy-start.3
  18.8 0.0 copy-start.5
  18.8 2.1 %shard_map.77.refs_5_.refs_4_ = bf16[3,2304,256]{2,1,0:T(8,128)(2,1)S(1)} custom-call(bf16[3,2304,256]{2,1,0:T(8,128)(2,1)} %bitcast.16), custom_call_target="tpu_custom_call" | custom-call | flops 1811939328 | bytes 4194304 | tf_op jit(solution)/shard_map/pallas_call | solution.py:316
  20.9 1.9 %collective-permute-start.4 = (bf16[4,32,256]{2,1,0:T(8,128)(2,1)S(1)}, bf16[4,32,256]{2,1,0:T(8,128)(2,1)S(1)}, u32[]{:S(2)}, u32[]{:S(2)}) collective-permute-start(bf16[4,32,256]{2,1,0:T(8,128)(2,1)S(1)} %get-tuple-element.35), channel_id=1, source_target_pairs={{1,0},{2,1},{3,2},{5,4},{6,5},{7,6},{9,8},{10,9},{11,10},{13,12},{... | collective-permute-start | bytes 196616 | tf_op jit(solution)/shard_map/ppermute | solution.py:54
  22.9 0.0 collective-permute-done.3.refs_3_
  22.9 5.1 %collective-permute-done.4.refs_4_ = bf16[4,32,256]{2,1,0:T(8,128)(2,1)S(1)} collective-permute-done((bf16[4,32,256]{2,1,0:T(8,128)(2,1)S(1)}, bf16[4,32,256]{2,1,0:T(8,128)(2,1)S(1)}, u32[]{:S(2)}, u32[]{:S(2)}) %collective-permute-start.4) | collective-permute-done | bytes 65568 | tf_op jit(solution)/shard_map/ppermute | solution.py:54
  28.0 3.2 %collective-permute-start.5 = (bf16[2,4,32,256]{3,2,1,0:T(8,128)(2,1)S(1)}, bf16[2,4,32,256]{3,2,1,0:T(8,128)(2,1)S(1)}, u32[]{:S(2)}, u32[]{:S(2)}) collective-permute-start(bf16[2,4,32,256]{3,2,1,0:T(8,128)(2,1)S(1)} %pad_maximum_fusion), channel_id=1, source_target_pairs={{0,32},{32,64},{64,96},{1,33},{33,65},{65,97},{2,34},{34,66},{66,9... | collective-permute-start | bytes 393224 | tf_op jit(solution)/shard_map/ppermute | solution.py:54
  31.2 0.0 copy-done.3
  31.2 0.0 copy-done.5
  31.3 5.5 %shard_map.78 = (bf16[4,16,32,256]{3,2,1,0:T(8,128)(2,1)}, bf16[2,16,32,256]{3,2,1,0:T(8,128)(2,1)S(1)}, bf16[3,4,18,32,256]{4,3,2,1,0:T(8,128)(2,1)S(1)}) custom-call(bf16[4,16,32,256]{3,2,1,0:T(8,128)(2,1)S(1)} %copy-done.1, bf16[4,1,32,256]{3,2,1,0:T(8,128)(2,1)S(1)} %collective-permute-done.1.refs_1_, ...), custom_call_target="tpu_custom_call" | custom-call | flops 3623878656 | bytes 4194304 | tf_op jit(solution)/shard_map/pallas_call | solution.py:316
  36.8 0.0 collective-permute-done.5.refs_1_
  36.8 0.0 collective-permute-done.refs_0_
  36.8 5.3 %shard_map.79 = (bf16[4,16,32,256]{3,2,1,0:T(8,128)(2,1)}, bf16[4,1,32,256]{3,2,1,0:T(8,128)(2,1)S(1)}, bf16[4,1,32,256]{3,2,1,0:T(8,128)(2,1)}, bf16[2,16,32,25...) custom-call(bf16[2,16,32,256]{3,2,1,0:T(8,128)(2,1)S(1)} %collective, ...), custom_call_target="tpu_custom_call", output_to_operand_aliasing={{0}: (7, {})} | custom-call | flops 3623878656 | bytes 4194304 | tf_op jit(solution)/shard_map/pallas_call | solution.py:316
  42.1 0.0 copy-start.4
  42.1 3.9 %shard_map.81 = bf16[28,128,256]{2,1,0:T(8,128)(2,1)S(1)} custom-call(bf16[3,2,18,32,256]{4,3,2,1,0:T(8,128)(2,1)S(1)} %get-tuple-element.40.refs_0_, bf16[3,4,18,32,256]{4,3,2,1,0:T(8,128)(2,1)S(1)} %get-tuple-element.36.refs_2_.refs_1_, bf16[4,16,32,256]{3,2,1,0:T(8,128)(2,1)S(1)} %get-tuple-element.41.refs_2_.refs_0_), custom_call_target="tpu_custom_call" | custom-call | bytes 1024 | tf_op jit(solution)/shard_map/pallas_call | solution.py:316
  46.0 0.0 copy-done.4
  46.0 0.3 collective-permute-start.6
  46.3 3.9 %shard_map.80.refs_0_ = f32[28,128,256]{2,1,0:T(8,128)S(1)} custom-call(bf16[3,2,18,32,256]{4,3,2,1,0:T(8,128)(2,1)S(1)} %get-tuple-element.40.refs_0_, bf16[3,4,18,32,256]{4,3,2,1,0:T(8,128)(2,1)S(1)} %get-tuple-element.36.refs_2_.refs_1_, bf16[4,16,32,256]{3,2,1,0:T(8,128)(2,1)S(1)} %get-tuple-element.41.refs_2_.refs_0_), custom_call_target="tpu_custom_call" | custom-call | bytes 1024 | tf_op jit(solution)/shard_map/pallas_call | solution.py:316
  50.2 0.0 collective-permute-done.6.refs_1_
  50.2 1.5 %shard_map.82 = bf16[28,128,256]{2,1,0:T(8,128)(2,1)} custom-call(f32[28,128,256]{2,1,0:T(8,128)S(1)} %shard_map.80.refs_0_, bf16[28,128,256]{2,1,0:T(8,128)(2,1)S(1)} %collective-permute-done.6.refs_1_), custom_call_target="tpu_custom_call" | custom-call | bytes 1024 | tf_op jit(solution)/shard_map/pallas_call | solution.py:316
  51.7 6.4 %all-to-all-start = ((bf16[8,448,256]{2,1,0:T(8,128)(2,1)}), bf16[8,448,256]{2,1,0:T(8,128)(2,1)S(1)}, u32[]{:S(2)}, u32[]{:S(2)}) async-start(bf16[8,448,256]{2,1,0:T(8,128)(2,1)} %bitcast.4), calls=%async_computation | async-start | bytes 3670016 | tf_op jit(solution)/shard_map/all_to_all | solution.py:45
  58.2 1.3 collective-permute-start.9
  59.5 1.3 collective-permute-start.7
  60.8 1.3 collective-permute-start.8
  62.2 0.9 collective-permute-done.7.refs_1_
  63.0 3.7 %collective-permute-done.8.refs_2_ = bf16[4,1,32,256]{3,2,1,0:T(8,128)(2,1)S(1)} collective-permute-done((bf16[4,1,32,256]{3,2,1,0:T(8,128)(2,1)}, bf16[4,1,32,256]{3,2,1,0:T(8,128)(2,1)S(1)}, u32[]{:S(2)}, u32[]{:S(2)}) %collective-permute-start.8) | collective-permute-done | bytes 65568 | tf_op jit(solution)/shard_map/ppermute | solution.py:54
  66.8 7.2 %all-to-all-done.refs_0_ = bf16[8,448,256]{2,1,0:T(8,128)(2,1)S(1)} async-done(((bf16[8,448,256]{2,1,0:T(8,128)(2,1)}), bf16[8,448,256]{2,1,0:T(8,128)(2,1)S(1)}, u32[]{:S(2)}, u32[]{:S(2)}) %all-to-all-start) | async-done | bytes 1835040 | tf_op jit(solution)/shard_map/all_to_all | solution.py:45
  74.0 1.6 %shard_map.83.refs_3_ = bf16[8,448,256]{2,1,0:T(8,128)(2,1)} custom-call(bf16[8,448,256]{2,1,0:T(8,128)(2,1)S(1)} %all-to-all-done.refs_0_, s32[1]{0:T(128)} %bitcast.5.refs_1_), custom_call_target="tpu_custom_call" | custom-call | bytes 4194304 | tf_op jit(solution)/shard_map/pallas_call | solution.py:316
  75.5 2.3 %collective-permute-done.9.refs_5_ = bf16[2,16,32,256]{3,2,1,0:T(8,128)(2,1)} collective-permute-done((bf16[2,16,32,256]{3,2,1,0:T(8,128)(2,1)S(1)}, bf16[2,16,32,256]{3,2,1,0:T(8,128)(2,1)}, u32[]{:S(2)}, u32[]{:S(2)}) %collective-permute-start.9) | collective-permute-done | bytes 524320 | tf_op jit(solution)/shard_map/ppermute | solution.py:54
  77.9 9.0 %all-to-all-start.1 = ((bf16[8,448,256]{2,1,0:T(8,128)(2,1)}), bf16[8,448,256]{2,1,0:T(8,128)(2,1)S(1)}, u32[]{:S(2)}, u32[]{:S(2)}) async-start(bf16[8,448,256]{2,1,0:T(8,128)(2,1)} %shard_map.83.refs_3_), calls=%async_computation.1 | async-start | bytes 3670016 | tf_op jit(solution)/shard_map/all_to_all | solution.py:45
  86.9 0.3 shard_map.84
  87.2 5.8 %collective-permute-start.10 = (bf16[4,32,256]{2,1,0:T(8,128)(2,1)S(1)}, bf16[4,32,256]{2,1,0:T(8,128)(2,1)S(1)}, u32[]{:S(2)}, u32[]{:S(2)}) collective-permute-start(bf16[4,32,256]{2,1,0:T(8,128)(2,1)S(1)} %get-tuple-element.49), channel_id=1, source_target_pairs={{0,1},{1,2},{2,3},{4,5},{5,6},{6,7},{8,9},{9,10},{10,11},{12,13},{... | collective-permute-start | bytes 196616 | tf_op jit(solution)/shard_map/ppermute | solution.py:54
  93.1 1.9 %collective-permute-start.11 = (bf16[4,32,256]{2,1,0:T(8,128)(2,1)S(1)}, bf16[4,32,256]{2,1,0:T(8,128)(2,1)S(1)}, u32[]{:S(2)}, u32[]{:S(2)}) collective-permute-start(bf16[4,32,256]{2,1,0:T(8,128)(2,1)S(1)} %get-tuple-element.50), channel_id=1, source_target_pairs={{1,0},{2,1},{3,2},{5,4},{6,5},{7,6},{9,8},{10,9},{11,10},{13,12},{... | collective-permute-start | bytes 196616 | tf_op jit(solution)/shard_map/ppermute | solution.py:54
  95.0 3.1 %collective-permute-done.10.refs_3_ = bf16[4,32,256]{2,1,0:T(8,128)(2,1)S(1)} collective-permute-done((bf16[4,32,256]{2,1,0:T(8,128)(2,1)S(1)}, bf16[4,32,256]{2,1,0:T(8,128)(2,1)S(1)}, u32[]{:S(2)}, u32[]{:S(2)}) %collective-permute-start.10) | collective-permute-done | bytes 65568 | tf_op jit(solution)/shard_map/ppermute | solution.py:54
  98.1 0.0 copy-start.6
  98.1 2.3 %collective-permute-done.11.refs_4_ = bf16[4,32,256]{2,1,0:T(8,128)(2,1)S(1)} collective-permute-done((bf16[4,32,256]{2,1,0:T(8,128)(2,1)S(1)}, bf16[4,32,256]{2,1,0:T(8,128)(2,1)S(1)}, u32[]{:S(2)}, u32[]{:S(2)}) %collective-permute-start.11) | collective-permute-done | bytes 65568 | tf_op jit(solution)/shard_map/ppermute | solution.py:54
  100.5 0.0 copy-start.7
  100.5 1.3 collective-permute-start.12
  101.8 4.4 %collective-permute-done.12.refs_6_ = bf16[2,4,32,256]{3,2,1,0:T(8,128)(2,1)S(1)} collective-permute-done((bf16[2,4,32,256]{3,2,1,0:T(8,128)(2,1)S(1)}, bf16[2,4,32,256]{3,2,1,0:T(8,128)(2,1)S(1)}, u32[]{:S(2)}, u32[]{:S(2)}) %collective-permute-start.12) | collective-permute-done | bytes 131104 | tf_op jit(solution)/shard_map/ppermute | solution.py:54
  106.2 0.0 copy-start.8
  106.2 0.0 all-to-all-done.1.refs_0_
  106.2 0.4 shard_map.85
  106.6 0.0 copy-done.6
  106.6 0.0 copy-done.7
  106.6 0.3 copy-done.8
  106.9 1.2 copy-done
  108.1 4.1 %all-to-all-start.2 = ((bf16[8,448,256]{2,1,0:T(8,128)(2,1)}), bf16[8,448,256]{2,1,0:T(8,128)(2,1)S(1)}, u32[]{:S(2)}, u32[]{:S(2)}) async-start(bf16[8,448,256]{2,1,0:T(8,128)(2,1)} %copy-done), calls=%async_computation.2 | async-start | bytes 3670016 | tf_op jit(solution)/shard_map/all_to_all | solution.py:45
  112.2 2.0 %copy-done.2 = bf16[27,256,256]{2,1,0:T(8,128)(2,1)S(1)} copy-done((bf16[27,256,256]{2,1,0:T(8,128)(2,1)S(1)}, bf16[27,256,256]{2,1,0:T(8,128)(2,1)}, u32[]{:S(2)}) %copy-start.2) | copy-done | bytes 3538968
  114.2 11.9 %shard_map.86 = bf16[4,16,32,256]{3,2,1,0:T(8,128)(2,1)} custom-call(bf16[4,16,32,256]{3,2,1,0:T(8,128)(2,1)S(1)} %get-tuple-element.41.refs_2_.refs_0_, bf16[4,1,32,256]{3,2,1,0:T(8,128)(2,1)S(1)} %collective-permute-done.7.refs_1_, bf16[4,1,32,256]{3,2,1,0:T(8,128)(2,1)S(1)} %collective-permute-done.8.refs_2_, bf16[4,32,256]{2,1,0:T(8,128)(2,1)} %copy-done.6, ...), custom_call_target="tpu_custom_call" | custom-call | flops 7247757312 | bytes 4194304 | tf_op jit(solution)/shard_map/pallas_call | solution.py:316
  126.1 1.9 %all-to-all-done.2 = bf16[8,448,256]{2,1,0:T(8,128)(2,1)S(1)} async-done(((bf16[8,448,256]{2,1,0:T(8,128)(2,1)}), bf16[8,448,256]{2,1,0:T(8,128)(2,1)S(1)}, u32[]{:S(2)}, u32[]{:S(2)}) %all-to-all-start.2) | async-done | bytes 1835040 | tf_op jit(solution)/shard_map/all_to_all | solution.py:45
  127.9 0.0 collective-permute-start.13
  128.0 2.4 %shard_map.87 = (f32[27,256,256]{2,1,0:T(8,128)}, f32[1,256]{1,0:T(1,128)}) custom-call(bf16[28,128,256]{2,1,0:T(8,128)(2,1)S(1)} %bitcast.15), custom_call_target="tpu_custom_call" | custom-call | bytes 4194304 | tf_op jit(solution)/shard_map/pallas_call | solution.py:316
  130.4 1.3 collective-permute-done.13.refs_0_
  131.7 1.9 %shard_map.88 = f32[27,256,256]{2,1,0:T(8,128)} custom-call(bf16[28,128,256]{2,1,0:T(8,128)(2,1)S(1)} %collective-permute-done.13.refs_0_, f32[27,256,256]{2,1,0:T(8,128)} %get-tuple-element.56.refs_1_), custom_call_target="tpu_custom_call", output_to_operand_aliasing={{}: (1, {})} | custom-call | bytes 4194304 | tf_op jit(solution)/shard_map/pallas_call | solution.py:316
  (12 shorter events, 0.1 us)
Async XLA Ops:
  0.6 1.2 copy-start.1
  2.0 8.5 %collective-permute-start.1 = (bf16[4,1,32,256]{3,2,1,0:T(8,128)(2,1)S(1)}, bf16[4,1,32,256]{3,2,1,0:T(8,128)(2,1)S(1)}, u32[]{:S(2)}, u32[]{:S(2)}) collective-permute-start(bf16[4,1,32,256]{3,2,1,0:T(8,128)(2,1)S(1)} %get-tuple-element.32), channel_id=1, source_target_pairs={{0,4},{4,8},{8,12},{12,16},{16,20},{20,24},{24,28},{1,5},{5,9},{9,... | collective-permute-start | bytes 196616 | tf_op jit(solution)/shard_map/ppermute | solution.py:54
  5.9 5.0 %collective-permute-start.2 = (bf16[4,1,32,256]{3,2,1,0:T(8,128)(2,1)S(1)}, bf16[4,1,32,256]{3,2,1,0:T(8,128)(2,1)S(1)}, u32[]{:S(2)}, u32[]{:S(2)}) collective-permute-start(bf16[4,1,32,256]{3,2,1,0:T(8,128)(2,1)S(1)} %get-tuple-element.33), channel_id=1, source_target_pairs={{4,0},{8,4},{12,8},{16,12},{20,16},{24,20},{28,24},{5,1},{9,5},{13... | collective-permute-start | bytes 196616 | tf_op jit(solution)/shard_map/ppermute | solution.py:54
  7.2 29.6 %collective-permute-start = (bf16[2,16,32,256]{3,2,1,0:T(8,128)(2,1)S(1)}, bf16[2,16,32,256]{3,2,1,0:T(8,128)(2,1)S(1)}, u32[]{:S(2)}, u32[]{:S(2)}) collective-permute-start(bf16[2,16,32,256]{3,2,1,0:T(8,128)(2,1)S(1)} %get-tuple-element.31), channel_id=1, source_target_pairs={{0,32},{32,64},{64,96},{1,33},{33,65},{65,97},{2,34},{34,66},{66,9... | collective-permute-start | bytes 1572872 | tf_op jit(solution)/shard_map/ppermute | solution.py:54
  11.3 11.6 %collective-permute-start.3 = (bf16[4,32,256]{2,1,0:T(8,128)(2,1)S(1)}, bf16[4,32,256]{2,1,0:T(8,128)(2,1)S(1)}, u32[]{:S(2)}, u32[]{:S(2)}) collective-permute-start(bf16[4,32,256]{2,1,0:T(8,128)(2,1)S(1)} %get-tuple-element.34), channel_id=1, source_target_pairs={{0,1},{1,2},{2,3},{4,5},{5,6},{6,7},{8,9},{9,10},{10,11},{12,13},{... | collective-permute-start | bytes 196616 | tf_op jit(solution)/shard_map/ppermute | solution.py:54
  18.8 12.5 %copy-start.3 = (bf16[4,16,32,256]{3,2,1,0:T(8,128)(2,1)S(1)}, bf16[4,16,32,256]{3,2,1,0:T(8,128)(2,1)}, u32[]{:S(2)}) copy-start(bf16[4,16,32,256]{3,2,1,0:T(8,128)(2,1)} %refs_5_.1) | copy-start | bytes 3145732
  18.8 12.5 %copy-start.5 = (f32[256]{0:T(256)S(1)}, f32[256]{0:T(256)}, u32[]{:S(2)}) copy-start(f32[256]{0:T(256)} %param.6) | copy-start | bytes 3076
  20.9 7.1 %collective-permute-start.4 = (bf16[4,32,256]{2,1,0:T(8,128)(2,1)S(1)}, bf16[4,32,256]{2,1,0:T(8,128)(2,1)S(1)}, u32[]{:S(2)}, u32[]{:S(2)}) collective-permute-start(bf16[4,32,256]{2,1,0:T(8,128)(2,1)S(1)} %get-tuple-element.35), channel_id=1, source_target_pairs={{1,0},{2,1},{3,2},{5,4},{6,5},{7,6},{9,8},{10,9},{11,10},{13,12},{... | collective-permute-start | bytes 196616 | tf_op jit(solution)/shard_map/ppermute | solution.py:54
  28.0 8.8 %collective-permute-start.5 = (bf16[2,4,32,256]{3,2,1,0:T(8,128)(2,1)S(1)}, bf16[2,4,32,256]{3,2,1,0:T(8,128)(2,1)S(1)}, u32[]{:S(2)}, u32[]{:S(2)}) collective-permute-start(bf16[2,4,32,256]{3,2,1,0:T(8,128)(2,1)S(1)} %pad_maximum_fusion), channel_id=1, source_target_pairs={{0,32},{32,64},{64,96},{1,33},{33,65},{65,97},{2,34},{34,66},{66,9... | collective-permute-start | bytes 393224 | tf_op jit(solution)/shard_map/ppermute | solution.py:54
  42.1 3.9 %copy-start.4 = (bf16[4,1,32,256]{3,2,1,0:T(8,128)(2,1)}, bf16[4,1,32,256]{3,2,1,0:T(8,128)(2,1)S(1)}, u32[]{:S(2)}) copy-start(bf16[4,1,32,256]{3,2,1,0:T(8,128)(2,1)S(1)} %get-tuple-element.43) | copy-start | bytes 196612
  46.0 4.2 %collective-permute-start.6 = (bf16[28,128,256]{2,1,0:T(8,128)(2,1)S(1)}, bf16[28,128,256]{2,1,0:T(8,128)(2,1)S(1)}, u32[]{:S(2)}, u32[]{:S(2)}) collective-permute-start(bf16[28,128,256]{2,1,0:T(8,128)(2,1)S(1)} %shard_map.81), channel_id=1, source_target_pairs={{0,1},{1,0},{2,3},{3,2},{4,5},{5,4},{6,7},{7,6},{8,9},{9,8},{10,11... | collective-permute-start | bytes 5505032 | tf_op jit(solution)/shard_map/ppermute | solution.py:449
  51.7 22.2 %all-to-all-start = ((bf16[8,448,256]{2,1,0:T(8,128)(2,1)}), bf16[8,448,256]{2,1,0:T(8,128)(2,1)S(1)}, u32[]{:S(2)}, u32[]{:S(2)}) async-start(bf16[8,448,256]{2,1,0:T(8,128)(2,1)} %bitcast.4), calls=%async_computation | async-start | bytes 3670016 | tf_op jit(solution)/shard_map/all_to_all | solution.py:45
  58.2 19.7 %collective-permute-start.9 = (bf16[2,16,32,256]{3,2,1,0:T(8,128)(2,1)S(1)}, bf16[2,16,32,256]{3,2,1,0:T(8,128)(2,1)}, u32[]{:S(2)}, u32[]{:S(2)}) collective-permute-start(bf16[2,16,32,256]{3,2,1,0:T(8,128)(2,1)S(1)} %get-tuple-element.45), channel_id=1, source_target_pairs={{32,0},{64,32},{96,64},{33,1},{65,33},{97,65},{34,2},{66,34},{98,6... | collective-permute-start | bytes 1572872 | tf_op jit(solution)/shard_map/ppermute | solution.py:54
  59.5 3.6 %collective-permute-start.7 = (bf16[4,1,32,256]{3,2,1,0:T(8,128)(2,1)}, bf16[4,1,32,256]{3,2,1,0:T(8,128)(2,1)S(1)}, u32[]{:S(2)}, u32[]{:S(2)}) collective-permute-start(bf16[4,1,32,256]{3,2,1,0:T(8,128)(2,1)} %get-tuple-element.42), channel_id=1, source_target_pairs={{0,4},{4,8},{8,12},{12,16},{16,20},{20,24},{24,28},{1,5},{5,9},{9,... | collective-permute-start | bytes 196616 | tf_op jit(solution)/shard_map/ppermute | solution.py:54
  60.8 6.0 %collective-permute-start.8 = (bf16[4,1,32,256]{3,2,1,0:T(8,128)(2,1)}, bf16[4,1,32,256]{3,2,1,0:T(8,128)(2,1)S(1)}, u32[]{:S(2)}, u32[]{:S(2)}) collective-permute-start(bf16[4,1,32,256]{3,2,1,0:T(8,128)(2,1)} %copy-done.4), channel_id=1, source_target_pairs={{4,0},{8,4},{12,8},{16,12},{20,16},{24,20},{28,24},{5,1},{9,5},{13... | collective-permute-start | bytes 196616 | tf_op jit(solution)/shard_map/ppermute | solution.py:54
  77.9 28.3 %all-to-all-start.1 = ((bf16[8,448,256]{2,1,0:T(8,128)(2,1)}), bf16[8,448,256]{2,1,0:T(8,128)(2,1)S(1)}, u32[]{:S(2)}, u32[]{:S(2)}) async-start(bf16[8,448,256]{2,1,0:T(8,128)(2,1)} %shard_map.83.refs_3_), calls=%async_computation.1 | async-start | bytes 3670016 | tf_op jit(solution)/shard_map/all_to_all | solution.py:45
  87.2 10.9 %collective-permute-start.10 = (bf16[4,32,256]{2,1,0:T(8,128)(2,1)S(1)}, bf16[4,32,256]{2,1,0:T(8,128)(2,1)S(1)}, u32[]{:S(2)}, u32[]{:S(2)}) collective-permute-start(bf16[4,32,256]{2,1,0:T(8,128)(2,1)S(1)} %get-tuple-element.49), channel_id=1, source_target_pairs={{0,1},{1,2},{2,3},{4,5},{5,6},{6,7},{8,9},{9,10},{10,11},{12,13},{... | collective-permute-start | bytes 196616 | tf_op jit(solution)/shard_map/ppermute | solution.py:54
  93.1 7.4 %collective-permute-start.11 = (bf16[4,32,256]{2,1,0:T(8,128)(2,1)S(1)}, bf16[4,32,256]{2,1,0:T(8,128)(2,1)S(1)}, u32[]{:S(2)}, u32[]{:S(2)}) collective-permute-start(bf16[4,32,256]{2,1,0:T(8,128)(2,1)S(1)} %get-tuple-element.50), channel_id=1, source_target_pairs={{1,0},{2,1},{3,2},{5,4},{6,5},{7,6},{9,8},{10,9},{11,10},{13,12},{... | collective-permute-start | bytes 196616 | tf_op jit(solution)/shard_map/ppermute | solution.py:54
  98.1 8.4 %copy-start.6 = (bf16[4,32,256]{2,1,0:T(8,128)(2,1)}, bf16[4,32,256]{2,1,0:T(8,128)(2,1)S(1)}, u32[]{:S(2)}) copy-start(bf16[4,32,256]{2,1,0:T(8,128)(2,1)S(1)} %collective-permute-done.10.refs_3_) | copy-start | bytes 196612
  100.5 6.1 %copy-start.7 = (bf16[4,32,256]{2,1,0:T(8,128)(2,1)}, bf16[4,32,256]{2,1,0:T(8,128)(2,1)S(1)}, u32[]{:S(2)}) copy-start(bf16[4,32,256]{2,1,0:T(8,128)(2,1)S(1)} %collective-permute-done.11.refs_4_) | copy-start | bytes 196612
  100.5 5.7 %collective-permute-start.12 = (bf16[2,4,32,256]{3,2,1,0:T(8,128)(2,1)S(1)}, bf16[2,4,32,256]{3,2,1,0:T(8,128)(2,1)S(1)}, u32[]{:S(2)}, u32[]{:S(2)}) collective-permute-start(bf16[2,4,32,256]{3,2,1,0:T(8,128)(2,1)S(1)} %pad_maximum_fusion.1), channel_id=1, source_target_pairs={{32,0},{64,32},{96,64},{33,1},{65,33},{97,65},{34,2},{66,34},{98,6... | collective-permute-start | bytes 393224 | tf_op jit(solution)/shard_map/ppermute | solution.py:54
  106.2 0.7 copy-start.8
  106.8 1.2 copy-start
  108.1 19.9 %all-to-all-start.2 = ((bf16[8,448,256]{2,1,0:T(8,128)(2,1)}), bf16[8,448,256]{2,1,0:T(8,128)(2,1)S(1)}, u32[]{:S(2)}, u32[]{:S(2)}) async-start(bf16[8,448,256]{2,1,0:T(8,128)(2,1)} %copy-done), calls=%async_computation.2 | async-start | bytes 3670016 | tf_op jit(solution)/shard_map/all_to_all | solution.py:45
  112.2 2.0 %copy-start.2 = (bf16[27,256,256]{2,1,0:T(8,128)(2,1)S(1)}, bf16[27,256,256]{2,1,0:T(8,128)(2,1)}, u32[]{:S(2)}) copy-start(bf16[27,256,256]{2,1,0:T(8,128)(2,1)} %refs_7_.1) | copy-start | bytes 10616836
  127.9 3.8 %collective-permute-start.13 = (bf16[28,128,256]{2,1,0:T(8,128)(2,1)S(1)}, bf16[28,128,256]{2,1,0:T(8,128)(2,1)S(1)}, u32[]{:S(2)}, u32[]{:S(2)}) collective-permute-start(bf16[28,128,256]{2,1,0:T(8,128)(2,1)S(1)} %bitcast.14), channel_id=1, source_target_pairs={{0,1},{1,0},{2,3},{3,2},{4,5},{5,4},{6,7},{7,6},{8,9},{9,8},{10,11... | collective-permute-start | bytes 5505032 | tf_op jit(solution)/shard_map/ppermute | solution.py:486

commit v6 on v5

--- a/solution.py
+++ b/solution.py
@@ -234,10 +234,10 @@
 
 
 def backward_kernel(field, low, high, *refs):
-    kernel, latent_grad, taps, held, sems = refs[4], refs[5], refs[6], refs[7:11], refs[11]
-    copies = transfers(sems, *zip(refs[:4], held))
-    left, right, remote, edges = held
-    for copy in copies:
+    latent_grad, taps, held, sems = refs[5], refs[6], refs[7:12], refs[12]
+    copies = transfers(sems, *zip(refs[:5], held))
+    left, right, remote, edges, kernel = held
+    for copy in copies[:4]:
         copy.wait()
     put = placer(taps)
 
@@ -247,6 +247,7 @@
     for t in (1, 0):
         put(4 + t, remote[t], edges[t, 0:1], edges[t, 1:2], edges[t, 2], edges[t, 3])
     put_own(3)
+    copies[4].wait()
 
     def one(t):
         total = jnp.zeros((512, 256), F32)
@@ -475,13 +476,13 @@
         backward_kernel,
         shape(*block),
         8,
-        [buffer(*bordered)] + [buffer(*x.shape) for x in sources[3:7]],
-        4,
+        [buffer(*bordered)] + [buffer(*x.shape) for x in sources[3:8]],
+        5,
         vmem=20,
         flops=conv_flops,
-        specs=[VMEM] * 3 + [HBM] * 4 + [VMEM],
+        specs=[VMEM] * 3 + [HBM] * 5,
         out_specs=VMEM,
-    )(*sources[:3], *[in_hbm(x) for x in sources[3:7]], kernel)
+    )(*sources[:3], *[in_hbm(x) for x in sources[3:8]])
     mine, latent_grad = lax.optimization_barrier((mine, latent_grad))
     other = lax.ppermute(mine, "wc", [(0, 1), (1, 0)])
     kernel_grad, bias_grad = finish(scale, 0, mine)

time: 134 us -> 134 us (level)
  local copies, waits for them, and re-layouts: 4.77 us -> 2.77 us
  waiting for transfers between devices: 32.8 us -> 34.3 us
    unnamed x18 -> x16, local copies, waits for them, and re-layouts: 4.74 us -> 2.74 us
    all_to_all x3, waiting for transfers between devices: 9.08 us -> 10.5 us  [exchange(): return lax.all_to_all(pieces, AXES, 0, 0, axis_index_groups=groups)]
where the time goes in v6:
time: 134 us
  starting transfers between devices  53.8 us (40%)
  Pallas kernels  41.7 us (31%)
  waiting for transfers between devices  34.3 us (26%)
  local copies, waits for them, and re-layouts  2.77 us (2%)
    pallas_call x14, Pallas kernels, call(): return lambda *operands: run(*operands, *after)  41.7 us
    ppermute x12, starting transfers between devices, shift(): return lax.ppermute(block, axis, route)  34 us
    ppermute x12, waiting for transfers between devices, shift(): return lax.ppermute(block, axis, route)  22.4 us
    all_to_all x3, starting transfers between devices, exchange(): return lax.all_to_all(pieces, AXES, 0, 0, axis_index_groups=groups)  19.5 us
    all_to_all x3, waiting for transfers between devices, exchange(): return lax.all_to_all(pieces, AXES, 0, 0, axis_index_groups=groups)  10.5 us
    unnamed x16, local copies, waits for them, and re-layouts  2.74 us
  transfers between devices with their start and end apart: 17, of which 11 were waited for; matrix products, arithmetic and copies ran while one was open for 0% of the time, Pallas kernels for 21%

profile of v6, /device:TPU:1, one launch (start us, length us, event | category | flops | bytes accessed | tf_op | source)
XLA Modules:
  0.0 133.8 jit_solution(5408418386312161553)
XLA Ops:
  0.6 0.0 copy-start.1
  0.6 1.2 copy-done.1
  1.9 0.1 shard_map.75
  2.0 3.9 %collective-permute-start.1 = (bf16[4,1,32,256]{3,2,1,0:T(8,128)(2,1)S(1)}, bf16[4,1,32,256]{3,2,1,0:T(8,128)(2,1)S(1)}, u32[]{:S(2)}, u32[]{:S(2)}) collective-permute-start(bf16[4,1,32,256]{3,2,1,0:T(8,128)(2,1)S(1)} %get-tuple-element.32), channel_id=1, source_target_pairs={{0,4},{4,8},{8,12},{12,16},{16,20},{20,24},{24,28},{1,5},{5,9},{9,... | collective-permute-start | bytes 196616 | tf_op jit(solution)/shard_map/ppermute | solution.py:54
  5.9 1.3 collective-permute-start.2
  7.2 3.2 %collective-permute-start = (bf16[2,16,32,256]{3,2,1,0:T(8,128)(2,1)S(1)}, bf16[2,16,32,256]{3,2,1,0:T(8,128)(2,1)S(1)}, u32[]{:S(2)}, u32[]{:S(2)}) collective-permute-start(bf16[2,16,32,256]{3,2,1,0:T(8,128)(2,1)S(1)} %get-tuple-element.31), channel_id=1, source_target_pairs={{0,32},{32,64},{64,96},{1,33},{33,65},{65,97},{2,34},{34,66},{66,9... | collective-permute-start | bytes 1572872 | tf_op jit(solution)/shard_map/ppermute | solution.py:54
  10.5 0.0 collective-permute-done.1.refs_1_
  10.5 0.5 collective-permute-done.2.refs_2_
  10.9 0.3 shard_map.76
  11.3 7.5 %collective-permute-start.3 = (bf16[4,32,256]{2,1,0:T(8,128)(2,1)S(1)}, bf16[4,32,256]{2,1,0:T(8,128)(2,1)S(1)}, u32[]{:S(2)}, u32[]{:S(2)}) collective-permute-start(bf16[4,32,256]{2,1,0:T(8,128)(2,1)S(1)} %get-tuple-element.34), channel_id=1, source_target_pairs={{0,1},{1,2},{2,3},{4,5},{5,6},{6,7},{8,9},{9,10},{10,11},{12,13},{... | collective-permute-start | bytes 196616 | tf_op jit(solution)/shard_map/ppermute | solution.py:54
  18.8 0.0 copy-start.2
  18.8 0.0 copy-start.4
  18.8 2.1 %shard_map.77.refs_5_.refs_4_ = bf16[3,2304,256]{2,1,0:T(8,128)(2,1)S(1)} custom-call(bf16[3,2304,256]{2,1,0:T(8,128)(2,1)} %bitcast.18), custom_call_target="tpu_custom_call" | custom-call | flops 1811939328 | bytes 4194304 | tf_op jit(solution)/shard_map/pallas_call | solution.py:317
  20.9 1.9 %collective-permute-start.4 = (bf16[4,32,256]{2,1,0:T(8,128)(2,1)S(1)}, bf16[4,32,256]{2,1,0:T(8,128)(2,1)S(1)}, u32[]{:S(2)}, u32[]{:S(2)}) collective-permute-start(bf16[4,32,256]{2,1,0:T(8,128)(2,1)S(1)} %get-tuple-element.35), channel_id=1, source_target_pairs={{1,0},{2,1},{3,2},{5,4},{6,5},{7,6},{9,8},{10,9},{11,10},{13,12},{... | collective-permute-start | bytes 196616 | tf_op jit(solution)/shard_map/ppermute | solution.py:54
  22.9 0.0 collective-permute-done.3.refs_3_
  22.9 5.1 %collective-permute-done.4.refs_4_ = bf16[4,32,256]{2,1,0:T(8,128)(2,1)S(1)} collective-permute-done((bf16[4,32,256]{2,1,0:T(8,128)(2,1)S(1)}, bf16[4,32,256]{2,1,0:T(8,128)(2,1)S(1)}, u32[]{:S(2)}, u32[]{:S(2)}) %collective-permute-start.4) | collective-permute-done | bytes 65568 | tf_op jit(solution)/shard_map/ppermute | solution.py:54
  28.0 3.2 %collective-permute-start.5 = (bf16[2,4,32,256]{3,2,1,0:T(8,128)(2,1)S(1)}, bf16[2,4,32,256]{3,2,1,0:T(8,128)(2,1)S(1)}, u32[]{:S(2)}, u32[]{:S(2)}) collective-permute-start(bf16[2,4,32,256]{3,2,1,0:T(8,128)(2,1)S(1)} %pad_maximum_fusion), channel_id=1, source_target_pairs={{0,32},{32,64},{64,96},{1,33},{33,65},{65,97},{2,34},{34,66},{66,9... | collective-permute-start | bytes 393224 | tf_op jit(solution)/shard_map/ppermute | solution.py:54
  31.2 0.0 copy-done.2
  31.2 0.0 copy-done.4
  31.3 5.5 %shard_map.78 = (bf16[4,16,32,256]{3,2,1,0:T(8,128)(2,1)}, bf16[2,16,32,256]{3,2,1,0:T(8,128)(2,1)S(1)}, bf16[3,4,18,32,256]{4,3,2,1,0:T(8,128)(2,1)S(1)}) custom-call(bf16[4,16,32,256]{3,2,1,0:T(8,128)(2,1)S(1)} %copy-done.1, bf16[4,1,32,256]{3,2,1,0:T(8,128)(2,1)S(1)} %collective-permute-done.1.refs_1_, ...), custom_call_target="tpu_custom_call" | custom-call | flops 3623878656 | bytes 4194304 | tf_op jit(solution)/shard_map/pallas_call | solution.py:317
  36.8 0.0 collective-permute-done.5.refs_1_
  36.8 0.0 collective-permute-done.refs_0_
  36.8 5.3 %shard_map.79 = (bf16[4,16,32,256]{3,2,1,0:T(8,128)(2,1)}, bf16[4,1,32,256]{3,2,1,0:T(8,128)(2,1)S(1)}, bf16[4,1,32,256]{3,2,1,0:T(8,128)(2,1)}, bf16[2,16,32,25...) custom-call(bf16[2,16,32,256]{3,2,1,0:T(8,128)(2,1)S(1)} %collective, ...), custom_call_target="tpu_custom_call", output_to_operand_aliasing={{0}: (7, {})} | custom-call | flops 3623878656 | bytes 4194304 | tf_op jit(solution)/shard_map/pallas_call | solution.py:317
  42.1 0.0 copy-start.3
  42.1 3.9 %shard_map.81 = bf16[28,128,256]{2,1,0:T(8,128)(2,1)S(1)} custom-call(bf16[3,2,18,32,256]{4,3,2,1,0:T(8,128)(2,1)S(1)} %get-tuple-element.40.refs_0_, bf16[3,4,18,32,256]{4,3,2,1,0:T(8,128)(2,1)S(1)} %get-tuple-element.36.refs_2_.refs_1_, bf16[4,16,32,256]{3,2,1,0:T(8,128)(2,1)S(1)} %get-tuple-element.41.refs_2_.refs_0_), custom_call_target="tpu_custom_call" | custom-call | bytes 1024 | tf_op jit(solution)/shard_map/pallas_call | solution.py:317
  46.0 0.0 copy-done.3
  46.0 0.3 collective-permute-start.6
  46.3 3.9 %shard_map.80.refs_0_ = f32[28,128,256]{2,1,0:T(8,128)S(1)} custom-call(bf16[3,2,18,32,256]{4,3,2,1,0:T(8,128)(2,1)S(1)} %get-tuple-element.40.refs_0_, bf16[3,4,18,32,256]{4,3,2,1,0:T(8,128)(2,1)S(1)} %get-tuple-element.36.refs_2_.refs_1_, bf16[4,16,32,256]{3,2,1,0:T(8,128)(2,1)S(1)} %get-tuple-element.41.refs_2_.refs_0_), custom_call_target="tpu_custom_call" | custom-call | bytes 1024 | tf_op jit(solution)/shard_map/pallas_call | solution.py:317
  50.2 0.0 collective-permute-done.6.refs_1_
  50.2 1.5 %shard_map.82 = bf16[28,128,256]{2,1,0:T(8,128)(2,1)} custom-call(f32[28,128,256]{2,1,0:T(8,128)S(1)} %shard_map.80.refs_0_, bf16[28,128,256]{2,1,0:T(8,128)(2,1)S(1)} %collective-permute-done.6.refs_1_), custom_call_target="tpu_custom_call" | custom-call | bytes 1024 | tf_op jit(solution)/shard_map/pallas_call | solution.py:317
  51.7 6.4 %all-to-all-start = ((bf16[8,448,256]{2,1,0:T(8,128)(2,1)}), bf16[8,448,256]{2,1,0:T(8,128)(2,1)S(1)}, u32[]{:S(2)}, u32[]{:S(2)}) async-start(bf16[8,448,256]{2,1,0:T(8,128)(2,1)} %bitcast.4), calls=%async_computation | async-start | bytes 3670016 | tf_op jit(solution)/shard_map/all_to_all | solution.py:45
  58.2 1.3 collective-permute-start.9
  59.5 1.3 collective-permute-start.7
  60.8 1.3 collective-permute-start.8
  62.2 0.9 collective-permute-done.7.refs_1_
  63.0 3.7 %collective-permute-done.8.refs_2_ = bf16[4,1,32,256]{3,2,1,0:T(8,128)(2,1)S(1)} collective-permute-done((bf16[4,1,32,256]{3,2,1,0:T(8,128)(2,1)}, bf16[4,1,32,256]{3,2,1,0:T(8,128)(2,1)S(1)}, u32[]{:S(2)}, u32[]{:S(2)}) %collective-permute-start.8) | collective-permute-done | bytes 65568 | tf_op jit(solution)/shard_map/ppermute | solution.py:54
  66.8 7.2 %all-to-all-done.refs_0_ = bf16[8,448,256]{2,1,0:T(8,128)(2,1)S(1)} async-done(((bf16[8,448,256]{2,1,0:T(8,128)(2,1)}), bf16[8,448,256]{2,1,0:T(8,128)(2,1)S(1)}, u32[]{:S(2)}, u32[]{:S(2)}) %all-to-all-start) | async-done | bytes 1835040 | tf_op jit(solution)/shard_map/all_to_all | solution.py:45
  74.0 1.6 %shard_map.83.refs_3_ = bf16[8,448,256]{2,1,0:T(8,128)(2,1)} custom-call(bf16[8,448,256]{2,1,0:T(8,128)(2,1)S(1)} %all-to-all-done.refs_0_, s32[1]{0:T(128)} %bitcast.5.refs_1_), custom_call_target="tpu_custom_call" | custom-call | bytes 4194304 | tf_op jit(solution)/shard_map/pallas_call | solution.py:317
  75.5 2.3 %collective-permute-done.9.refs_5_ = bf16[2,16,32,256]{3,2,1,0:T(8,128)(2,1)} collective-permute-done((bf16[2,16,32,256]{3,2,1,0:T(8,128)(2,1)S(1)}, bf16[2,16,32,256]{3,2,1,0:T(8,128)(2,1)}, u32[]{:S(2)}, u32[]{:S(2)}) %collective-permute-start.9) | collective-permute-done | bytes 524320 | tf_op jit(solution)/shard_map/ppermute | solution.py:54
  77.9 9.0 %all-to-all-start.1 = ((bf16[8,448,256]{2,1,0:T(8,128)(2,1)}), bf16[8,448,256]{2,1,0:T(8,128)(2,1)S(1)}, u32[]{:S(2)}, u32[]{:S(2)}) async-start(bf16[8,448,256]{2,1,0:T(8,128)(2,1)} %shard_map.83.refs_3_), calls=%async_computation.1 | async-start | bytes 3670016 | tf_op jit(solution)/shard_map/all_to_all | solution.py:45
  86.9 0.3 shard_map.84
  87.2 5.8 %collective-permute-start.10 = (bf16[4,32,256]{2,1,0:T(8,128)(2,1)S(1)}, bf16[4,32,256]{2,1,0:T(8,128)(2,1)S(1)}, u32[]{:S(2)}, u32[]{:S(2)}) collective-permute-start(bf16[4,32,256]{2,1,0:T(8,128)(2,1)S(1)} %get-tuple-element.49), channel_id=1, source_target_pairs={{0,1},{1,2},{2,3},{4,5},{5,6},{6,7},{8,9},{9,10},{10,11},{12,13},{... | collective-permute-start | bytes 196616 | tf_op jit(solution)/shard_map/ppermute | solution.py:54
  93.1 1.9 %collective-permute-start.11 = (bf16[4,32,256]{2,1,0:T(8,128)(2,1)S(1)}, bf16[4,32,256]{2,1,0:T(8,128)(2,1)S(1)}, u32[]{:S(2)}, u32[]{:S(2)}) collective-permute-start(bf16[4,32,256]{2,1,0:T(8,128)(2,1)S(1)} %get-tuple-element.50), channel_id=1, source_target_pairs={{1,0},{2,1},{3,2},{5,4},{6,5},{7,6},{9,8},{10,9},{11,10},{13,12},{... | collective-permute-start | bytes 196616 | tf_op jit(solution)/shard_map/ppermute | solution.py:54
  95.0 3.1 %collective-permute-done.10.refs_3_ = bf16[4,32,256]{2,1,0:T(8,128)(2,1)S(1)} collective-permute-done((bf16[4,32,256]{2,1,0:T(8,128)(2,1)S(1)}, bf16[4,32,256]{2,1,0:T(8,128)(2,1)S(1)}, u32[]{:S(2)}, u32[]{:S(2)}) %collective-permute-start.10) | collective-permute-done | bytes 65568 | tf_op jit(solution)/shard_map/ppermute | solution.py:54
  98.1 0.0 copy-start.5
  98.1 2.3 %collective-permute-done.11.refs_4_ = bf16[4,32,256]{2,1,0:T(8,128)(2,1)S(1)} collective-permute-done((bf16[4,32,256]{2,1,0:T(8,128)(2,1)S(1)}, bf16[4,32,256]{2,1,0:T(8,128)(2,1)S(1)}, u32[]{:S(2)}, u32[]{:S(2)}) %collective-permute-start.11) | collective-permute-done | bytes 65568 | tf_op jit(solution)/shard_map/ppermute | solution.py:54
  100.5 0.0 copy-start.6
  100.5 1.3 collective-permute-start.12
  101.8 4.4 %collective-permute-done.12.refs_6_ = bf16[2,4,32,256]{3,2,1,0:T(8,128)(2,1)S(1)} collective-permute-done((bf16[2,4,32,256]{3,2,1,0:T(8,128)(2,1)S(1)}, bf16[2,4,32,256]{3,2,1,0:T(8,128)(2,1)S(1)}, u32[]{:S(2)}, u32[]{:S(2)}) %collective-permute-start.12) | collective-permute-done | bytes 131104 | tf_op jit(solution)/shard_map/ppermute | solution.py:54
  106.2 0.0 copy-start.7
  106.2 0.0 all-to-all-done.1.refs_0_
  106.2 0.4 shard_map.85
  106.6 0.0 copy-done.5
  106.6 0.0 copy-done.6
  106.6 0.3 copy-done.7
  106.8 0.0 copy-start
  106.8 1.2 copy-done
  108.1 4.1 %all-to-all-start.2 = ((bf16[8,448,256]{2,1,0:T(8,128)(2,1)}), bf16[8,448,256]{2,1,0:T(8,128)(2,1)S(1)}, u32[]{:S(2)}, u32[]{:S(2)}) async-start(bf16[8,448,256]{2,1,0:T(8,128)(2,1)} %copy-done), calls=%async_computation.2 | async-start | bytes 3670016 | tf_op jit(solution)/shard_map/all_to_all | solution.py:45
  112.2 12.4 %shard_map.86 = bf16[4,16,32,256]{3,2,1,0:T(8,128)(2,1)} custom-call(bf16[4,16,32,256]{3,2,1,0:T(8,128)(2,1)S(1)} %get-tuple-element.41.refs_2_.refs_0_, bf16[4,1,32,256]{3,2,1,0:T(8,128)(2,1)S(1)} %collective-permute-done.7.refs_1_, bf16[4,1,32,256]{3,2,1,0:T(8,128)(2,1)S(1)} %collective-permute-done.8.refs_2_, bf16[4,32,256]{2,1,0:T(8,128)(2,1)} %copy-done.5, ...), custom_call_target="tpu_custom_call" | custom-call | flops 7247757312 | bytes 4194304 | tf_op jit(solution)/shard_map/pallas_call | solution.py:317
  124.6 3.3 %all-to-all-done.2 = bf16[8,448,256]{2,1,0:T(8,128)(2,1)S(1)} async-done(((bf16[8,448,256]{2,1,0:T(8,128)(2,1)}), bf16[8,448,256]{2,1,0:T(8,128)(2,1)S(1)}, u32[]{:S(2)}, u32[]{:S(2)}) %all-to-all-start.2) | async-done | bytes 1835040 | tf_op jit(solution)/shard_map/all_to_all | solution.py:45
  127.9 0.0 collective-permute-start.13
  127.9 2.4 %shard_map.87 = (f32[27,256,256]{2,1,0:T(8,128)}, f32[1,256]{1,0:T(1,128)}) custom-call(bf16[28,128,256]{2,1,0:T(8,128)(2,1)S(1)} %bitcast.15), custom_call_target="tpu_custom_call" | custom-call | bytes 4194304 | tf_op jit(solution)/shard_map/pallas_call | solution.py:317
  130.4 1.3 collective-permute-done.13.refs_0_
  131.7 1.9 %shard_map.88 = f32[27,256,256]{2,1,0:T(8,128)} custom-call(bf16[28,128,256]{2,1,0:T(8,128)(2,1)S(1)} %collective-permute-done.13.refs_0_, f32[27,256,256]{2,1,0:T(8,128)} %get-tuple-element.56.refs_1_), custom_call_target="tpu_custom_call", output_to_operand_aliasing={{}: (1, {})} | custom-call | bytes 4194304 | tf_op jit(solution)/shard_map/pallas_call | solution.py:317
  (10 shorter events, 0.1 us)
Async XLA Ops:
  0.6 1.2 copy-start.1
  2.0 8.5 %collective-permute-start.1 = (bf16[4,1,32,256]{3,2,1,0:T(8,128)(2,1)S(1)}, bf16[4,1,32,256]{3,2,1,0:T(8,128)(2,1)S(1)}, u32[]{:S(2)}, u32[]{:S(2)}) collective-permute-start(bf16[4,1,32,256]{3,2,1,0:T(8,128)(2,1)S(1)} %get-tuple-element.32), channel_id=1, source_target_pairs={{0,4},{4,8},{8,12},{12,16},{16,20},{20,24},{24,28},{1,5},{5,9},{9,... | collective-permute-start | bytes 196616 | tf_op jit(solution)/shard_map/ppermute | solution.py:54
  5.9 5.0 %collective-permute-start.2 = (bf16[4,1,32,256]{3,2,1,0:T(8,128)(2,1)S(1)}, bf16[4,1,32,256]{3,2,1,0:T(8,128)(2,1)S(1)}, u32[]{:S(2)}, u32[]{:S(2)}) collective-permute-start(bf16[4,1,32,256]{3,2,1,0:T(8,128)(2,1)S(1)} %get-tuple-element.33), channel_id=1, source_target_pairs={{4,0},{8,4},{12,8},{16,12},{20,16},{24,20},{28,24},{5,1},{9,5},{13... | collective-permute-start | bytes 196616 | tf_op jit(solution)/shard_map/ppermute | solution.py:54
  7.2 29.6 %collective-permute-start = (bf16[2,16,32,256]{3,2,1,0:T(8,128)(2,1)S(1)}, bf16[2,16,32,256]{3,2,1,0:T(8,128)(2,1)S(1)}, u32[]{:S(2)}, u32[]{:S(2)}) collective-permute-start(bf16[2,16,32,256]{3,2,1,0:T(8,128)(2,1)S(1)} %get-tuple-element.31), channel_id=1, source_target_pairs={{0,32},{32,64},{64,96},{1,33},{33,65},{65,97},{2,34},{34,66},{66,9... | collective-permute-start | bytes 1572872 | tf_op jit(solution)/shard_map/ppermute | solution.py:54
  11.3 11.6 %collective-permute-start.3 = (bf16[4,32,256]{2,1,0:T(8,128)(2,1)S(1)}, bf16[4,32,256]{2,1,0:T(8,128)(2,1)S(1)}, u32[]{:S(2)}, u32[]{:S(2)}) collective-permute-start(bf16[4,32,256]{2,1,0:T(8,128)(2,1)S(1)} %get-tuple-element.34), channel_id=1, source_target_pairs={{0,1},{1,2},{2,3},{4,5},{5,6},{6,7},{8,9},{9,10},{10,11},{12,13},{... | collective-permute-start | bytes 196616 | tf_op jit(solution)/shard_map/ppermute | solution.py:54
  18.8 12.5 %copy-start.2 = (bf16[4,16,32,256]{3,2,1,0:T(8,128)(2,1)S(1)}, bf16[4,16,32,256]{3,2,1,0:T(8,128)(2,1)}, u32[]{:S(2)}) copy-start(bf16[4,16,32,256]{3,2,1,0:T(8,128)(2,1)} %refs_5_.1) | copy-start | bytes 3145732
  18.8 12.5 %copy-start.4 = (f32[256]{0:T(256)S(1)}, f32[256]{0:T(256)}, u32[]{:S(2)}) copy-start(f32[256]{0:T(256)} %param.6) | copy-start | bytes 3076
  20.9 7.1 %collective-permute-start.4 = (bf16[4,32,256]{2,1,0:T(8,128)(2,1)S(1)}, bf16[4,32,256]{2,1,0:T(8,128)(2,1)S(1)}, u32[]{:S(2)}, u32[]{:S(2)}) collective-permute-start(bf16[4,32,256]{2,1,0:T(8,128)(2,1)S(1)} %get-tuple-element.35), channel_id=1, source_target_pairs={{1,0},{2,1},{3,2},{5,4},{6,5},{7,6},{9,8},{10,9},{11,10},{13,12},{... | collective-permute-start | bytes 196616 | tf_op jit(solution)/shard_map/ppermute | solution.py:54
  28.0 8.8 %collective-permute-start.5 = (bf16[2,4,32,256]{3,2,1,0:T(8,128)(2,1)S(1)}, bf16[2,4,32,256]{3,2,1,0:T(8,128)(2,1)S(1)}, u32[]{:S(2)}, u32[]{:S(2)}) collective-permute-start(bf16[2,4,32,256]{3,2,1,0:T(8,128)(2,1)S(1)} %pad_maximum_fusion), channel_id=1, source_target_pairs={{0,32},{32,64},{64,96},{1,33},{33,65},{65,97},{2,34},{34,66},{66,9... | collective-permute-start | bytes 393224 | tf_op jit(solution)/shard_map/ppermute | solution.py:54
  42.1 3.9 %copy-start.3 = (bf16[4,1,32,256]{3,2,1,0:T(8,128)(2,1)}, bf16[4,1,32,256]{3,2,1,0:T(8,128)(2,1)S(1)}, u32[]{:S(2)}) copy-start(bf16[4,1,32,256]{3,2,1,0:T(8,128)(2,1)S(1)} %get-tuple-element.43) | copy-start | bytes 196612
  46.0 4.2 %collective-permute-start.6 = (bf16[28,128,256]{2,1,0:T(8,128)(2,1)S(1)}, bf16[28,128,256]{2,1,0:T(8,128)(2,1)S(1)}, u32[]{:S(2)}, u32[]{:S(2)}) collective-permute-start(bf16[28,128,256]{2,1,0:T(8,128)(2,1)S(1)} %shard_map.81), channel_id=1, source_target_pairs={{0,1},{1,0},{2,3},{3,2},{4,5},{5,4},{6,7},{7,6},{8,9},{9,8},{10,11... | collective-permute-start | bytes 5505032 | tf_op jit(solution)/shard_map/ppermute | solution.py:450
  51.7 22.2 %all-to-all-start = ((bf16[8,448,256]{2,1,0:T(8,128)(2,1)}), bf16[8,448,256]{2,1,0:T(8,128)(2,1)S(1)}, u32[]{:S(2)}, u32[]{:S(2)}) async-start(bf16[8,448,256]{2,1,0:T(8,128)(2,1)} %bitcast.4), calls=%async_computation | async-start | bytes 3670016 | tf_op jit(solution)/shard_map/all_to_all | solution.py:45
  58.2 19.7 %collective-permute-start.9 = (bf16[2,16,32,256]{3,2,1,0:T(8,128)(2,1)S(1)}, bf16[2,16,32,256]{3,2,1,0:T(8,128)(2,1)}, u32[]{:S(2)}, u32[]{:S(2)}) collective-permute-start(bf16[2,16,32,256]{3,2,1,0:T(8,128)(2,1)S(1)} %get-tuple-element.45), channel_id=1, source_target_pairs={{32,0},{64,32},{96,64},{33,1},{65,33},{97,65},{34,2},{66,34},{98,6... | collective-permute-start | bytes 1572872 | tf_op jit(solution)/shard_map/ppermute | solution.py:54
  59.5 3.6 %collective-permute-start.7 = (bf16[4,1,32,256]{3,2,1,0:T(8,128)(2,1)}, bf16[4,1,32,256]{3,2,1,0:T(8,128)(2,1)S(1)}, u32[]{:S(2)}, u32[]{:S(2)}) collective-permute-start(bf16[4,1,32,256]{3,2,1,0:T(8,128)(2,1)} %get-tuple-element.42), channel_id=1, source_target_pairs={{0,4},{4,8},{8,12},{12,16},{16,20},{20,24},{24,28},{1,5},{5,9},{9,... | collective-permute-start | bytes 196616 | tf_op jit(solution)/shard_map/ppermute | solution.py:54
  60.8 6.0 %collective-permute-start.8 = (bf16[4,1,32,256]{3,2,1,0:T(8,128)(2,1)}, bf16[4,1,32,256]{3,2,1,0:T(8,128)(2,1)S(1)}, u32[]{:S(2)}, u32[]{:S(2)}) collective-permute-start(bf16[4,1,32,256]{3,2,1,0:T(8,128)(2,1)} %copy-done.3), channel_id=1, source_target_pairs={{4,0},{8,4},{12,8},{16,12},{20,16},{24,20},{28,24},{5,1},{9,5},{13... | collective-permute-start | bytes 196616 | tf_op jit(solution)/shard_map/ppermute | solution.py:54
  77.9 28.3 %all-to-all-start.1 = ((bf16[8,448,256]{2,1,0:T(8,128)(2,1)}), bf16[8,448,256]{2,1,0:T(8,128)(2,1)S(1)}, u32[]{:S(2)}, u32[]{:S(2)}) async-start(bf16[8,448,256]{2,1,0:T(8,128)(2,1)} %shard_map.83.refs_3_), calls=%async_computation.1 | async-start | bytes 3670016 | tf_op jit(solution)/shard_map/all_to_all | solution.py:45
  87.2 10.9 %collective-permute-start.10 = (bf16[4,32,256]{2,1,0:T(8,128)(2,1)S(1)}, bf16[4,32,256]{2,1,0:T(8,128)(2,1)S(1)}, u32[]{:S(2)}, u32[]{:S(2)}) collective-permute-start(bf16[4,32,256]{2,1,0:T(8,128)(2,1)S(1)} %get-tuple-element.49), channel_id=1, source_target_pairs={{0,1},{1,2},{2,3},{4,5},{5,6},{6,7},{8,9},{9,10},{10,11},{12,13},{... | collective-permute-start | bytes 196616 | tf_op jit(solution)/shard_map/ppermute | solution.py:54
  93.1 7.4 %collective-permute-start.11 = (bf16[4,32,256]{2,1,0:T(8,128)(2,1)S(1)}, bf16[4,32,256]{2,1,0:T(8,128)(2,1)S(1)}, u32[]{:S(2)}, u32[]{:S(2)}) collective-permute-start(bf16[4,32,256]{2,1,0:T(8,128)(2,1)S(1)} %get-tuple-element.50), channel_id=1, source_target_pairs={{1,0},{2,1},{3,2},{5,4},{6,5},{7,6},{9,8},{10,9},{11,10},{13,12},{... | collective-permute-start | bytes 196616 | tf_op jit(solution)/shard_map/ppermute | solution.py:54
  98.1 8.4 %copy-start.5 = (bf16[4,32,256]{2,1,0:T(8,128)(2,1)}, bf16[4,32,256]{2,1,0:T(8,128)(2,1)S(1)}, u32[]{:S(2)}) copy-start(bf16[4,32,256]{2,1,0:T(8,128)(2,1)S(1)} %collective-permute-done.10.refs_3_) | copy-start | bytes 196612
  100.5 6.1 %copy-start.6 = (bf16[4,32,256]{2,1,0:T(8,128)(2,1)}, bf16[4,32,256]{2,1,0:T(8,128)(2,1)S(1)}, u32[]{:S(2)}) copy-start(bf16[4,32,256]{2,1,0:T(8,128)(2,1)S(1)} %collective-permute-done.11.refs_4_) | copy-start | bytes 196612
  100.5 5.7 %collective-permute-start.12 = (bf16[2,4,32,256]{3,2,1,0:T(8,128)(2,1)S(1)}, bf16[2,4,32,256]{3,2,1,0:T(8,128)(2,1)S(1)}, u32[]{:S(2)}, u32[]{:S(2)}) collective-permute-start(bf16[2,4,32,256]{3,2,1,0:T(8,128)(2,1)S(1)} %pad_maximum_fusion.1), channel_id=1, source_target_pairs={{32,0},{64,32},{96,64},{33,1},{65,33},{97,65},{34,2},{66,34},{98,6... | collective-permute-start | bytes 393224 | tf_op jit(solution)/shard_map/ppermute | solution.py:54
  106.2 0.6 copy-start.7
  106.8 1.2 copy-start
  108.1 19.9 %all-to-all-start.2 = ((bf16[8,448,256]{2,1,0:T(8,128)(2,1)}), bf16[8,448,256]{2,1,0:T(8,128)(2,1)S(1)}, u32[]{:S(2)}, u32[]{:S(2)}) async-start(bf16[8,448,256]{2,1,0:T(8,128)(2,1)} %copy-done), calls=%async_computation.2 | async-start | bytes 3670016 | tf_op jit(solution)/shard_map/all_to_all | solution.py:45
  127.9 3.8 %collective-permute-start.13 = (bf16[28,128,256]{2,1,0:T(8,128)(2,1)S(1)}, bf16[28,128,256]{2,1,0:T(8,128)(2,1)S(1)}, u32[]{:S(2)}, u32[]{:S(2)}) collective-permute-start(bf16[28,128,256]{2,1,0:T(8,128)(2,1)S(1)} %bitcast.14), channel_id=1, source_target_pairs={{0,1},{1,0},{2,3},{3,2},{4,5},{5,4},{6,7},{7,6},{8,9},{9,8},{10,11... | collective-permute-start | bytes 5505032 | tf_op jit(solution)/shard_map/ppermute | solution.py:487
